TPU v7x, 128 devices: a whole 4x4x4 slice. The times are simulated.
128 devices in a mesh: tm: 8 (over x, core), rows: 16 (over z, y).
Axes of the slice: x: 4, y: 4, z: 4, core: 2. Of those that a mesh axis runs over, the one named last changes fastest.
Arguments:
- features: bfloat16 [16, 32, 128, 384], P('tm', 'rows'), may hold values from -6 to 6
- block_gain: float32 [384], replicated, may hold values from 0.5 to 1.5
- conv_weight: bfloat16 [3, 3, 3, 384, 384], replicated, may hold values from -0.0625 to 0.0625
- conv_bias: float32 [384], replicated, may hold values from -3 to 3
- latent_weight: bfloat16 [384, 16], replicated, may hold values from -0.3125 to 0.3125
- latent_bias: float32 [16], replicated, may hold values from -3 to 3
- patch_weight: bfloat16 [64, 5120], replicated, may hold values from -0.75 to 0.75
- patch_bias: float32 [5120], replicated, may hold values from -3 to 3
- shift_mod: float32 [5120], replicated, may hold values from -4 to 4
- scale_mod: float32 [5120], replicated, may hold values from -2 to 2
- query_weight: bfloat16 [5120, 5120], P(None, 'tm'), may hold values from -0.078125 to 0.078125
- query_bias: float32 [5120], P('tm'), may hold values from -4 to 4
- query_gain: float32 [5120], P('tm'), may hold values from 0.5 to 1.5
- key_weight: bfloat16 [5120, 5120], P(None, 'tm'), may hold values from -0.078125 to 0.078125
- key_bias: float32 [5120], P('tm'), may hold values from -4 to 4
- key_gain: float32 [5120], P('tm'), may hold values from 0.5 to 1.5
- packing: int32 [128], replicated, may hold values from 0 to 127, each once
Outputs:
- queries: bfloat16 [16384, 5120], P('rows', 'tm')
- keys: bfloat16 [16384, 5120], P('rows', 'tm')
All inputs are finite; a program needn't handle non-finite values.
Results may differ from a plain program's by a relative error of at most 0.0054.
Values may be sent and summed in bfloat16 or wider, within the bound.
No kernel may reach another device: no remote copies, remote signals or barrier semaphores. Data moves between devices by JAX's collectives and lax.ppermute only.
A program may use at most 128 MiB of HBM per device.

v0:
```python
import jax
import jax.numpy as jnp
from jax import lax
from jax.sharding import PartitionSpec as P

epsilon = 1e-06


def with_halo(shard, sides, width):
    for axis, dim in sides:
        size, length = (lax.axis_size(axis), shard.shape[dim])
        up = [(i, (i + 1) % size) for i in range(size - 1)]
        down = [(j, i) for i, j in up]
        last = lax.slice_in_dim(shard, length - width, length, axis=dim)
        leading = lax.slice_in_dim(shard, 0, width, axis=dim)
        before = lax.ppermute(last, axis, up)
        after = lax.ppermute(leading, axis, down)
        shard = jnp.concatenate([before, shard, after], axis=dim)
    return shard


def from_behind(block, axis, distance):
    devices = range(lax.axis_size(axis))
    route = [(i - distance, i) for i in devices if i - distance in devices]
    return lax.ppermute(block, axis, route)


def joined_along(parts, dim):
    parts = jnp.moveaxis(parts, 0, dim)
    lengths = parts.shape
    return parts.reshape(*lengths[:dim], lengths[dim] * lengths[dim + 1], *lengths[dim + 2 :])


def sent_to_all(shard, axis):
    length = lax.axis_size(axis)
    return lax.all_to_all(
        jnp.broadcast_to(shard[None], (length, *shard.shape)), axis, 0, 0, tiled=True
    )


def gathered_copies(shard, axis, dim):
    return joined_along(sent_to_all(shard, axis), dim)


def over_copies(shard, axis):
    return sent_to_all(shard, axis).sum(axis=0)


def in_one(arrays, axis):
    ends = [0]
    for a in arrays:
        ends.append(ends[-1] + a.size)
    subtotal = over_copies(jnp.concatenate([a.ravel() for a in arrays]), axis)
    return tuple((subtotal[b:e].reshape(a.shape) for a, b, e in zip(arrays, ends, ends[1:])))


def normed_act(features, block_gain):
    values = features.astype(jnp.float32)
    square_mean = jnp.mean(values * values, axis=-1, keepdims=True)
    return jax.nn.silu(values * lax.rsqrt(square_mean + epsilon) * block_gain).astype(jnp.bfloat16)


def causal_conv(extended, conv_weight, frames, rows_count, cols_count, channels):
    padded = jnp.pad(extended, ((0, 0), (0, 0), (1, 1), (0, 0)))
    total = jnp.zeros((frames * rows_count * cols_count, channels), jnp.float32)
    for depth_at in range(3):
        for row_at in range(3):
            slab_part = padded[depth_at : depth_at + frames, row_at : row_at + rows_count]
            joined = jnp.concatenate(
                [
                    slab_part[:, :, 0:cols_count],
                    slab_part[:, :, 1 : cols_count + 1],
                    slab_part[:, :, 2 : cols_count + 2],
                ],
                axis=-1,
            )
            kernel = conv_weight[depth_at, row_at].reshape(3 * channels, channels)
            total = total + jnp.dot(
                joined.reshape(-1, 3 * channels), kernel, preferred_element_type=jnp.float32
            )
    return total.reshape(frames, rows_count, cols_count, channels)


def per_device(
    features,
    block_gain,
    conv_weight,
    conv_bias,
    latent_weight,
    latent_bias,
    patch_weight,
    patch_bias,
    shift_mod,
    scale_mod,
    query_weight,
    query_bias,
    query_gain,
    key_weight,
    key_bias,
    key_gain,
    packing,
):
    frames, rows_count, cols_count, channels = features.shape
    latent_width = latent_weight.shape[1]
    act = normed_act(features, block_gain)
    rimmed = with_halo(act, (("rows", 1),), 1)
    before = from_behind(rimmed, "tm", 1)
    extended = jnp.concatenate([before, rimmed], axis=0)
    conv = causal_conv(extended, conv_weight, frames, rows_count, cols_count, channels)
    block_out = (features.astype(jnp.float32) + conv + conv_bias).astype(jnp.bfloat16)
    latent = (
        jnp.dot(block_out.reshape(-1, channels), latent_weight, preferred_element_type=jnp.float32)
        + latent_bias
    ).astype(jnp.bfloat16)
    latent = latent.reshape(frames, rows_count // 2, 2, cols_count // 2, 2, latent_width)
    own_block = jnp.transpose(latent, (5, 2, 4, 0, 1, 3)).reshape(4 * latent_width, -1)
    count_tm = lax.axis_size("tm")
    count_rows = lax.axis_size("rows")
    shard = lax.axis_index("rows")
    own_ident = lax.axis_index("tm") * count_rows + shard
    targets = jnp.transpose(packing.reshape(count_rows, count_tm)).reshape(-1)
    marker = (targets == own_ident).astype(jnp.bfloat16)
    outgoing = marker[:, None, None] * own_block[None]
    arrived = lax.all_to_all(outgoing, ("tm", "rows"), split_axis=0, concat_axis=0, tiled=True)
    mine = jnp.sum(arrived.astype(jnp.float32), axis=0).astype(jnp.bfloat16)
    slots = gathered_copies(mine[None], "tm", 0)
    packed = jnp.transpose(slots, (0, 2, 1)).reshape(-1, slots.shape[1])
    embedded = jnp.dot(packed, patch_weight, preferred_element_type=jnp.float32) + patch_bias
    center = jnp.mean(embedded, axis=-1, keepdims=True)
    spread = jnp.mean((embedded - center) ** 2, axis=-1, keepdims=True)
    modulated = (
        (embedded - center) * lax.rsqrt(spread + epsilon) * (1.0 + scale_mod) + shift_mod
    ).astype(jnp.bfloat16)
    query_part = jnp.dot(modulated, query_weight, preferred_element_type=jnp.float32) + query_bias
    key_part = jnp.dot(modulated, key_weight, preferred_element_type=jnp.float32) + key_bias
    width_all = embedded.shape[1]
    query_sum, key_sum = in_one(
        (
            jnp.sum(query_part * query_part, axis=-1, keepdims=True),
            jnp.sum(key_part * key_part, axis=-1, keepdims=True),
        ),
        "tm",
    )
    queries = (query_part * lax.rsqrt(query_sum / width_all + epsilon) * query_gain).astype(
        jnp.bfloat16
    )
    keys = (key_part * lax.rsqrt(key_sum / width_all + epsilon) * key_gain).astype(jnp.bfloat16)
    return (queries, keys)


def solution(mesh):
    in_specs = (
        P("tm", "rows", None, None),
        P(),
        P(),
        P(),
        P(),
        P(),
        P(),
        P(),
        P(),
        P(),
        P(None, "tm"),
        P("tm"),
        P("tm"),
        P(None, "tm"),
        P("tm"),
        P("tm"),
        P(),
    )
    out_specs = (P("rows", "tm"), P("rows", "tm"))
    return jax.shard_map(
        per_device, mesh=mesh, in_specs=in_specs, out_specs=out_specs, check_vma=False
    )
```

profile of v0, /device:TPU:1, one launch (start us, length us, event | category | flops | bytes accessed | tf_op | source)
XLA Modules:
  0.0 144.3 jit_solution(15639560910312201606)
XLA Ops:
  0.7 1.2 fusion.5
  1.9 1.3 fusion.12
  3.2 4.0 %collective-permute-start = (bf16[2,1,128,384]{3,2,1,0:T(8,128)(2,1)S(1)}, bf16[2,1,128,384]{3,2,1,0:T(8,128)(2,1)S(1)}, u32[]{:S(2)}, u32[]{:S(2)}) collective-permute-start(bf16[2,1,128,384]{3,2,1,0:T(8,128)(2,1)S(1)} %get-tuple-element.47), channel_id=1, source_target_pairs={{0,1},{1,2},{2,3},{3,4},{4,5},{5,6},{6,7},{7,8},{8,9},{9,10},{10,1... | collective-permute-start | bytes 589832 | tf_op jit(solution)/shard_map/ppermute | solution.py:16
  7.3 1.3 collective-permute-start.1
  8.6 2.2 %collective-permute-done = bf16[2,1,128,384]{3,2,1,0:T(8,128)(2,1)S(1)} collective-permute-done((bf16[2,1,128,384]{3,2,1,0:T(8,128)(2,1)S(1)}, bf16[2,1,128,384]{3,2,1,0:T(8,128)(2,1)S(1)}, u32[]{:S(2)}, u32[]{:S(2)}) %collective-permute-start) | collective-permute-done | bytes 196640 | tf_op jit(solution)/shard_map/ppermute | solution.py:16
  10.8 3.8 %collective-permute-done.1 = bf16[2,1,128,384]{3,2,1,0:T(8,128)(2,1)S(1)} collective-permute-done((bf16[2,1,128,384]{3,2,1,0:T(8,128)(2,1)S(1)}, bf16[2,1,128,384]{3,2,1,0:T(8,128)(2,1)S(1)}, u32[]{:S(2)}, u32[]{:S(2)}) %collective-permute-start.1) | collective-permute-done | bytes 196640 | tf_op jit(solution)/shard_map/ppermute | solution.py:17
  14.8 4.9 %collective-permute-start.2 = (bf16[2,4,128,384]{3,2,1,0:T(8,128)(2,1)S(1)}, bf16[2,4,128,384]{3,2,1,0:T(8,128)(2,1)S(1)}, u32[]{:S(2)}, u32[]{:S(2)}) collective-permute-start(bf16[2,4,128,384]{3,2,1,0:T(8,128)(2,1)S(1)} %pad_maximum_fusion.9), channel_id=1, source_target_pairs={{0,16},{16,32},{32,48},{48,64},{64,80},{80,96},{96,112},{1,17},{17... | collective-permute-start | bytes 2359304 | tf_op jit(solution)/shard_map/ppermute | solution.py:25
  19.9 3.9 %fusion.22 = (bf16[1,1,3,384,384]{4,3,2,1,0:T(8,128)(2,1)S(1)}, bf16[1,1,3,384,384]{4,3,2,1,0:T(8,128)(2,1)S(1)}, bf16[1,1,3,384,384]{4,3,2,1,0:T(8,128)(2,1)S(1...) fusion(bf16[3,3,3,384,384]{4,3,2,1,0:T(8,128)(2,1)} %param.19), kind=kLoop, calls=%fused_computation.79 | loop fusion | bytes 15925248 | tf_op jit(solution)/shard_map/slice | solution.py:77
  23.9 4.7 %collective-permute-done.2 = bf16[2,4,128,384]{3,2,1,0:T(8,128)(2,1)S(1)} collective-permute-done((bf16[2,4,128,384]{3,2,1,0:T(8,128)(2,1)S(1)}, bf16[2,4,128,384]{3,2,1,0:T(8,128)(2,1)S(1)}, u32[]{:S(2)}, u32[]{:S(2)}) %collective-permute-start.2) | collective-permute-done | bytes 786464 | tf_op jit(solution)/shard_map/ppermute | solution.py:25
  29.6 0.8 pad_slice_fusion.1
  30.9 0.8 fusion.25
  31.7 0.8 convolution_add_fusion.7
  32.8 0.8 convolution_add_fusion.6
  33.6 0.8 convolution_add_fusion.5
  34.7 0.8 convolution_add_fusion.4
  35.5 0.8 convolution_add_fusion.3
  36.8 0.8 convolution_add_fusion.2
  37.6 0.8 convolution_add_fusion.1
  38.5 0.8 convolution_add_fusion
  40.3 41.9 %all_to_all.16 = bf16[128,64,128]{2,1,0:T(8,128)(2,1)S(1)} all-to-all(bf16[128,64,128]{2,1,0:T(8,128)(2,1)S(1)} %broadcast_multiply_fusion), channel_id=1, replica_groups=mesh['tm'=8,'rows'=16] {'tm','rows'}, dimensions={0} | all-to-all | bytes 4194304 | tf_op jit(solution)/shard_map/all_to_all | solution.py:124
  83.3 4.8 %all-to-all-start.1 = ((bf16[8,1,64,128]{3,2,1,0:T(8,128)(2,1)}), bf16[8,1,64,128]{3,2,1,0:T(8,128)(2,1)S(1)}, u32[]{:S(2)}, u32[]{:S(2)}) async-start(bf16[8,1,64,128]{3,2,1,0:T(8,128)(2,1)} %broadcast_in_dim.4), calls=%async_computation.1 | async-start | bytes 262144 | tf_op jit(solution)/shard_map/all_to_all | solution.py:36
  88.1 5.3 %all-to-all-done.1 = bf16[8,1,64,128]{3,2,1,0:T(8,128)(2,1)S(1)} async-done(((bf16[8,1,64,128]{3,2,1,0:T(8,128)(2,1)}), bf16[8,1,64,128]{3,2,1,0:T(8,128)(2,1)S(1)}, u32[]{:S(2)}, u32[]{:S(2)}) %all-to-all-start.1) | async-done | bytes 131104 | tf_op jit(solution)/shard_map/all_to_all | solution.py:36
  93.4 3.0 %add_reduce_fusion = (f32[1024]{0:T(1024)S(1)}, f32[1024,5120]{1,0:T(8,128)S(1)}) fusion(f32[5120]{0:T(1024)S(1)} %copy-done.3, bf16[64,5120]{1,0:T(8,128)(2,1)S(1)} %copy-done, bf16[8,1,64,128]{3,2,1,0:T(8,128)(2,1)S(1)} %all-to-all-done.1), kind=kOutput, calls=%fused_computation.2 | convolution fusion | flops 681573376 | bytes 21782528 | tf_op jit(solution)/shard_map/dot_general | solution.py:128
  96.4 3.5 %multiply_reduce_fusion = f32[1024]{0:T(1024)S(1)} fusion(f32[1024,5120]{1,0:T(8,128)S(1)} %get-tuple-element.52, f32[1024]{0:T(1024)S(1)} %broadcast_multiply_fusion.1, f32[5120]{0:T(1024)S(1)} %copy-done.3), kind=kLoop, calls=%fused_computation.1 | loop fusion | flops 20970496 | bytes 21000192 | tf_op jit(solution)/shard_map/reduce_sum | solution.py:130
  99.9 5.3 %add_convert_fusion = bf16[1024,5120]{1,0:T(8,128)(2,1)S(1)} fusion(f32[1024,5120]{1,0:T(8,128)S(1)} %get-tuple-element.52, f32[5120]{0:T(1024)S(1)} %copy-done.4, f32[5120]{0:T(1024)S(1)} %broadcast_add_fusion, f32[1024]{0:T(1024)S(1)} %add_rsqrt_fusion, f32[1024]{0:T(1024)S(1)} %broadcast_multiply_fusion.1, f32[5120]{0:T(1024)S(1)} %copy-done.3), kind=kLoop, calls=%fused_computation | loop fusion | flops 31457280 | bytes 31526912 | tf_op jit(solution)/shard_map/convert_element_type | solution.py:133
  105.3 11.7 %multiply_reduce_fusion.2 = (f32[1024]{0:T(1024)S(1)}, f32[1024,640]{0,1:T(8,128)}) fusion(f32[640]{0:T(1024)S(1)} %copy-done.9, bf16[1024,5120]{1,0:T(8,128)(2,1)S(1)} %add_convert_fusion, bf16[5120,640]{1,0:T(8,128)(2,1)} %param.27), kind=kOutput, calls=%fused_computation.6 | convolution fusion | flops 6712851456 | bytes 19667456 | tf_op jit(solution)/shard_map/dot_general | solution.py:134
  117.0 11.9 %multiply_reduce_fusion.1 = (f32[1024]{0:T(1024)S(1)}, f32[1024,640]{0,1:T(8,128)}) fusion(f32[640]{0:T(1024)S(1)} %copy-done.7, bf16[1024,5120]{1,0:T(8,128)(2,1)S(1)} %add_convert_fusion, bf16[5120,640]{1,0:T(8,128)(2,1)} %param.30), kind=kOutput, calls=%fused_computation.5 | convolution fusion | flops 6712851456 | bytes 19667456 | tf_op jit(solution)/shard_map/dot_general | solution.py:135
  129.0 8.1 %all_to_all.17 = f32[8,1,2048]{2,1,0:T(1,128)S(1)} all-to-all(f32[8,1,2048]{2,1,0:T(1,128)S(1)} %broadcast_in_dim.5), channel_id=1, replica_groups=mesh['tm'=8,'rows'=16] {'tm'}, dimensions={0} | all-to-all | bytes 131072 | tf_op jit(solution)/shard_map/all_to_all | solution.py:36
  137.1 2.1 %multiply_convert_fusion = bf16[1024,640]{0,1:T(8,128)(2,1)S(1)} fusion(f32[1024,640]{0,1:T(8,128)} %get-tuple-element.54, f32[640]{0:T(1024)S(1)} %copy-done.8, f32[1024]{0:T(1024)S(1)} %get-tuple-element.49, f32[640]{0:T(1024)S(1)} %copy-done.7), kind=kLoop, calls=%fused_computation.3 | loop fusion | flops 2621440 | bytes 3941376 | tf_op jit(solution)/shard_map/convert_element_type | solution.py:147
  139.3 1.4 copy.45
  140.7 2.2 %multiply_convert_fusion.1 = bf16[1024,640]{0,1:T(8,128)(2,1)S(1)} fusion(f32[1024,640]{0,1:T(8,128)} %get-tuple-element.56, f32[640]{0:T(1024)S(1)} %copy-done.10, f32[1024]{0:T(1024)S(1)} %get-tuple-element.50, f32[640]{0:T(1024)S(1)} %copy-done.9), kind=kLoop, calls=%fused_computation.4 | loop fusion | flops 2621440 | bytes 3941376 | tf_op jit(solution)/shard_map/convert_element_type | solution.py:144
  142.9 1.4 copy.44
  (58 shorter events, 5.3 us)
Async XLA Ops:
  0.6 92.8 %copy-start = (bf16[64,5120]{1,0:T(8,128)(2,1)S(1)}, bf16[64,5120]{1,0:T(8,128)(2,1)}, u32[]{:S(2)}) copy-start(bf16[64,5120]{1,0:T(8,128)(2,1)} %param.23) | copy-start | bytes 1966084
  0.6 19.0 %copy-start.13 = (s32[128]{0:T(128)S(1)}, s32[128]{0:T(128)}, u32[]{:S(2)}) copy-start(s32[128]{0:T(128)} %param.33) | copy-start | bytes 1540
  3.2 7.6 %collective-permute-start = (bf16[2,1,128,384]{3,2,1,0:T(8,128)(2,1)S(1)}, bf16[2,1,128,384]{3,2,1,0:T(8,128)(2,1)S(1)}, u32[]{:S(2)}, u32[]{:S(2)}) collective-permute-start(bf16[2,1,128,384]{3,2,1,0:T(8,128)(2,1)S(1)} %get-tuple-element.47), channel_id=1, source_target_pairs={{0,1},{1,2},{2,3},{3,4},{4,5},{5,6},{6,7},{7,8},{8,9},{9,10},{10,1... | collective-permute-start | bytes 589832 | tf_op jit(solution)/shard_map/ppermute | solution.py:16
  7.3 7.3 %collective-permute-start.1 = (bf16[2,1,128,384]{3,2,1,0:T(8,128)(2,1)S(1)}, bf16[2,1,128,384]{3,2,1,0:T(8,128)(2,1)S(1)}, u32[]{:S(2)}, u32[]{:S(2)}) collective-permute-start(bf16[2,1,128,384]{3,2,1,0:T(8,128)(2,1)S(1)} %get-tuple-element.48), channel_id=1, source_target_pairs={{1,0},{2,1},{3,2},{4,3},{5,4},{6,5},{7,6},{8,7},{9,8},{10,9},{11,1... | collective-permute-start | bytes 589832 | tf_op jit(solution)/shard_map/ppermute | solution.py:17
  14.8 13.8 %collective-permute-start.2 = (bf16[2,4,128,384]{3,2,1,0:T(8,128)(2,1)S(1)}, bf16[2,4,128,384]{3,2,1,0:T(8,128)(2,1)S(1)}, u32[]{:S(2)}, u32[]{:S(2)}) collective-permute-start(bf16[2,4,128,384]{3,2,1,0:T(8,128)(2,1)S(1)} %pad_maximum_fusion.9), channel_id=1, source_target_pairs={{0,16},{16,32},{32,48},{48,64},{64,80},{80,96},{96,112},{1,17},{17... | collective-permute-start | bytes 2359304 | tf_op jit(solution)/shard_map/ppermute | solution.py:25
  38.4 1.0 copy-start.2
  38.5 1.0 copy-start.11
  38.5 1.1 copy-start.6
  38.5 1.1 copy-start.12
  82.2 5.8 %copy-start.5 = (f32[5120]{0:T(1024)S(1)}, f32[5120]{0:T(1024)}, u32[]{:S(2)}) copy-start(f32[5120]{0:T(1024)} %param.26) | copy-start | bytes 61444
  82.3 11.1 %copy-start.3 = (f32[5120]{0:T(1024)S(1)}, f32[5120]{0:T(1024)}, u32[]{:S(2)}) copy-start(f32[5120]{0:T(1024)} %param.24) | copy-start | bytes 61444
  83.3 10.1 %all-to-all-start.1 = ((bf16[8,1,64,128]{3,2,1,0:T(8,128)(2,1)}), bf16[8,1,64,128]{3,2,1,0:T(8,128)(2,1)S(1)}, u32[]{:S(2)}, u32[]{:S(2)}) async-start(bf16[8,1,64,128]{3,2,1,0:T(8,128)(2,1)} %broadcast_in_dim.4), calls=%async_computation.1 | async-start | bytes 262144 | tf_op jit(solution)/shard_map/all_to_all | solution.py:36
  96.4 3.5 %copy-start.4 = (f32[5120]{0:T(1024)S(1)}, f32[5120]{0:T(1024)}, u32[]{:S(2)}) copy-start(f32[5120]{0:T(1024)} %param.25) | copy-start | bytes 61444
  99.9 5.4 %copy-start.9 = (f32[640]{0:T(1024)S(1)}, f32[640]{0:T(1024)}, u32[]{:S(2)}) copy-start(f32[640]{0:T(1024)} %param.28) | copy-start | bytes 7684
  105.3 11.7 %copy-start.7 = (f32[640]{0:T(1024)S(1)}, f32[640]{0:T(1024)}, u32[]{:S(2)}) copy-start(f32[640]{0:T(1024)} %param.31) | copy-start | bytes 7684
  117.0 20.1 %copy-start.8 = (f32[640]{0:T(1024)S(1)}, f32[640]{0:T(1024)}, u32[]{:S(2)}) copy-start(f32[640]{0:T(1024)} %param.32) | copy-start | bytes 7684
  139.2 1.5 %copy-start.10 = (f32[640]{0:T(1024)S(1)}, f32[640]{0:T(1024)}, u32[]{:S(2)}) copy-start(f32[640]{0:T(1024)} %param.29) | copy-start | bytes 7684
  140.7 3.6 %copy-start.1 = (bf16[64,5120]{1,0:T(8,128)(2,1)S(1)}, bf16[64,5120]{1,0:T(8,128)(2,1)}, u32[]{:S(2)}) copy-start(bf16[64,5120]{1,0:T(8,128)(2,1)} %param.23) | copy-start | bytes 1966084
where the time goes:
time: 145 us; the launch traced here: 144 us
  blocking collectives  50 us (34%)
  matrix products  34 us (23%)
  other arithmetic  18.1 us (12%)
  waiting for transfers between devices  16 us (11%)
  starting transfers between devices  15 us (10%)
  local copies, waits for them, and re-layouts  10.2 us (7%)
    all_to_all x1, blocking collectives, per_device(): lax.all_to_all(outgoing, ('tm', 'rows'), split_axis=0, concat_axis=0, til...  41.9 us
    dot_general x1, matrix products, per_device(): jnp.dot(modulated, key_weight, preferred_element_type=jnp.float32)  11.9 us
    dot_general x1, matrix products, per_device(): jnp.dot(modulated, query_weight, preferred_element_type=jnp.float32)  11.7 us
    all_to_all x1, blocking collectives, sent_to_all(): lax.all_to_all(jnp.broadcast_to(shard[None], (length, *shard.shape)), axi...  8.08 us
    dot_general x9, matrix products, causal_conv(): jnp.dot(joined.reshape(-1, 3 * channels), kernel, preferred_element_type=...  7.17 us
    convert_element_type x1, other arithmetic, per_device(): modulated = ((embedded - center) * lax.rsqrt(spread + epsilon) * (1.0 + s...  5.35 us
    all_to_all x1, waiting for transfers between devices, sent_to_all(): lax.all_to_all(jnp.broadcast_to(shard[None], (length, *shard.shape)), axi...  5.28 us
    ppermute x1, starting transfers between devices, from_behind(): return lax.ppermute(block, axis, route)  4.87 us
  transfers between devices with their start and end apart: 4, of which 4 were waited for; matrix products, arithmetic and copies ran while one was open for 3% of the time, Pallas kernels for 0%

commit v1 on v0

v1 whole, which is shorter than its diff:
```python
import jax
import jax.numpy as jnp
from jax import lax
from jax.experimental import pallas as pl
from jax.experimental.pallas import tpu as pltpu
from jax.sharding import PartitionSpec as P

epsilon = 1e-06
bf16 = jnp.bfloat16
f32 = jnp.float32
VMEM = pl.BlockSpec(memory_space=pltpu.VMEM)
SMEM = pl.BlockSpec(memory_space=pltpu.SMEM)
MIB = 1 << 20
EXT = 80


def mm(a, b, ca, cb):
    return lax.dot_general(a, b, (((ca,), (cb,)), ((), ())), preferred_element_type=f32)


def halves(x):
    high = x.astype(bf16)
    return high, (x - high.astype(f32)).astype(bf16)


def iota(shape, dim):
    return lax.broadcasted_iota(jnp.int32, shape, dim)


def partial_kernel(feat, gain, bias, lw, lb, cw_hbm, out, cw, wt, gt, sems):
    chunk = 3
    copies = [
        pltpu.make_async_copy(
            cw_hbm.at[pl.ds(i * chunk, chunk)], cw.at[pl.ds(i * chunk, chunk)], sems.at[i]
        )
        for i in range(27 // chunk)
    ]
    for c in copies:
        c.start()
    values = feat[...].astype(f32)
    mean = jnp.mean(values * values, axis=-1, keepdims=True)
    y = values * lax.rsqrt(mean + epsilon) * gain[...]
    act = (y / (1.0 + jnp.exp(-y))).astype(bf16)
    lwt_f = jnp.transpose(lw[...].astype(f32))
    lwt = lwt_f.astype(bf16)
    direct = mm(lwt, feat[...], 1, 1)
    const = jnp.sum(lwt_f * bias[...], axis=1, keepdims=True) + jnp.transpose(lb[...])
    for i, c in enumerate(copies):
        c.wait()
        for k in range(i * chunk, (i + 1) * chunk):
            high, low = halves(mm(lwt, cw[k], 1, 1))
            wt[pl.ds(k * 16, 16), :] = high
            wt[pl.ds(432 + k * 16, 16), :] = low
    gt[...] = mm(wt[...], act, 1, 1)
    lane = iota((16, 128), 1)
    for fo in range(4):
        for ro in range(4):
            by_e = []
            for e in range(3):
                total = None
                for f in range(2):
                    for r in range(2):
                        a, b = f + 2 - fo, r + 2 - ro
                        if not (0 <= a < 3 and 0 <= b < 3):
                            continue
                        k, q = (a * 3 + b) * 3 + e, f * 2 + r
                        part = (
                            gt[pl.ds(k * 16, 16), pl.ds(q * 128, 128)]
                            + gt[pl.ds(432 + k * 16, 16), pl.ds(q * 128, 128)]
                        )
                        total = part if total is None else total + part
                by_e.append(total)
            left = jnp.where(lane == 0, 0.0, pltpu.roll(by_e[0], 1, 1))
            right = jnp.where(lane == 127, 0.0, pltpu.roll(by_e[2], 127, 1))
            value = left + by_e[1] + right
            if fo < 2 and 1 <= ro < 3:
                q = fo * 2 + ro - 1
                value = value + direct[:, q * 128 : (q + 1) * 128] + const
            out[fo, ro] = value


def partial_latents(features, gain, bias, lw, lb, cw):
    return pl.pallas_call(
        partial_kernel,
        out_shape=jax.ShapeDtypeStruct((4, 4, 16, 128), f32),
        in_specs=[VMEM] * 5 + [pl.BlockSpec(memory_space=pl.ANY)],
        out_specs=VMEM,
        scratch_shapes=[
            pltpu.VMEM((27, 384, 384), bf16),
            pltpu.VMEM((864, 384), bf16),
            pltpu.VMEM((864, 512), f32),
            pltpu.SemaphoreType.DMA((9,)),
        ],
        compiler_params=pltpu.CompilerParams(vmem_limit_bytes=40 * MIB),
        name="partial_latents",
    )(features, gain, bias, lw, lb, cw)


def prepare_kernel(pw, pb, shift, scale, parts, gram):
    width = pw.shape[1]
    to, at = iota((64, 64), 0), iota((64, 64), 1)
    wanted = 4 * (to % 16) + 2 * ((to // 16) % 2) + to // 32
    order = jnp.where(at == wanted, 1.0, 0.0).astype(bf16)
    rows = mm(order, pw[...], 1, 0)
    rows = rows - jnp.mean(rows, axis=1, keepdims=True)
    const = pb[...] - jnp.mean(pb[...], axis=1, keepdims=True)
    tail = iota((16, width), 0)
    const_tail = jnp.where(tail == 0, const, 0.0)
    centered = jnp.concatenate([rows, const_tail], axis=0)
    high, low = halves(centered)
    both = mm(jnp.concatenate([high, low], axis=0), high, 1, 1)
    cross = both[EXT:, :]
    gram[...] = (both[:EXT, :] + cross + jnp.transpose(cross)) * (1.0 / width)
    scaled = centered * (1.0 + scale[...])
    last = jnp.where(iota((EXT, width), 0) == 65, shift[...], scaled)
    high, low = halves(last)
    parts[pl.ds(0, EXT), :] = high
    parts[pl.ds(EXT, EXT), :] = low


def prepared(pw, pb, shift, scale):
    return pl.pallas_call(
        prepare_kernel,
        out_shape=[
            jax.ShapeDtypeStruct((2 * EXT, pw.shape[1]), bf16),
            jax.ShapeDtypeStruct((EXT, EXT), f32),
        ],
        in_specs=[VMEM] * 4,
        out_specs=[VMEM] * 2,
        compiler_params=pltpu.CompilerParams(vmem_limit_bytes=40 * MIB),
        name="prepare_patch",
    )(pw, pb, shift, scale)


def project_kernel(parts, w, bias, gain, right, gram):
    both = mm(parts[...], w[...], 1, 0)
    rows = both[:EXT, :] + both[EXT:, :]
    rows = rows + jnp.where(iota(rows.shape, 0) == 65, bias[...], 0.0)
    high, low = halves(rows)
    pairs = mm(jnp.concatenate([high, low], axis=0), high, 1, 1)
    cross = pairs[EXT:, :]
    gram[...] = pairs[:EXT, :] + cross + jnp.transpose(cross)
    high, low = halves(rows * gain[...])
    right[pl.ds(0, EXT), :] = high
    right[pl.ds(EXT, EXT), :] = high
    right[pl.ds(2 * EXT, EXT), :] = low


def projected(parts, w, bias, gain, name):
    return pl.pallas_call(
        project_kernel,
        out_shape=[
            jax.ShapeDtypeStruct((3 * EXT, w.shape[1]), bf16),
            jax.ShapeDtypeStruct((EXT, EXT), f32),
        ],
        in_specs=[VMEM] * 4,
        out_specs=[VMEM] * 2,
        compiler_params=pltpu.CompilerParams(vmem_limit_bytes=40 * MIB),
        name=name,
    )(parts, w, bias, gain)


def pack_kernel(gq, gk, out):
    i, j = iota((EXT, EXT), 0), iota((EXT, EXT), 1)
    square = jnp.where(i >= j, gq[...], gk[...])
    diagonal = jnp.sum(jnp.where(i == j, gk[...], 0.0), axis=1, keepdims=True)
    out[:, :EXT] = square
    out[:, EXT:] = jnp.broadcast_to(diagonal, (EXT, 128 - EXT))


def packed_grams(gq, gk):
    return pl.pallas_call(
        pack_kernel,
        out_shape=jax.ShapeDtypeStruct((EXT, 128), f32),
        in_specs=[VMEM] * 2,
        out_specs=VMEM,
        name="pack_grams",
    )(gq, gk)


def block_kernel(own, above, below, out):
    row = lax.axis_index("rows")
    first = jnp.where(row == 0, 0.0, 1.0)
    final = jnp.where(row == lax.axis_size("rows") - 1, 0.0, 1.0)
    upper = [(own[f, 1] + above[f] * first).astype(bf16) for f in range(2)]
    lower = [(own[f, 2] + below[f] * final).astype(bf16) for f in range(2)]
    values = jnp.concatenate(
        [jnp.concatenate(upper, axis=1), jnp.concatenate(lower, axis=1)], axis=0
    )
    source, target = iota((256, 256), 0), iota((256, 256), 1)
    wanted = ((target // 64) % 2) * 128 + 2 * (target % 64) + target // 128
    pick = jnp.where(source == wanted, 1.0, 0.0).astype(bf16)
    spread = mm(values, pick, 1, 0).astype(bf16)
    out[pl.ds(0, 32), :] = spread[:, :128]
    out[pl.ds(32, 32), :] = spread[:, 128:]


def own_block(own, above, below):
    return pl.pallas_call(
        block_kernel,
        out_shape=jax.ShapeDtypeStruct((64, 128), bf16),
        in_specs=[VMEM] * 3,
        out_specs=VMEM,
        name="own_block",
    )(own, above, below)


def select_kernel(packing, b0, b1, b2, b3, keep, send):
    t, r = lax.axis_index("tm"), lax.axis_index("rows")
    blocks = (b0, b1, b2, b3)
    core = t % 2
    for out, half in ((keep, core), (send, 1 - core)):
        for i in range(4):
            ident = packing[r * 8 + half * 4 + i]
            frame, place = ident // 16, ident % 16
            dz = (r // 4) ^ (place // 4)
            dy = (r % 4) ^ (place % 4)
            out[i] = jnp.zeros((64, 128), bf16)
            for m in range(4):

                @pl.when((frame == t) & (dz == m))
                def _(out=out, i=i, m=m, dy=dy):
                    out[i] = blocks[m][dy]


def selected(packing, quads):
    return pl.pallas_call(
        select_kernel,
        out_shape=[jax.ShapeDtypeStruct((4, 64, 128), bf16)] * 2,
        in_specs=[SMEM] + [VMEM] * 4,
        out_specs=[VMEM] * 2,
        name="select_blocks",
    )(packing, *quads)


def token_kernel(core, mine, other, patch_gram, grams, rq, rk, q_out, k_out, left, ends):
    step = pl.program_id(0)
    width = 5120.0

    @pl.when(step == 0)
    def _():
        i, j = iota((EXT, EXT), 0), iota((EXT, EXT), 1)
        total = grams[...] * (1.0 / width)
        square = total[:, :EXT]
        diagonal = jnp.where(i == j, total[:, EXT : EXT + 1], 0.0)
        gq = jnp.where(i > j, 2.0 * square, 0.0) + jnp.where(i == j, square, 0.0)
        gk = jnp.where(i > j, 2.0 * jnp.transpose(square), 0.0) + diagonal
        for n, g in enumerate((patch_gram[...], gq, gk)):
            high, low = halves(g)
            left[pl.ds(n * EXT, EXT), pl.ds(0, EXT)] = high
            left[pl.ds(n * EXT, EXT), pl.ds(EXT, EXT)] = low
        corner = (i == 65) & (j == 65)
        ends[0] = jnp.sum(jnp.where(corner, gq, 0.0))
        ends[1] = jnp.sum(jnp.where(corner, gk, 0.0))

    x = jnp.where(step < 4, mine[step % 4], other[step % 4])
    tail = iota((EXT - 64, 128), 0)
    xf = jnp.concatenate([x.astype(f32), jnp.where(tail == 0, 1.0, 0.0)], axis=0)
    xe = xf.astype(bf16)
    t = mm(left[...], jnp.concatenate([xe, xe], axis=0), 1, 0)
    spread = jnp.sum(t[:EXT] * xf, axis=0, keepdims=True)
    scale = lax.rsqrt(spread + epsilon)
    for n, (right, out) in enumerate(((rq, q_out), (rk, k_out))):
        tn = t[(n + 1) * EXT : (n + 2) * EXT]
        squares = (
            scale * scale * jnp.sum(tn * xf, axis=0, keepdims=True)
            + scale * tn[65:66]
            + ends[n]
        )
        beta = lax.rsqrt(squares + epsilon)
        alpha = scale * beta
        y = xf * alpha + jnp.where(iota((EXT, 128), 0) == 65, beta, 0.0)
        high, low = halves(y)
        out[...] = mm(jnp.concatenate([high, low, high], axis=0), right[...], 0, 0).astype(bf16)


def tokens(core, mine, other, patch_gram, grams, rq, rk):
    def out_at(step, core_ref):
        c = core_ref[0]
        return (jnp.where(step < 4, c * 4 + step, (1 - c) * 4 + step - 4), 0)

    width = rq.shape[1]
    whole = lambda a: pl.BlockSpec(a.shape, lambda step, core_ref: (0,) * a.ndim)
    args = (mine, other, patch_gram, grams, rq, rk)
    return pl.pallas_call(
        token_kernel,
        grid_spec=pltpu.PrefetchScalarGridSpec(
            num_scalar_prefetch=1,
            grid=(8,),
            in_specs=[whole(a) for a in args],
            out_specs=[pl.BlockSpec((128, width), out_at)] * 2,
            scratch_shapes=[
                pltpu.VMEM((3 * EXT, 2 * EXT), bf16),
                pltpu.SMEM((2,), f32),
            ],
        ),
        out_shape=[jax.ShapeDtypeStruct((1024, width), bf16)] * 2,
        compiler_params=pltpu.CompilerParams(vmem_limit_bytes=40 * MIB),
        name="tokens",
    )(core, *args)


def swapped(x, axis, bits):
    return lax.ppermute(x, axis, [(i, i ^ bits) for i in range(lax.axis_size(axis))])


def moved(x, axis, by):
    size = lax.axis_size(axis)
    return lax.ppermute(x, axis, [(i, (i + by) % size) for i in range(size)])


def per_device(
    features,
    block_gain,
    conv_weight,
    conv_bias,
    latent_weight,
    latent_bias,
    patch_weight,
    patch_bias,
    shift_mod,
    scale_mod,
    query_weight,
    query_bias,
    query_gain,
    key_weight,
    key_bias,
    key_gain,
    packing,
):
    channels = features.shape[-1]
    row = lambda v: v.reshape(1, -1)
    partial = partial_latents(
        features.reshape(-1, channels),
        row(block_gain),
        row(conv_bias),
        latent_weight,
        row(latent_bias),
        conv_weight.reshape(27, channels, channels),
    )
    before = moved(partial[2:], "tm", 1)
    own = partial[:2] + jnp.where(lax.axis_index("tm") == 0, 0.0, before)
    above = moved(own[:, 3], "rows", 1)
    below = moved(own[:, 0], "rows", -1)

    parts, patch_gram = prepared(
        patch_weight, row(patch_bias), row(shift_mod), row(scale_mod)
    )
    rq, gq = projected(parts, query_weight, row(query_bias), row(query_gain), "project_query")
    rk, gk = projected(parts, key_weight, row(key_bias), row(key_gain), "project_key")
    grams = packed_grams(gq, gk)
    grams = grams + swapped(grams, "tm", 1)
    grams = grams + swapped(grams, "tm", 2) + swapped(grams, "tm", 4) + swapped(grams, "tm", 6)

    block = own_block(own, above, below)
    quad = jnp.stack([block] + [swapped(block, "rows", k) for k in (1, 2, 3)])
    quads = [quad] + [swapped(quad, "rows", 4 * k) for k in (1, 2, 3)]
    keep, send = selected(packing, quads)
    mine = keep + swapped(send, "tm", 1)
    mine = mine + swapped(mine, "tm", 2) + swapped(mine, "tm", 4) + swapped(mine, "tm", 6)
    other = swapped(mine, "tm", 1)
    core = (lax.axis_index("tm") % 2).astype(jnp.int32).reshape(1)
    return tokens(core, mine, other, patch_gram, grams, rq, rk)


def solution(mesh):
    in_specs = (
        P("tm", "rows", None, None),
        P(),
        P(),
        P(),
        P(),
        P(),
        P(),
        P(),
        P(),
        P(),
        P(None, "tm"),
        P("tm"),
        P("tm"),
        P(None, "tm"),
        P("tm"),
        P("tm"),
        P(),
    )
    out_specs = (P("rows", "tm"), P("rows", "tm"))
    return jax.shard_map(
        per_device, mesh=mesh, in_specs=in_specs, out_specs=out_specs, check_vma=False
    )
```

time: 145 us -> 85.1 us (0.59)
  blocking collectives: 50 us -> 0 us
  matrix products: 34 us -> 0 us
  Pallas kernels: 0 us -> 21.7 us
  starting transfers between devices: 15 us -> 31.2 us
  other arithmetic: 18.1 us -> 2.41 us
  local copies, waits for them, and re-layouts: 10.2 us -> 13.8 us
  waiting for transfers between devices: 16 us -> 13.7 us
    all_to_all x2 -> x0, blocking collectives: 50 us -> none  [the longest x1 41.9 us: per_device(): lax.all_to_all(outgoing, ('tm', 'rows'), split_axis=0, concat_axis=0, til...]
    dot_general x13 -> x0, matrix products: 34 us -> none  [the longest x1 11.9 us: per_device(): jnp.dot(modulated, key_weight, preferred_element_type=jnp.float32)]
    pallas_call x0 -> x8, Pallas kernels: none -> 21.7 us  [the longest x1 6.24 us: partial_latents(): pl.pallas_call(partial_kernel, out_shape=jax.ShapeDtypeStruct((4, 4, 16,...]
    ppermute x3 -> x18, starting transfers between devices: 10.2 us -> 31.2 us  [the longest x15 22.3 us: swapped(): lax.ppermute(x, axis, [(i, i ^ bits) for i in range(lax.axis_size(axis))])]
    convert_element_type x6 -> x0, other arithmetic: 11.1 us -> none  [the longest x1 5.35 us: per_device(): modulated = ((embedded - center) * lax.rsqrt(spread + epsilon) * (1.0 + s...]
    unnamed x30 -> x44, local copies, waits for them, and re-layouts: 3.11 us -> 11.7 us
    slice x6 -> x1, local copies, waits for them, and re-layouts: 5.76 us -> 0.01 us  [per_device(): before = moved(partial[2:], 'tm', 1)]
    all_to_all x1 -> x0, waiting for transfers between devices: 5.28 us -> none  [sent_to_all(): lax.all_to_all(jnp.broadcast_to(shard[None], (length, *shard.shape)), axi...]
  transfers between devices with their start and end apart: 4 -> 18, of which waited for: 4 -> 12; matrix products, arithmetic and copies ran while one was open for 3% -> 2% of each run, Pallas kernels for 0% -> 8%
where the time goes in v1:
time: 85.1 us; the launch traced here: 83.8 us
  starting transfers between devices  31.2 us (37%)
  Pallas kernels  21.7 us (25%)
  local copies, waits for them, and re-layouts  13.8 us (16%)
  waiting for transfers between devices  13.7 us (16%)
  other arithmetic  2.41 us (3%)
  between operations  0.91 us (1%)
    ppermute x15, starting transfers between devices, swapped(): lax.ppermute(x, axis, [(i, i ^ bits) for i in range(lax.axis_size(axis))])  22.3 us
    unnamed x44, local copies, waits for them, and re-layouts  11.7 us
    ppermute x3, starting transfers between devices, moved(): return lax.ppermute(x, axis, [(i, (i + by) % size) for i in range(size)])  8.89 us
    ppermute x15, waiting for transfers between devices, swapped(): lax.ppermute(x, axis, [(i, i ^ bits) for i in range(lax.axis_size(axis))])  7.14 us
    ppermute x3, waiting for transfers between devices, moved(): return lax.ppermute(x, axis, [(i, (i + by) % size) for i in range(size)])  6.6 us
    pallas_call x1, Pallas kernels, partial_latents(): pl.pallas_call(partial_kernel, out_shape=jax.ShapeDtypeStruct((4, 4, 16,...  6.24 us
    pallas_call x1, Pallas kernels, tokens(): pl.pallas_call(token_kernel, grid_spec=pltpu.PrefetchScalarGridSpec(num_s...  5.6 us
    pallas_call x2, Pallas kernels, projected(): pl.pallas_call(project_kernel, out_shape=[jax.ShapeDtypeStruct((3 * EXT,...  3.39 us
  transfers between devices with their start and end apart: 18, of which 12 were waited for; matrix products, arithmetic and copies ran while one was open for 2% of the time, Pallas kernels for 8%

profile of v1, /device:TPU:1, one launch (start us, length us, event | category | flops | bytes accessed | tf_op | source)
XLA Modules:
  0.0 83.8 jit_solution(4598451966343175050)
XLA Ops:
  2.1 0.8 copy.19.lw
  2.9 3.3 %copy-done = bf16[3,3,3,384,384]{4,3,2,1,0:T(8,128)(2,1)S(1)} copy-done((bf16[3,3,3,384,384]{4,3,2,1,0:T(8,128)(2,1)S(1)}, bf16[3,3,3,384,384]{4,3,2,1,0:T(8,128)(2,1)}, u32[]{:S(2)}) %copy-start) | copy-done | bytes 7962648
  6.2 1.0 %copy-done.4 = bf16[2,2,128,384]{3,2,1,0:T(8,128)(2,1)S(1)} copy-done((bf16[2,2,128,384]{3,2,1,0:T(8,128)(2,1)S(1)}, bf16[2,2,128,384]{3,2,1,0:T(8,128)(2,1)}, u32[]{:S(2)}) %copy-start.4) | copy-done | bytes 393240
  7.9 6.2 %partial_latents.1 = f32[4,4,16,128]{3,2,1,0:T(8,128)S(1)} custom-call(bf16[512,384]{1,0:T(8,128)(2,1)S(1)} %bitcast.16, f32[1,384]{1,0:T(1,128)S(1)} %reshape.45.gain, f32[1,384]{1,0:T(1,128)S(1)} %reshape.46.bias, bf16[384,16]{1,0:T(8,128)(2,1)S(1)} %copy.19.lw, f32[1,16]{1,0:T(1,128)S(1)} %bitcast.20, bf16[27,384,384]{2,1,0:T(8,128)(2,1)S(1)} %bitcast.15), custom_call_target="tpu_custom_call" | custom-call | tf_op jit(solution)/shard_map/partial_latents/pallas_call | solution.py:83
  14.1 2.6 %collective-permute-start = (f32[2,4,16,128]{3,2,0,1:T(8,128)S(1)}, f32[2,4,16,128]{3,2,0,1:T(8,128)S(1)}, u32[]{:S(2)}, u32[]{:S(2)}) collective-permute-start(f32[2,4,16,128]{3,2,0,1:T(8,128)S(1)} %copy.24), channel_id=1, source_target_pairs={{0,16},{16,32},{32,48},{48,64},{64,80},{80,96},{96,112},{112,0},{1... | collective-permute-start | bytes 196616 | tf_op jit(solution)/shard_map/ppermute | solution.py:309
  16.7 1.3 %collective-permute-done = f32[2,4,16,128]{3,2,0,1:T(8,128)S(1)} collective-permute-done((f32[2,4,16,128]{3,2,0,1:T(8,128)S(1)}, f32[2,4,16,128]{3,2,0,1:T(8,128)S(1)}, u32[]{:S(2)}, u32[]{:S(2)}) %collective-permute-start) | collective-permute-done | bytes 65568 | tf_op jit(solution)/shard_map/ppermute | solution.py:309
  18.1 6.3 %collective-permute-start.2 = (f32[2,16,128]{2,1,0:T(8,128)S(1)}, f32[2,16,128]{2,1,0:T(8,128)S(1)}, u32[]{:S(2)}, u32[]{:S(2)}) collective-permute-start(f32[2,16,128]{2,1,0:T(8,128)S(1)} %get-tuple-element.20), channel_id=1, source_target_pairs={{0,15},{1,0},{2,1},{3,2},{4,3},{5,4},{6,5},{7,6},{8,7},{9,8},{10,9... | collective-permute-start | bytes 49160 | tf_op jit(solution)/shard_map/ppermute | solution.py:309
  25.3 5.0 %collective-permute-done.1.above = f32[2,16,128]{2,1,0:T(8,128)S(1)} collective-permute-done((f32[2,16,128]{2,1,0:T(8,128)S(1)}, f32[2,16,128]{2,1,0:T(8,128)S(1)}, u32[]{:S(2)}, u32[]{:S(2)}) %collective-permute-start.1) | collective-permute-done | bytes 16416 | tf_op jit(solution)/shard_map/ppermute | solution.py:309
  30.9 1.6 %own_block.1 = bf16[64,128]{1,0:T(8,128)(2,1)} custom-call(f32[2,4,16,128]{3,2,1,0:T(8,128)} %copy.22.own, f32[2,16,128]{2,1,0:T(8,128)} %copy-done.16, f32[2,16,128]{2,1,0:T(8,128)} %copy-done.15), custom_call_target="tpu_custom_call" | custom-call | tf_op jit(solution)/shard_map/own_block/pallas_call | solution.py:199
  32.5 3.2 %collective-permute-start.3 = (bf16[64,128]{1,0:T(8,128)(2,1)}, bf16[64,128]{1,0:T(8,128)(2,1)S(1)}, u32[]{:S(2)}, u32[]{:S(2)}) collective-permute-start(bf16[64,128]{1,0:T(8,128)(2,1)} %own_block.1), channel_id=1, source_target_pairs={{0,1},{1,0},{2,3},{3,2},{4,5},{5,4},{6,7},{7,6},{8,9},{9,8},{10,11... | collective-permute-start | bytes 49160 | tf_op jit(solution)/shard_map/ppermute | solution.py:304
  38.5 2.8 %collective-permute-start.6 = (bf16[4,64,128]{2,1,0:T(8,128)(2,1)S(1)}, bf16[4,64,128]{2,1,0:T(8,128)(2,1)S(1)}, u32[]{:S(2)}, u32[]{:S(2)}) collective-permute-start(bf16[4,64,128]{2,1,0:T(8,128)(2,1)S(1)} %pad_maximum_fusion.b0), channel_id=1, source_target_pairs={{0,4},{1,5},{2,6},{3,7},{4,0},{5,1},{6,2},{7,3},{8,12},{9,13},{10,... | collective-permute-start | bytes 196616 | tf_op jit(solution)/shard_map/ppermute | solution.py:304
  41.4 1.1 %collective-permute-done.8.b3 = bf16[4,64,128]{2,1,0:T(8,128)(2,1)S(1)} collective-permute-done((bf16[4,64,128]{2,1,0:T(8,128)(2,1)S(1)}, bf16[4,64,128]{2,1,0:T(8,128)(2,1)S(1)}, u32[]{:S(2)}, u32[]{:S(2)}) %collective-permute-start.8) | collective-permute-done | bytes 65568 | tf_op jit(solution)/shard_map/ppermute | solution.py:304
  44.4 1.9 %select_blocks.1 = (bf16[4,64,128]{2,1,0:T(8,128)(2,1)}, bf16[4,64,128]{2,1,0:T(8,128)(2,1)}) custom-call(s32[128]{0:T(128)} %packing.1, bf16[4,64,128]{2,1,0:T(8,128)(2,1)} %copy-done.11, bf16[4,64,128]{2,1,0:T(8,128)(2,1)} %copy-done.14, bf16[4,64,128]{2,1,0:T(8,128)(2,1)} %copy-done.13, bf16[4,64,128]{2,1,0:T(8,128)(2,1)} %copy-done.12), custom_call_target="tpu_custom_call" | custom-call | tf_op jit(solution)/shard_map/select_blocks/pallas_call | solution.py:227
  46.3 6.7 %collective-permute-start.9 = (bf16[4,64,128]{2,1,0:T(8,128)(2,1)}, bf16[4,64,128]{2,1,0:T(8,128)(2,1)S(1)}, u32[]{:S(2)}, u32[]{:S(2)}) collective-permute-start(bf16[4,64,128]{2,1,0:T(8,128)(2,1)} %get-tuple-element.11), channel_id=1, source_target_pairs={{0,16},{16,0},{32,48},{48,32},{64,80},{80,64},{96,112},{112,96},{1... | collective-permute-start | bytes 196616 | tf_op jit(solution)/shard_map/ppermute | solution.py:304
  53.0 1.1 %collective-permute-done.9 = bf16[4,64,128]{2,1,0:T(8,128)(2,1)S(1)} collective-permute-done((bf16[4,64,128]{2,1,0:T(8,128)(2,1)}, bf16[4,64,128]{2,1,0:T(8,128)(2,1)S(1)}, u32[]{:S(2)}, u32[]{:S(2)}) %collective-permute-start.9) | collective-permute-done | bytes 65568 | tf_op jit(solution)/shard_map/ppermute | solution.py:304
  54.2 0.9 %add.33 = bf16[4,64,128]{2,1,0:T(8,128)(2,1)S(1)} add(bf16[4,64,128]{2,1,0:T(8,128)(2,1)} %get-tuple-element.10, bf16[4,64,128]{2,1,0:T(8,128)(2,1)S(1)} %collective-permute-done.9) | non-fusion elementwise | flops 32768 | bytes 196608 | tf_op jit(solution)/shard_map/add | solution.py:359
  55.0 1.4 %collective-permute-start.12 = (bf16[4,64,128]{2,1,0:T(8,128)(2,1)S(1)}, bf16[4,64,128]{2,1,0:T(8,128)(2,1)S(1)}, u32[]{:S(2)}, u32[]{:S(2)}) collective-permute-start(bf16[4,64,128]{2,1,0:T(8,128)(2,1)S(1)} %add.33), channel_id=1, source_target_pairs={{0,96},{16,112},{32,64},{48,80},{64,32},{80,48},{96,0},{112,16},{1... | collective-permute-start | bytes 196616 | tf_op jit(solution)/shard_map/ppermute | solution.py:304
  56.9 1.5 %collective-permute-start.10 = (bf16[4,64,128]{2,1,0:T(8,128)(2,1)S(1)}, bf16[4,64,128]{2,1,0:T(8,128)(2,1)S(1)}, u32[]{:S(2)}, u32[]{:S(2)}) collective-permute-start(bf16[4,64,128]{2,1,0:T(8,128)(2,1)S(1)} %add.33), channel_id=1, source_target_pairs={{0,32},{16,48},{32,0},{48,16},{64,96},{80,112},{96,64},{112,80},{1... | collective-permute-start | bytes 196616 | tf_op jit(solution)/shard_map/ppermute | solution.py:304
  58.5 1.5 %prepare_patch.1 = (bf16[160,5120]{1,0:T(8,128)(2,1)S(1)}, f32[80,80]{1,0:T(8,128)S(1)}) custom-call(bf16[64,5120]{1,0:T(8,128)(2,1)S(1)} %copy-done.3, f32[1,5120]{1,0:T(1,128)S(1)} %bitcast.17, f32[1,5120]{1,0:T(1,128)S(1)} %bitcast.18, f32[1,5120]{1,0:T(1,128)S(1)} %bitcast.19), custom_call_target="tpu_custom_call" | custom-call | tf_op jit(solution)/shard_map/prepare_patch/pallas_call | solution.py:122
  59.9 2.9 %copy-done.1 = bf16[5120,640]{1,0:T(8,128)(2,1)S(1)} copy-done((bf16[5120,640]{1,0:T(8,128)(2,1)S(1)}, bf16[5120,640]{1,0:T(8,128)(2,1)}, u32[]{:S(2)}) %copy-start.1) | copy-done | bytes 6553624
  62.8 1.7 %project_key.1 = (bf16[240,640]{1,0:T(8,128)(2,1)S(1)}, f32[80,80]{1,0:T(8,128)S(1)}) custom-call(bf16[160,5120]{1,0:T(8,128)(2,1)S(1)} %get-tuple-element.13.parts, bf16[5120,640]{1,0:T(8,128)(2,1)S(1)} %copy-done.1, f32[1,640]{1,0:T(1,128)S(1)} %reshape.54.bias, f32[1,640]{1,0:T(1,128)S(1)} %reshape.55.gain), custom_call_target="tpu_custom_call" | custom-call | tf_op jit(solution)/shard_map/project_key/pallas_call | solution.py:150
  64.5 1.2 %copy-done.2 = bf16[5120,640]{1,0:T(8,128)(2,1)S(1)} copy-done((bf16[5120,640]{1,0:T(8,128)(2,1)S(1)}, bf16[5120,640]{1,0:T(8,128)(2,1)}, u32[]{:S(2)}) %copy-start.2) | copy-done | bytes 6553624
  65.7 1.7 %project_query.1 = (bf16[240,640]{1,0:T(8,128)(2,1)S(1)}, f32[80,80]{1,0:T(8,128)S(1)}) custom-call(bf16[160,5120]{1,0:T(8,128)(2,1)S(1)} %get-tuple-element.13.parts, bf16[5120,640]{1,0:T(8,128)(2,1)S(1)} %copy-done.2, f32[1,640]{1,0:T(1,128)S(1)} %reshape.52.bias, f32[1,640]{1,0:T(1,128)S(1)} %reshape.53.gain), custom_call_target="tpu_custom_call" | custom-call | tf_op jit(solution)/shard_map/project_query/pallas_call | solution.py:150
  68.0 1.5 %pack_grams.1 = f32[80,128]{1,0:T(8,128)} custom-call(f32[80,80]{1,0:T(8,128)} %copy-done.6, f32[80,80]{1,0:T(8,128)} %copy-done.5), custom_call_target="tpu_custom_call" | custom-call | tf_op jit(solution)/shard_map/pack_grams/pallas_call | solution.py:172
  69.5 1.2 %collective-permute-start.14 = (f32[80,128]{1,0:T(8,128)}, f32[80,128]{1,0:T(8,128)S(1)}, u32[]{:S(2)}, u32[]{:S(2)}) collective-permute-start(f32[80,128]{1,0:T(8,128)} %pack_grams.1), channel_id=1, source_target_pairs={{0,16},{16,0},{32,48},{48,32},{64,80},{80,64},{96,112},{112,96},{1... | collective-permute-start | bytes 122888 | tf_op jit(solution)/shard_map/ppermute | solution.py:304
  70.7 1.1 %collective-permute-done.14 = f32[80,128]{1,0:T(8,128)S(1)} collective-permute-done((f32[80,128]{1,0:T(8,128)}, f32[80,128]{1,0:T(8,128)S(1)}, u32[]{:S(2)}, u32[]{:S(2)}) %collective-permute-start.14) | collective-permute-done | bytes 40992 | tf_op jit(solution)/shard_map/ppermute | solution.py:304
  71.8 0.8 add.37
  72.5 1.3 %collective-permute-start.17 = (f32[80,128]{1,0:T(8,128)S(1)}, f32[80,128]{1,0:T(8,128)S(1)}, u32[]{:S(2)}, u32[]{:S(2)}) collective-permute-start(f32[80,128]{1,0:T(8,128)S(1)} %add.37), channel_id=1, source_target_pairs={{0,96},{16,112},{32,64},{48,80},{64,32},{80,48},{96,0},{112,16},{1... | collective-permute-start | bytes 122888 | tf_op jit(solution)/shard_map/ppermute | solution.py:304
  74.3 1.5 %collective-permute-start.15 = (f32[80,128]{1,0:T(8,128)S(1)}, f32[80,128]{1,0:T(8,128)S(1)}, u32[]{:S(2)}, u32[]{:S(2)}) collective-permute-start(f32[80,128]{1,0:T(8,128)S(1)} %add.37), channel_id=1, source_target_pairs={{0,32},{16,48},{32,0},{48,16},{64,96},{80,112},{96,64},{112,80},{1... | collective-permute-start | bytes 122888 | tf_op jit(solution)/shard_map/ppermute | solution.py:304
  75.8 1.3 %collective-permute-start.13 = (bf16[4,64,128]{2,1,0:T(8,128)(2,1)S(1)}, bf16[4,64,128]{2,1,0:T(8,128)(2,1)S(1)}, u32[]{:S(2)}, u32[]{:S(2)}) collective-permute-start(bf16[4,64,128]{2,1,0:T(8,128)(2,1)S(1)} %add_add_fusion.mine), channel_id=1, source_target_pairs={{0,16},{16,0},{32,48},{48,32},{64,80},{80,64},{96,112},{112,96},{1... | collective-permute-start | bytes 196616 | tf_op jit(solution)/shard_map/ppermute | solution.py:304
  77.1 1.1 %collective-permute-done.16 = f32[80,128]{1,0:T(8,128)S(1)} collective-permute-done((f32[80,128]{1,0:T(8,128)S(1)}, f32[80,128]{1,0:T(8,128)S(1)}, u32[]{:S(2)}, u32[]{:S(2)}) %collective-permute-start.16) | collective-permute-done | bytes 40992 | tf_op jit(solution)/shard_map/ppermute | solution.py:304
  78.2 5.6 %tokens.1 = (bf16[1024,640]{1,0:T(8,128)(2,1)}, bf16[1024,640]{1,0:T(8,128)(2,1)}) custom-call(s32[1]{0:T(128)} %bitcast.core, bf16[4,64,128]{2,1,0:T(8,128)(2,1)S(1)} %add_add_fusion.mine, bf16[4,64,128]{2,1,0:T(8,128)(2,1)S(1)} %collective-permute-done.13.other, f32[80,80]{1,0:T(8,128)S(1)} %get-tuple-element.12.patch_gram, ...), custom_call_target="tpu_custom_call" | custom-call | tf_op jit(solution)/shard_map/tokens/pallas_call | solution.py:285
  (71 shorter events, 10.0 us)
Async XLA Ops:
  0.6 57.7 %copy-start.17 = (f32[640]{0:T(1024)S(1)}, f32[640]{0:T(1024)}, u32[]{:S(2)}) copy-start(f32[640]{0:T(1024)} %param.28) | copy-start | bytes 7684
  0.6 57.7 %copy-start.18 = (f32[640]{0:T(1024)S(1)}, f32[640]{0:T(1024)}, u32[]{:S(2)}) copy-start(f32[640]{0:T(1024)} %param.29) | copy-start | bytes 7684
  0.7 57.7 %copy-start.19 = (f32[640]{0:T(1024)S(1)}, f32[640]{0:T(1024)}, u32[]{:S(2)}) copy-start(f32[640]{0:T(1024)} %param.31) | copy-start | bytes 7684
  0.7 57.7 %copy-start.20 = (f32[640]{0:T(1024)S(1)}, f32[640]{0:T(1024)}, u32[]{:S(2)}) copy-start(f32[640]{0:T(1024)} %param.32) | copy-start | bytes 7684
  0.7 57.7 %copy-start.9 = (f32[5120]{0:T(1024)S(1)}, f32[5120]{0:T(1024)}, u32[]{:S(2)}) copy-start(f32[5120]{0:T(1024)} %param.26) | copy-start | bytes 61444
  0.7 57.7 %copy-start.8 = (f32[5120]{0:T(1024)S(1)}, f32[5120]{0:T(1024)}, u32[]{:S(2)}) copy-start(f32[5120]{0:T(1024)} %param.25) | copy-start | bytes 61444
  0.7 57.7 %copy-start.7 = (f32[5120]{0:T(1024)S(1)}, f32[5120]{0:T(1024)}, u32[]{:S(2)}) copy-start(f32[5120]{0:T(1024)} %param.24) | copy-start | bytes 61444
  2.9 3.3 %copy-start = (bf16[3,3,3,384,384]{4,3,2,1,0:T(8,128)(2,1)S(1)}, bf16[3,3,3,384,384]{4,3,2,1,0:T(8,128)(2,1)}, u32[]{:S(2)}) copy-start(bf16[3,3,3,384,384]{4,3,2,1,0:T(8,128)(2,1)} %param.19) | copy-start | bytes 23887876
  7.9 50.6 %copy-start.3 = (bf16[64,5120]{1,0:T(8,128)(2,1)S(1)}, bf16[64,5120]{1,0:T(8,128)(2,1)}, u32[]{:S(2)}) copy-start(bf16[64,5120]{1,0:T(8,128)(2,1)} %pw.1) | copy-start | bytes 1966084
  14.1 3.9 %collective-permute-start = (f32[2,4,16,128]{3,2,0,1:T(8,128)S(1)}, f32[2,4,16,128]{3,2,0,1:T(8,128)S(1)}, u32[]{:S(2)}, u32[]{:S(2)}) collective-permute-start(f32[2,4,16,128]{3,2,0,1:T(8,128)S(1)} %copy.24), channel_id=1, source_target_pairs={{0,16},{16,32},{32,48},{48,64},{64,80},{80,96},{96,112},{112,0},{1... | collective-permute-start | bytes 196616 | tf_op jit(solution)/shard_map/ppermute | solution.py:309
  18.1 7.1 %collective-permute-start.2 = (f32[2,16,128]{2,1,0:T(8,128)S(1)}, f32[2,16,128]{2,1,0:T(8,128)S(1)}, u32[]{:S(2)}, u32[]{:S(2)}) collective-permute-start(f32[2,16,128]{2,1,0:T(8,128)S(1)} %get-tuple-element.20), channel_id=1, source_target_pairs={{0,15},{1,0},{2,1},{3,2},{4,3},{5,4},{6,5},{7,6},{8,7},{9,8},{10,9... | collective-permute-start | bytes 49160 | tf_op jit(solution)/shard_map/ppermute | solution.py:309
  24.4 5.9 %collective-permute-start.1 = (f32[2,16,128]{2,1,0:T(8,128)S(1)}, f32[2,16,128]{2,1,0:T(8,128)S(1)}, u32[]{:S(2)}, u32[]{:S(2)}) collective-permute-start(f32[2,16,128]{2,1,0:T(8,128)S(1)} %get-tuple-element.21), channel_id=1, source_target_pairs={{0,1},{1,2},{2,3},{3,4},{4,5},{5,6},{6,7},{7,8},{8,9},{9,10},{10,1... | collective-permute-start | bytes 49160 | tf_op jit(solution)/shard_map/ppermute | solution.py:309
  25.3 5.0 %copy-start.15 = (f32[2,16,128]{2,1,0:T(8,128)}, f32[2,16,128]{2,1,0:T(8,128)S(1)}, u32[]{:S(2)}) copy-start(f32[2,16,128]{2,1,0:T(8,128)S(1)} %collective-permute-done.2.below) | copy-start | bytes 49156
  32.5 4.0 %collective-permute-start.5 = (bf16[64,128]{1,0:T(8,128)(2,1)}, bf16[64,128]{1,0:T(8,128)(2,1)S(1)}, u32[]{:S(2)}, u32[]{:S(2)}) collective-permute-start(bf16[64,128]{1,0:T(8,128)(2,1)} %own_block.1), channel_id=1, source_target_pairs={{0,3},{1,2},{2,1},{3,0},{4,7},{5,6},{6,5},{7,4},{8,11},{9,10},{10,... | collective-permute-start | bytes 49160 | tf_op jit(solution)/shard_map/ppermute | solution.py:304
  32.5 4.3 %collective-permute-start.4 = (bf16[64,128]{1,0:T(8,128)(2,1)}, bf16[64,128]{1,0:T(8,128)(2,1)S(1)}, u32[]{:S(2)}, u32[]{:S(2)}) collective-permute-start(bf16[64,128]{1,0:T(8,128)(2,1)} %own_block.1), channel_id=1, source_target_pairs={{0,2},{1,3},{2,0},{3,1},{4,6},{5,7},{6,4},{7,5},{8,10},{9,11},{10,... | collective-permute-start | bytes 49160 | tf_op jit(solution)/shard_map/ppermute | solution.py:304
  32.5 4.8 %collective-permute-start.3 = (bf16[64,128]{1,0:T(8,128)(2,1)}, bf16[64,128]{1,0:T(8,128)(2,1)S(1)}, u32[]{:S(2)}, u32[]{:S(2)}) collective-permute-start(bf16[64,128]{1,0:T(8,128)(2,1)} %own_block.1), channel_id=1, source_target_pairs={{0,1},{1,0},{2,3},{3,2},{4,5},{5,4},{6,7},{7,6},{8,9},{9,8},{10,11... | collective-permute-start | bytes 49160 | tf_op jit(solution)/shard_map/ppermute | solution.py:304
  38.0 5.7 %copy-start.11 = (bf16[4,64,128]{2,1,0:T(8,128)(2,1)}, bf16[4,64,128]{2,1,0:T(8,128)(2,1)S(1)}, u32[]{:S(2)}) copy-start(bf16[4,64,128]{2,1,0:T(8,128)(2,1)S(1)} %pad_maximum_fusion.b0) | copy-start | bytes 196612
  38.0 4.4 %collective-permute-start.8 = (bf16[4,64,128]{2,1,0:T(8,128)(2,1)S(1)}, bf16[4,64,128]{2,1,0:T(8,128)(2,1)S(1)}, u32[]{:S(2)}, u32[]{:S(2)}) collective-permute-start(bf16[4,64,128]{2,1,0:T(8,128)(2,1)S(1)} %pad_maximum_fusion.b0), channel_id=1, source_target_pairs={{0,12},{1,13},{2,14},{3,15},{4,8},{5,9},{6,10},{7,11},{8,4},{9,5},... | collective-permute-start | bytes 196616 | tf_op jit(solution)/shard_map/ppermute | solution.py:304
  38.5 4.6 %collective-permute-start.7 = (bf16[4,64,128]{2,1,0:T(8,128)(2,1)S(1)}, bf16[4,64,128]{2,1,0:T(8,128)(2,1)S(1)}, u32[]{:S(2)}, u32[]{:S(2)}) collective-permute-start(bf16[4,64,128]{2,1,0:T(8,128)(2,1)S(1)} %pad_maximum_fusion.b0), channel_id=1, source_target_pairs={{0,8},{1,9},{2,10},{3,11},{4,12},{5,13},{6,14},{7,15},{8,0},{9,1},... | collective-permute-start | bytes 196616 | tf_op jit(solution)/shard_map/ppermute | solution.py:304
  38.5 5.2 %collective-permute-start.6 = (bf16[4,64,128]{2,1,0:T(8,128)(2,1)S(1)}, bf16[4,64,128]{2,1,0:T(8,128)(2,1)S(1)}, u32[]{:S(2)}, u32[]{:S(2)}) collective-permute-start(bf16[4,64,128]{2,1,0:T(8,128)(2,1)S(1)} %pad_maximum_fusion.b0), channel_id=1, source_target_pairs={{0,4},{1,5},{2,6},{3,7},{4,0},{5,1},{6,2},{7,3},{8,12},{9,13},{10,... | collective-permute-start | bytes 196616 | tf_op jit(solution)/shard_map/ppermute | solution.py:304
  46.3 7.8 %collective-permute-start.9 = (bf16[4,64,128]{2,1,0:T(8,128)(2,1)}, bf16[4,64,128]{2,1,0:T(8,128)(2,1)S(1)}, u32[]{:S(2)}, u32[]{:S(2)}) collective-permute-start(bf16[4,64,128]{2,1,0:T(8,128)(2,1)} %get-tuple-element.11), channel_id=1, source_target_pairs={{0,16},{16,0},{32,48},{48,32},{64,80},{80,64},{96,112},{112,96},{1... | collective-permute-start | bytes 196616 | tf_op jit(solution)/shard_map/ppermute | solution.py:304
  55.0 19.3 %collective-permute-start.12 = (bf16[4,64,128]{2,1,0:T(8,128)(2,1)S(1)}, bf16[4,64,128]{2,1,0:T(8,128)(2,1)S(1)}, u32[]{:S(2)}, u32[]{:S(2)}) collective-permute-start(bf16[4,64,128]{2,1,0:T(8,128)(2,1)S(1)} %add.33), channel_id=1, source_target_pairs={{0,96},{16,112},{32,64},{48,80},{64,32},{80,48},{96,0},{112,16},{1... | collective-permute-start | bytes 196616 | tf_op jit(solution)/shard_map/ppermute | solution.py:304
  56.4 19.4 %collective-permute-start.11 = (bf16[4,64,128]{2,1,0:T(8,128)(2,1)S(1)}, bf16[4,64,128]{2,1,0:T(8,128)(2,1)S(1)}, u32[]{:S(2)}, u32[]{:S(2)}) collective-permute-start(bf16[4,64,128]{2,1,0:T(8,128)(2,1)S(1)} %add.33), channel_id=1, source_target_pairs={{0,64},{16,80},{32,96},{48,112},{64,0},{80,16},{96,32},{112,48},{1... | collective-permute-start | bytes 196616 | tf_op jit(solution)/shard_map/ppermute | solution.py:304
  56.9 18.9 %collective-permute-start.10 = (bf16[4,64,128]{2,1,0:T(8,128)(2,1)S(1)}, bf16[4,64,128]{2,1,0:T(8,128)(2,1)S(1)}, u32[]{:S(2)}, u32[]{:S(2)}) collective-permute-start(bf16[4,64,128]{2,1,0:T(8,128)(2,1)S(1)} %add.33), channel_id=1, source_target_pairs={{0,32},{16,48},{32,0},{48,16},{64,96},{80,112},{96,64},{112,80},{1... | collective-permute-start | bytes 196616 | tf_op jit(solution)/shard_map/ppermute | solution.py:304
  59.9 2.9 %copy-start.1 = (bf16[5120,640]{1,0:T(8,128)(2,1)S(1)}, bf16[5120,640]{1,0:T(8,128)(2,1)}, u32[]{:S(2)}) copy-start(bf16[5120,640]{1,0:T(8,128)(2,1)} %w.3) | copy-start | bytes 19660804
  62.8 2.9 %copy-start.2 = (bf16[5120,640]{1,0:T(8,128)(2,1)S(1)}, bf16[5120,640]{1,0:T(8,128)(2,1)}, u32[]{:S(2)}) copy-start(bf16[5120,640]{1,0:T(8,128)(2,1)} %w.2) | copy-start | bytes 19660804
  65.7 1.7 %copy-start.5 = (f32[80,80]{1,0:T(8,128)}, f32[80,80]{1,0:T(8,128)S(1)}, u32[]{:S(2)}) copy-start(f32[80,80]{1,0:T(8,128)S(1)} %get-tuple-element.15.gk) | copy-start | bytes 76804
  69.5 2.3 %collective-permute-start.14 = (f32[80,128]{1,0:T(8,128)}, f32[80,128]{1,0:T(8,128)S(1)}, u32[]{:S(2)}, u32[]{:S(2)}) collective-permute-start(f32[80,128]{1,0:T(8,128)} %pack_grams.1), channel_id=1, source_target_pairs={{0,16},{16,0},{32,48},{48,32},{64,80},{80,64},{96,112},{112,96},{1... | collective-permute-start | bytes 122888 | tf_op jit(solution)/shard_map/ppermute | solution.py:304
  72.5 4.6 %collective-permute-start.17 = (f32[80,128]{1,0:T(8,128)S(1)}, f32[80,128]{1,0:T(8,128)S(1)}, u32[]{:S(2)}, u32[]{:S(2)}) collective-permute-start(f32[80,128]{1,0:T(8,128)S(1)} %add.37), channel_id=1, source_target_pairs={{0,96},{16,112},{32,64},{48,80},{64,32},{80,48},{96,0},{112,16},{1... | collective-permute-start | bytes 122888 | tf_op jit(solution)/shard_map/ppermute | solution.py:304
  73.8 4.4 %collective-permute-start.16 = (f32[80,128]{1,0:T(8,128)S(1)}, f32[80,128]{1,0:T(8,128)S(1)}, u32[]{:S(2)}, u32[]{:S(2)}) collective-permute-start(f32[80,128]{1,0:T(8,128)S(1)} %add.37), channel_id=1, source_target_pairs={{0,64},{16,80},{32,96},{48,112},{64,0},{80,16},{96,32},{112,48},{1... | collective-permute-start | bytes 122888 | tf_op jit(solution)/shard_map/ppermute | solution.py:304
  74.3 3.8 %collective-permute-start.15 = (f32[80,128]{1,0:T(8,128)S(1)}, f32[80,128]{1,0:T(8,128)S(1)}, u32[]{:S(2)}, u32[]{:S(2)}) collective-permute-start(f32[80,128]{1,0:T(8,128)S(1)} %add.37), channel_id=1, source_target_pairs={{0,32},{16,48},{32,0},{48,16},{64,96},{80,112},{96,64},{112,80},{1... | collective-permute-start | bytes 122888 | tf_op jit(solution)/shard_map/ppermute | solution.py:304
  75.8 2.4 %collective-permute-start.13 = (bf16[4,64,128]{2,1,0:T(8,128)(2,1)S(1)}, bf16[4,64,128]{2,1,0:T(8,128)(2,1)S(1)}, u32[]{:S(2)}, u32[]{:S(2)}) collective-permute-start(bf16[4,64,128]{2,1,0:T(8,128)(2,1)S(1)} %add_add_fusion.mine), channel_id=1, source_target_pairs={{0,16},{16,0},{32,48},{48,32},{64,80},{80,64},{96,112},{112,96},{1... | collective-permute-start | bytes 196616 | tf_op jit(solution)/shard_map/ppermute | solution.py:304
  (7 other events, 5.4 us)

commit v2 on v1

v2 whole, which is shorter than its diff:
```python
import functools

import jax
import jax.numpy as jnp
from jax import lax
from jax.experimental import pallas as pl
from jax.experimental.pallas import tpu as pltpu
from jax.sharding import PartitionSpec as P

epsilon = 1e-06
bf16 = jnp.bfloat16
f32 = jnp.float32
VMEM = pl.BlockSpec(memory_space=pltpu.VMEM)
SMEM = pl.BlockSpec(memory_space=pltpu.SMEM)
HBM = pl.BlockSpec(memory_space=pltpu.HBM)
MIB = 1 << 20
EXT = 80


def mm(a, b, ca, cb):
    return lax.dot_general(a, b, (((ca,), (cb,)), ((), ())), preferred_element_type=f32)


def halves(x):
    high = x.astype(bf16)
    return high, (x - high.astype(f32)).astype(bf16)


def iota(shape, dim):
    return lax.broadcasted_iota(jnp.int32, shape, dim)


def call(kernel, name, out_shape, in_specs, limit, scratch=(), cost=None, **more):
    more.setdefault("out_specs", jax.tree.map(lambda _: VMEM, out_shape))
    return pl.pallas_call(
        kernel,
        out_shape=out_shape,
        in_specs=in_specs,
        scratch_shapes=list(scratch),
        compiler_params=pltpu.CompilerParams(vmem_limit_bytes=limit * MIB),
        cost_estimate=cost,
        name=name,
        **more,
    )


def array(shape, kind):
    return jax.ShapeDtypeStruct(shape, kind)


def partial_kernel(
    feat_hbm, gain_hbm, bias_hbm, lwt_hbm, lb_hbm, cw_hbm, out,
    feat, gain, bias, lwt_ref, lb, cw, wt, gt, sems,
):
    small = [
        pltpu.make_async_copy(a, b, sems.at[9 + i])
        for i, (a, b) in enumerate(
            (
                (feat_hbm, feat),
                (gain_hbm, gain),
                (bias_hbm, bias),
                (lwt_hbm, lwt_ref),
                (lb_hbm, lb),
            )
        )
    ]
    for c in small:
        c.start()
    chunk = 3
    copies = [
        pltpu.make_async_copy(
            cw_hbm.at[pl.ds(i * chunk, chunk)], cw.at[pl.ds(i * chunk, chunk)], sems.at[i]
        )
        for i in range(27 // chunk)
    ]
    for c in copies:
        c.start()
    for c in small:
        c.wait()
    values = feat[...].astype(f32)
    mean = jnp.mean(values * values, axis=-1, keepdims=True)
    y = values * lax.rsqrt(mean + epsilon) * gain[...].reshape(1, -1)
    act = (y / (1.0 + jnp.exp(-y))).astype(bf16)
    lwt = lwt_ref[...]
    direct = mm(lwt, feat[...], 1, 1)
    const = jnp.sum(lwt.astype(f32) * bias[...].reshape(1, -1), axis=1, keepdims=True)
    const = const + jnp.transpose(lb[...].reshape(1, -1))
    for i, c in enumerate(copies):
        c.wait()
        for k in range(i * chunk, (i + 1) * chunk):
            high, low = halves(mm(lwt, cw[k], 1, 1))
            wt[pl.ds(k * 16, 16), :] = high
            wt[pl.ds(432 + k * 16, 16), :] = low
    gt[...] = mm(wt[...], act, 1, 1)
    lane = iota((16, 128), 1)
    for fo in range(4):
        for ro in range(4):
            by_e = []
            for e in range(3):
                total = None
                for f in range(2):
                    for r in range(2):
                        a, b = f + 2 - fo, r + 2 - ro
                        if not (0 <= a < 3 and 0 <= b < 3):
                            continue
                        k, q = (a * 3 + b) * 3 + e, f * 2 + r
                        part = (
                            gt[pl.ds(k * 16, 16), pl.ds(q * 128, 128)]
                            + gt[pl.ds(432 + k * 16, 16), pl.ds(q * 128, 128)]
                        )
                        total = part if total is None else total + part
                by_e.append(total)
            left = jnp.where(lane == 0, 0.0, pltpu.roll(by_e[0], 1, 1))
            right = jnp.where(lane == 127, 0.0, pltpu.roll(by_e[2], 127, 1))
            value = left + by_e[1] + right
            if fo < 2 and 1 <= ro < 3:
                q = fo * 2 + ro - 1
                value = value + direct[:, q * 128 : (q + 1) * 128] + const
            out[fo, ro] = value


def partial_latents(*args):
    return call(
        partial_kernel,
        "partial_latents",
        array((4, 4, 16, 128), f32),
        [HBM] * 6,
        20,
        scratch=[
            pltpu.VMEM((512, 384), bf16),
            pltpu.VMEM((384,), f32),
            pltpu.VMEM((384,), f32),
            pltpu.VMEM((16, 384), bf16),
            pltpu.VMEM((16,), f32),
            pltpu.VMEM((27, 384, 384), bf16),
            pltpu.VMEM((864, 384), bf16),
            pltpu.VMEM((864, 512), f32),
            pltpu.SemaphoreType.DMA((14,)),
        ],
    )(*args)


def weights_kernel(
    pw, pb, shift, scale, wq_hbm, wk_hbm, bq, bk, gq, gk,
    rq, rk, patch_gram, grams, wq, wk, parts, sems,
):
    width = pw.shape[1]
    chunk = width // 4
    copies = []
    for n, (a, b) in enumerate(((wq_hbm, wq), (wk_hbm, wk))):
        copies.append([])
        for i in range(4):
            at = pl.ds(i * chunk, chunk)
            c = pltpu.make_async_copy(a.at[at], b.at[at], sems.at[n * 4 + i])
            c.start()
            copies[n].append(c)
    to, at = iota((64, 64), 0), iota((64, 64), 1)
    wanted = 4 * (to % 16) + 2 * ((to // 16) % 2) + to // 32
    order = jnp.where(at == wanted, 1.0, 0.0).astype(bf16)
    rows = mm(order, pw[...], 1, 0)
    rows = rows - jnp.mean(rows, axis=1, keepdims=True)
    const = pb[...] - jnp.mean(pb[...], axis=1, keepdims=True)
    const_tail = jnp.where(iota((16, width), 0) == 0, const, 0.0)
    centered = jnp.concatenate([rows, const_tail], axis=0)
    high, low = halves(centered)
    both = mm(jnp.concatenate([high, low], axis=0), high, 1, 1)
    cross = both[EXT:, :]
    patch_gram[...] = (both[:EXT, :] + cross + jnp.transpose(cross)) * (1.0 / width)
    scaled = centered * (1.0 + scale[...])
    high, low = halves(jnp.where(iota((EXT, width), 0) == 65, shift[...], scaled))
    parts[pl.ds(0, EXT), :] = high
    parts[pl.ds(EXT, EXT), :] = low
    found = []
    for n, (w, bias, gain, right) in enumerate(((wq, bq, gq, rq), (wk, bk, gk, rk))):
        both = None
        for i, c in enumerate(copies[n]):
            c.wait()
            at = pl.ds(i * chunk, chunk)
            part = mm(parts[:, at], w[at, :], 1, 0)
            both = part if both is None else both + part
        rows = both[:EXT, :] + both[EXT:, :]
        rows = rows + jnp.where(iota(rows.shape, 0) == 65, bias[...], 0.0)
        high, low = halves(rows)
        pairs = mm(jnp.concatenate([high, low], axis=0), high, 1, 1)
        cross = pairs[EXT:, :]
        found.append(pairs[:EXT, :] + cross + jnp.transpose(cross))
        high, low = halves(rows * gain[...])
        right[pl.ds(0, EXT), :] = high
        right[pl.ds(EXT, EXT), :] = high
        right[pl.ds(2 * EXT, EXT), :] = low
    i, j = iota((EXT, EXT), 0), iota((EXT, EXT), 1)
    diagonal = jnp.sum(jnp.where(i == j, found[1], 0.0), axis=1, keepdims=True)
    grams[:, :EXT] = jnp.where(i >= j, found[0], found[1])
    grams[:, EXT:] = jnp.broadcast_to(diagonal, (EXT, 128 - EXT))


def weights_only(pw, pb, shift, scale, wq, wk, bq, bk, gq, gk):
    width, part = wq.shape
    return call(
        weights_kernel,
        "weights_only",
        [
            array((3 * EXT, part), bf16),
            array((3 * EXT, part), bf16),
            array((EXT, EXT), f32),
            array((EXT, 128), f32),
        ],
        [VMEM] * 4 + [HBM] * 2 + [VMEM] * 4,
        36,
        scratch=[
            pltpu.VMEM((width, part), bf16),
            pltpu.VMEM((width, part), bf16),
            pltpu.VMEM((2 * EXT, width), bf16),
            pltpu.SemaphoreType.DMA((8,)),
        ],
        cost=pl.CostEstimate(
            flops=4 * 2 * EXT * width * part * 4, bytes_accessed=2 * width * part * 2, transcendentals=0
        ),
    )(pw, pb, shift, scale, wq, wk, bq, bk, gq, gk)


def block_kernel(own, above, below, out):
    row = lax.axis_index("rows")
    first = jnp.where(row == 0, 0.0, 1.0)
    final = jnp.where(row == lax.axis_size("rows") - 1, 0.0, 1.0)
    upper = [(own[f, 1] + above[f] * first).astype(bf16) for f in range(2)]
    lower = [(own[f, 2] + below[f] * final).astype(bf16) for f in range(2)]
    values = jnp.concatenate(
        [jnp.concatenate(upper, axis=1), jnp.concatenate(lower, axis=1)], axis=0
    )
    source, target = iota((256, 256), 0), iota((256, 256), 1)
    wanted = ((target // 64) % 2) * 128 + 2 * (target % 64) + target // 128
    pick = jnp.where(source == wanted, 1.0, 0.0).astype(bf16)
    spread = mm(values, pick, 1, 0).astype(bf16)
    block = jnp.concatenate([spread[:, :128], spread[:, 128:]], axis=0)
    for i in range(out.shape[0]):
        out[i] = block


def own_block(own, above, below):
    return call(
        block_kernel, "own_block", array((lax.axis_size("rows"), 64, 128), bf16), [VMEM] * 3, 4
    )(own, above, below)


def select_kernel(packing, blocks, keep, send):
    t, r = lax.axis_index("tm"), lax.axis_index("rows")
    core = t % 2
    for out, half in ((keep, core), (send, 1 - core)):
        for i in range(4):
            ident = packing[r * 8 + half * 4 + i]
            here = jnp.where(ident // 16 == t, 1.0, 0.0).astype(bf16)
            out[i] = blocks[ident % 16] * here


def selected(packing, blocks):
    return call(
        select_kernel, "select_blocks", [array((4, 64, 128), bf16)] * 2, [SMEM, VMEM], 4
    )(packing, blocks)


def forms_kernel(patch_gram, grams, left):
    i, j = iota((EXT, EXT), 0), iota((EXT, EXT), 1)
    total = grams[...] * (1.0 / 5120.0)
    square = total[:, :EXT]
    gq = jnp.where(i > j, 2.0 * square, 0.0) + jnp.where(i == j, square, 0.0)
    gk = jnp.where(i > j, 2.0 * jnp.transpose(square), 0.0)
    gk = gk + jnp.where(i == j, total[:, EXT : EXT + 1], 0.0)
    left[pl.ds(0, EXT), :] = jnp.concatenate(halves(patch_gram[...]), axis=1)
    for n, g in enumerate((gq, gk)):
        end = jnp.sum(jnp.where((i == 65) & (j == 65), g, 0.0), keepdims=True)
        g = jnp.where((i == 66) & (j == 64), end, g)
        left[pl.ds((n + 1) * EXT, EXT), :] = jnp.concatenate(halves(g), axis=1)


def quadratic_forms(patch_gram, grams):
    return call(
        forms_kernel, "quadratic_forms", array((3 * EXT, 2 * EXT), bf16), [VMEM] * 2, 4
    )(patch_gram, grams)


def token_kernel(other_half, x_ref, left, rq, rk, *refs):
    q_out, k_out, q_buf, k_buf, sems = refs[-5:]
    core = lax.axis_index("tm") % 2
    place = (1 - core if other_half else core) * 512
    copies = []
    for part in range(2):
        x = jnp.concatenate([x_ref[2 * part], x_ref[2 * part + 1]], axis=1)
        tail = iota((EXT - 64, 256), 0)
        xf = jnp.concatenate([x.astype(f32), jnp.where(tail == 0, 1.0, 0.0)], axis=0)
        xe = xf.astype(bf16)
        t = mm(left[...], jnp.concatenate([xe, xe], axis=0), 1, 0)
        spread = jnp.sum(t[:EXT] * xf, axis=0, keepdims=True)
        scale = lax.rsqrt(spread + epsilon)
        for n, (right, buf, out) in enumerate(((rq, q_buf, q_out), (rk, k_buf, k_out))):
            tn = t[(n + 1) * EXT : (n + 2) * EXT]
            squares = (
                scale * scale * jnp.sum(tn * xf, axis=0, keepdims=True)
                + scale * tn[65:66]
                + tn[66:67]
            )
            beta = lax.rsqrt(squares + epsilon)
            alpha = scale * beta
            y = xf * alpha + jnp.where(iota((EXT, 256), 0) == 65, beta, 0.0)
            high, low = halves(y)
            lhs = jnp.concatenate([high, low, high], axis=0)
            buf[part] = mm(lhs, right[...], 0, 0).astype(bf16)
            c = pltpu.make_async_copy(
                buf.at[part], out.at[pl.ds(pl.multiple_of(place + part * 256, 256), 256)], sems.at[part * 2 + n]
            )
            c.start()
            copies.append(c)
    for c in copies:
        c.wait()


def tokens(x, left, rq, rk, before=None):
    width = rq.shape[1]
    given = () if before is None else tuple(before)
    return call(
        functools.partial(token_kernel, before is not None),
        "tokens_other" if given else "tokens_mine",
        [array((1024, width), bf16)] * 2,
        [VMEM] * 4 + [HBM] * len(given),
        12,
        scratch=[
            pltpu.VMEM((2, 256, width), bf16),
            pltpu.VMEM((2, 256, width), bf16),
            pltpu.SemaphoreType.DMA((4,)),
        ],
        out_specs=[HBM, HBM],
        input_output_aliases={4: 0, 5: 1} if given else {},
    )(x, left, rq, rk, *given)


def in_hbm(x):
    return pltpu.with_memory_space_constraint(x, pltpu.HBM)


def swapped(x, axis, bits):
    return lax.ppermute(x, axis, [(i, i ^ bits) for i in range(lax.axis_size(axis))])


def moved(x, axis, by):
    size = lax.axis_size(axis)
    return lax.ppermute(x, axis, [(i, (i + by) % size) for i in range(size)])


def per_device(
    features,
    block_gain,
    conv_weight,
    conv_bias,
    latent_weight,
    latent_bias,
    patch_weight,
    patch_bias,
    shift_mod,
    scale_mod,
    query_weight,
    query_bias,
    query_gain,
    key_weight,
    key_bias,
    key_gain,
    packing,
):
    channels = features.shape[-1]
    row = lambda v: v.reshape(1, -1)
    partial = partial_latents(
        *map(
            in_hbm,
            (
                features.reshape(-1, channels),
                block_gain,
                conv_bias,
                latent_weight.T,
                latent_bias,
                conv_weight.reshape(27, channels, channels),
            ),
        )
    )
    before = moved(partial[2:], "tm", 1)
    own = partial[:2] + jnp.where(lax.axis_index("tm") == 0, 0.0, before)
    above = moved(own[:, 3], "rows", 1)
    below = moved(own[:, 0], "rows", -1)
    copies = own_block(own, above, below)
    copies, patch_weight = lax.optimization_barrier((copies, patch_weight))
    plane = lax.all_to_all(copies, "rows", 0, 0, tiled=True)

    rq, rk, patch_gram, grams = weights_only(
        patch_weight,
        row(patch_bias),
        row(shift_mod),
        row(scale_mod),
        in_hbm(query_weight),
        in_hbm(key_weight),
        row(query_bias),
        row(key_bias),
        row(query_gain),
        row(key_gain),
    )
    plane, grams = lax.optimization_barrier((plane, grams))
    grams = grams + swapped(grams, "tm", 1)
    grams = grams + swapped(grams, "tm", 2) + swapped(grams, "tm", 4) + swapped(grams, "tm", 6)
    left = quadratic_forms(patch_gram, grams)

    keep, send = selected(packing, plane)
    mine = keep + swapped(send, "tm", 1)
    mine = mine + swapped(mine, "tm", 2) + swapped(mine, "tm", 4) + swapped(mine, "tm", 6)
    other = swapped(mine, "tm", 1)
    return tokens(other, left, rq, rk, tokens(mine, left, rq, rk))


def solution(mesh):
    in_specs = (
        P("tm", "rows", None, None),
        P(),
        P(),
        P(),
        P(),
        P(),
        P(),
        P(),
        P(),
        P(),
        P(None, "tm"),
        P("tm"),
        P("tm"),
        P(None, "tm"),
        P("tm"),
        P("tm"),
        P(),
    )
    out_specs = (P("rows", "tm"), P("rows", "tm"))
    return jax.shard_map(
        per_device, mesh=mesh, in_specs=in_specs, out_specs=out_specs, check_vma=False
    )
```

time: 85.1 us -> 56.9 us (0.67)
  local copies, waits for them, and re-layouts: 13.8 us -> 0.09 us
  starting transfers between devices: 31.2 us -> 26.2 us
  waiting for transfers between devices: 13.7 us -> 10 us
  Pallas kernels: 21.7 us -> 19.1 us
  other arithmetic: 2.41 us -> 0.07 us
    unnamed x44 -> x19, local copies, waits for them, and re-layouts: 11.7 us -> 0.05 us
    ppermute x15 -> x9, starting transfers between devices: 22.3 us -> 13.8 us  [swapped(): lax.ppermute(x, axis, [(i, i ^ bits) for i in range(lax.axis_size(axis))])]
    ppermute x15 -> x9, waiting for transfers between devices: 7.14 us -> 2.85 us  [swapped(): lax.ppermute(x, axis, [(i, i ^ bits) for i in range(lax.axis_size(axis))])]
    all_to_all x0 -> x1, starting transfers between devices: none -> 3.53 us  [per_device(): plane = lax.all_to_all(copies, 'rows', 0, 0, tiled=True)]
    pallas_call x8 -> x7, Pallas kernels: 21.7 us -> 19.1 us  [the longest x1 7.83 us: weights_only(): call(weights_kernel, 'weights_only', [array((3 * EXT, part), bf16), array...]
    reshape x6 -> x4, local copies, waits for them, and re-layouts: 1.42 us -> 0.01 us  [per_device(): row = lambda v: v.reshape(1, -1)]
  transfers between devices with their start and end apart: 18 -> 13, of which waited for: 12 -> 6; matrix products, arithmetic and copies ran while one was open for 2% -> 0% of each run, Pallas kernels for 8% -> 18%
where the time goes in v2:
time: 56.9 us; the launch traced here: 56.3 us
  starting transfers between devices  26.2 us (46%)
  Pallas kernels  19.1 us (34%)
  waiting for transfers between devices  10 us (18%)
  between operations  0.91 us (2%)
    ppermute x9, starting transfers between devices, swapped(): lax.ppermute(x, axis, [(i, i ^ bits) for i in range(lax.axis_size(axis))])  13.8 us
    ppermute x3, starting transfers between devices, moved(): return lax.ppermute(x, axis, [(i, (i + by) % size) for i in range(size)])  8.89 us
    pallas_call x1, Pallas kernels, weights_only(): call(weights_kernel, 'weights_only', [array((3 * EXT, part), bf16), array...  7.83 us
    ppermute x3, waiting for transfers between devices, moved(): return lax.ppermute(x, axis, [(i, (i + by) % size) for i in range(size)])  7.15 us
    pallas_call x1, Pallas kernels, partial_latents(): call(partial_kernel, 'partial_latents', array((4, 4, 16, 128), f32), [HBM...  5.65 us
    pallas_call x2, Pallas kernels, tokens(): call(functools.partial(token_kernel, before is not None), 'tokens_other'...  3.74 us
    all_to_all x1, starting transfers between devices, per_device(): plane = lax.all_to_all(copies, 'rows', 0, 0, tiled=True)  3.53 us
    ppermute x9, waiting for transfers between devices, swapped(): lax.ppermute(x, axis, [(i, i ^ bits) for i in range(lax.axis_size(axis))])  2.85 us
  transfers between devices with their start and end apart: 13, of which 6 were waited for; matrix products, arithmetic and copies ran while one was open for 0% of the time, Pallas kernels for 18%

profile of v2, /device:TPU:1, one launch (start us, length us, event | category | flops | bytes accessed | tf_op | source)
XLA Modules:
  0.0 56.3 jit_solution(2646102974849460699)
XLA Ops:
  0.7 5.6 %partial_latents.1 = f32[4,4,16,128]{3,2,1,0:T(8,128)S(1)} custom-call(bf16[512,384]{1,0:T(8,128)(2,1)} %bitcast.14, f32[384]{0:T(512)} %gain_hbm.1, f32[384]{0:T(512)} %bias_hbm.1, bf16[16,384]{1,0:T(8,128)(2,1)} %bitcast.15, f32[16]{0:T(128)} %lb_hbm.1, bf16[27,384,384]{2,1,0:T(8,128)(2,1)} %bitcast.13), custom_call_target="tpu_custom_call" | custom-call | tf_op jit(solution)/shard_map/partial_latents/pallas_call | solution.py:123
  6.3 0.0 copy-start.1
  6.3 0.0 copy-start.2
  6.4 0.0 copy-start.3
  6.4 0.0 copy-start.4
  6.4 2.6 %collective-permute-start = (f32[2,4,16,128]{3,2,0,1:T(8,128)S(1)}, f32[2,4,16,128]{3,2,0,1:T(8,128)S(1)}, u32[]{:S(2)}, u32[]{:S(2)}) collective-permute-start(f32[2,4,16,128]{3,2,0,1:T(8,128)S(1)} %copy.25), channel_id=1, source_target_pairs={{0,16},{16,32},{32,48},{48,64},{64,80},{80,96},{96,112},{112,0},{1... | collective-permute-start | bytes 196616 | tf_op jit(solution)/shard_map/ppermute | solution.py:346
  9.0 1.3 %collective-permute-done = f32[2,4,16,128]{3,2,0,1:T(8,128)S(1)} collective-permute-done((f32[2,4,16,128]{3,2,0,1:T(8,128)S(1)}, f32[2,4,16,128]{3,2,0,1:T(8,128)S(1)}, u32[]{:S(2)}, u32[]{:S(2)}) %collective-permute-start) | collective-permute-done | bytes 65568 | tf_op jit(solution)/shard_map/ppermute | solution.py:346
  10.4 6.3 %collective-permute-start.2 = (f32[2,16,128]{2,1,0:T(8,128)S(1)}, f32[2,16,128]{2,1,0:T(8,128)S(1)}, u32[]{:S(2)}, u32[]{:S(2)}) collective-permute-start(f32[2,16,128]{2,1,0:T(8,128)S(1)} %get-tuple-element.28), channel_id=1, source_target_pairs={{0,15},{1,0},{2,1},{3,2},{4,3},{5,4},{6,5},{7,6},{8,7},{9,8},{10,9... | collective-permute-start | bytes 49160 | tf_op jit(solution)/shard_map/ppermute | solution.py:346
  16.8 0.8 %collective-permute-done.2.below = f32[2,16,128]{2,1,0:T(8,128)S(1)} collective-permute-done((f32[2,16,128]{2,1,0:T(8,128)S(1)}, f32[2,16,128]{2,1,0:T(8,128)S(1)}, u32[]{:S(2)}, u32[]{:S(2)}) %collective-permute-start.2) | collective-permute-done | bytes 16416 | tf_op jit(solution)/shard_map/ppermute | solution.py:346
  17.5 5.0 %collective-permute-done.1.above = f32[2,16,128]{2,1,0:T(8,128)S(1)} collective-permute-done((f32[2,16,128]{2,1,0:T(8,128)S(1)}, f32[2,16,128]{2,1,0:T(8,128)S(1)}, u32[]{:S(2)}, u32[]{:S(2)}) %collective-permute-start.1) | collective-permute-done | bytes 16416 | tf_op jit(solution)/shard_map/ppermute | solution.py:346
  22.6 0.9 %own_block.1 = bf16[16,64,128]{2,1,0:T(8,128)(2,1)} custom-call(f32[2,4,16,128]{3,2,1,0:T(8,128)S(1)} %copy.23.own, f32[2,16,128]{2,1,0:T(8,128)S(1)} %collective-permute-done.1.above, f32[2,16,128]{2,1,0:T(8,128)S(1)} %collective-permute-done.2.below), custom_call_target="tpu_custom_call" | custom-call | tf_op jit(solution)/shard_map/own_block/pallas_call | solution.py:241
  23.5 3.5 %all-to-all-start = ((bf16[16,64,128]{2,1,0:T(8,128)(2,1)}), bf16[16,64,128]{2,1,0:T(8,128)(2,1)S(1)}, u32[]{:S(2)}, u32[]{:S(2)}) async-start(bf16[16,64,128]{2,1,0:T(8,128)(2,1)} %own_block.1), calls=%async_computation | async-start | bytes 524288 | tf_op jit(solution)/shard_map/all_to_all | solution.py:389
  27.0 0.0 copy-start
  27.1 7.8 %weights_only.1 = (bf16[240,640]{1,0:T(8,128)(2,1)S(1)}, bf16[240,640]{1,0:T(8,128)(2,1)S(1)}, f32[80,80]{1,0:T(8,128)S(1)}, f32[80,128]{1,0:T(8,128)S(1)}) custom-call(bf16[64,5120]{1,0:T(8,128)(2,1)S(1)} %copy-done.1, f32[1,5120]{1,0:T(1,128)S(1)} %bitcast.10, f32[1,5120]{1,0:T(1,128)S(1)} %bitcast.11, f32[1,5120]{1,0:T(1,128)S(1)} %bitcast.12, ...), custom_call_target="tpu_custom_call" | custom-call | flops 8388608000 | bytes 13107200 | tf_op jit(solution)/shard_map/weights_only/pallas_call | solution.py:199
  34.9 0.0 all-to-all-done.blocks
  34.9 0.6 %select_blocks.1 = (bf16[4,64,128]{2,1,0:T(8,128)(2,1)S(1)}, bf16[4,64,128]{2,1,0:T(8,128)(2,1)S(1)}) custom-call(s32[128]{0:T(128)S(1)} %copy-done, bf16[16,64,128]{2,1,0:T(8,128)(2,1)S(1)} %all-to-all-done.blocks), custom_call_target="tpu_custom_call" | custom-call | tf_op jit(solution)/shard_map/select_blocks/pallas_call | solution.py:257
  35.6 4.7 %collective-permute-start.3 = (bf16[4,64,128]{2,1,0:T(8,128)(2,1)S(1)}, bf16[4,64,128]{2,1,0:T(8,128)(2,1)S(1)}, u32[]{:S(2)}, u32[]{:S(2)}) collective-permute-start(bf16[4,64,128]{2,1,0:T(8,128)(2,1)S(1)} %get-tuple-element.19), channel_id=1, source_target_pairs={{0,16},{16,0},{32,48},{48,32},{64,80},{80,64},{96,112},{112,96},{1... | collective-permute-start | bytes 196616 | tf_op jit(solution)/shard_map/ppermute | solution.py:341
  40.3 0.9 %collective-permute-done.3 = bf16[4,64,128]{2,1,0:T(8,128)(2,1)S(1)} collective-permute-done((bf16[4,64,128]{2,1,0:T(8,128)(2,1)S(1)}, bf16[4,64,128]{2,1,0:T(8,128)(2,1)S(1)}, u32[]{:S(2)}, u32[]{:S(2)}) %collective-permute-start.3) | collective-permute-done | bytes 65568 | tf_op jit(solution)/shard_map/ppermute | solution.py:341
  41.2 1.3 %collective-permute-start.6 = (bf16[4,64,128]{2,1,0:T(8,128)(2,1)S(1)}, bf16[4,64,128]{2,1,0:T(8,128)(2,1)S(1)}, u32[]{:S(2)}, u32[]{:S(2)}) collective-permute-start(bf16[4,64,128]{2,1,0:T(8,128)(2,1)S(1)} %add.28), channel_id=1, source_target_pairs={{0,96},{16,112},{32,64},{48,80},{64,32},{80,48},{96,0},{112,16},{1... | collective-permute-start | bytes 196616 | tf_op jit(solution)/shard_map/ppermute | solution.py:341
  42.6 0.5 collective-permute-start.5
  43.1 1.5 %collective-permute-start.4 = (bf16[4,64,128]{2,1,0:T(8,128)(2,1)S(1)}, bf16[4,64,128]{2,1,0:T(8,128)(2,1)S(1)}, u32[]{:S(2)}, u32[]{:S(2)}) collective-permute-start(bf16[4,64,128]{2,1,0:T(8,128)(2,1)S(1)} %add.28), channel_id=1, source_target_pairs={{0,32},{16,48},{32,0},{48,16},{64,96},{80,112},{96,64},{112,80},{1... | collective-permute-start | bytes 196616 | tf_op jit(solution)/shard_map/ppermute | solution.py:341
  44.6 1.2 %collective-permute-start.8 = (f32[80,128]{1,0:T(8,128)S(1)}, f32[80,128]{1,0:T(8,128)S(1)}, u32[]{:S(2)}, u32[]{:S(2)}) collective-permute-start(f32[80,128]{1,0:T(8,128)S(1)} %get-tuple-element.21), channel_id=1, source_target_pairs={{0,16},{16,0},{32,48},{48,32},{64,80},{80,64},{96,112},{112,96},{1... | collective-permute-start | bytes 122888 | tf_op jit(solution)/shard_map/ppermute | solution.py:341
  45.7 0.9 %collective-permute-done.8 = f32[80,128]{1,0:T(8,128)S(1)} collective-permute-done((f32[80,128]{1,0:T(8,128)S(1)}, f32[80,128]{1,0:T(8,128)S(1)}, u32[]{:S(2)}, u32[]{:S(2)}) %collective-permute-start.8) | collective-permute-done | bytes 40992 | tf_op jit(solution)/shard_map/ppermute | solution.py:341
  46.6 1.3 %collective-permute-start.11 = (f32[80,128]{1,0:T(8,128)S(1)}, f32[80,128]{1,0:T(8,128)S(1)}, u32[]{:S(2)}, u32[]{:S(2)}) collective-permute-start(f32[80,128]{1,0:T(8,128)S(1)} %add.32), channel_id=1, source_target_pairs={{0,96},{16,112},{32,64},{48,80},{64,32},{80,48},{96,0},{112,16},{1... | collective-permute-start | bytes 122888 | tf_op jit(solution)/shard_map/ppermute | solution.py:341
  47.9 0.5 collective-permute-start.10
  48.4 1.5 %collective-permute-start.9 = (f32[80,128]{1,0:T(8,128)S(1)}, f32[80,128]{1,0:T(8,128)S(1)}, u32[]{:S(2)}, u32[]{:S(2)}) collective-permute-start(f32[80,128]{1,0:T(8,128)S(1)} %add.32), channel_id=1, source_target_pairs={{0,32},{16,48},{32,0},{48,16},{64,96},{80,112},{96,64},{112,80},{1... | collective-permute-start | bytes 122888 | tf_op jit(solution)/shard_map/ppermute | solution.py:341
  49.9 0.0 collective-permute-done.5
  49.9 1.3 %collective-permute-start.7 = (bf16[4,64,128]{2,1,0:T(8,128)(2,1)S(1)}, bf16[4,64,128]{2,1,0:T(8,128)(2,1)S(1)}, u32[]{:S(2)}, u32[]{:S(2)}) collective-permute-start(bf16[4,64,128]{2,1,0:T(8,128)(2,1)S(1)} %add_add_fusion.x_ref), channel_id=1, source_target_pairs={{0,16},{16,0},{32,48},{48,32},{64,80},{80,64},{96,112},{112,96},{1... | collective-permute-start | bytes 196616 | tf_op jit(solution)/shard_map/ppermute | solution.py:341
  51.2 1.1 %collective-permute-done.10 = f32[80,128]{1,0:T(8,128)S(1)} collective-permute-done((f32[80,128]{1,0:T(8,128)S(1)}, f32[80,128]{1,0:T(8,128)S(1)}, u32[]{:S(2)}, u32[]{:S(2)}) %collective-permute-start.10) | collective-permute-done | bytes 40992 | tf_op jit(solution)/shard_map/ppermute | solution.py:341
  52.3 0.3 quadratic_forms.1.left
  52.6 1.9 %tokens_mine.1 = (bf16[1024,640]{1,0:T(8,128)(2,1)}, bf16[1024,640]{1,0:T(8,128)(2,1)}) custom-call(bf16[4,64,128]{2,1,0:T(8,128)(2,1)S(1)} %add_add_fusion.x_ref, bf16[240,160]{1,0:T(8,128)(2,1)S(1)} %quadratic_forms.1.left, bf16[240,640]{1,0:T(8,128)(2,1)S(1)} %get-tuple-element.22.rq, bf16[240,640]{1,0:T(8,128)(2,1)S(1)} %get-tuple-element.23.rk), custom_call_target="tpu_custom_call" | custom-call | tf_op jit(solution)/shard_map/tokens_mine/pallas_call | solution.py:320
  54.5 1.9 %tokens_other.1 = (bf16[1024,640]{1,0:T(8,128)(2,1)}, bf16[1024,640]{1,0:T(8,128)(2,1)}) custom-call(bf16[4,64,128]{2,1,0:T(8,128)(2,1)S(1)} %collective-permute-done.7.x_ref, bf16[240,160]{1,0:T(8,128)(2,1)S(1)} %quadratic_forms.1.left, bf16[240,640]{1,0:T(8,128)(2,1)S(1)} %get-tuple-element.22.rq, ...), custom_call_target="tpu_custom_call", output_to_operand_aliasing={{0}: (4, {}), {1}: (5, {})} | custom-call | tf_op jit(solution)/shard_map/tokens_other/pallas_call | solution.py:320
  (32 shorter events, 0.2 us)
Async XLA Ops:
  0.6 16.0 %copy-start.5 = (f32[640]{0:T(1024)S(1)}, f32[640]{0:T(1024)}, u32[]{:S(2)}) copy-start(f32[640]{0:T(1024)} %param.28) | copy-start | bytes 7684
  0.6 16.0 %copy-start.6 = (f32[640]{0:T(1024)S(1)}, f32[640]{0:T(1024)}, u32[]{:S(2)}) copy-start(f32[640]{0:T(1024)} %param.29) | copy-start | bytes 7684
  0.7 16.0 %copy-start.7 = (f32[640]{0:T(1024)S(1)}, f32[640]{0:T(1024)}, u32[]{:S(2)}) copy-start(f32[640]{0:T(1024)} %param.31) | copy-start | bytes 7684
  0.7 16.1 %copy-start.8 = (f32[640]{0:T(1024)S(1)}, f32[640]{0:T(1024)}, u32[]{:S(2)}) copy-start(f32[640]{0:T(1024)} %param.32) | copy-start | bytes 7684
  6.3 20.7 %copy-start.1 = (bf16[64,5120]{1,0:T(8,128)(2,1)S(1)}, bf16[64,5120]{1,0:T(8,128)(2,1)}, u32[]{:S(2)}) copy-start(bf16[64,5120]{1,0:T(8,128)(2,1)} %pw) | copy-start | bytes 1966084
  6.3 20.7 %copy-start.2 = (f32[5120]{0:T(1024)S(1)}, f32[5120]{0:T(1024)}, u32[]{:S(2)}) copy-start(f32[5120]{0:T(1024)} %param.24) | copy-start | bytes 61444
  6.4 20.7 %copy-start.3 = (f32[5120]{0:T(1024)S(1)}, f32[5120]{0:T(1024)}, u32[]{:S(2)}) copy-start(f32[5120]{0:T(1024)} %param.25) | copy-start | bytes 61444
  6.4 20.7 %copy-start.4 = (f32[5120]{0:T(1024)S(1)}, f32[5120]{0:T(1024)}, u32[]{:S(2)}) copy-start(f32[5120]{0:T(1024)} %param.26) | copy-start | bytes 61444
  6.4 3.9 %collective-permute-start = (f32[2,4,16,128]{3,2,0,1:T(8,128)S(1)}, f32[2,4,16,128]{3,2,0,1:T(8,128)S(1)}, u32[]{:S(2)}, u32[]{:S(2)}) collective-permute-start(f32[2,4,16,128]{3,2,0,1:T(8,128)S(1)} %copy.25), channel_id=1, source_target_pairs={{0,16},{16,32},{32,48},{48,64},{64,80},{80,96},{96,112},{112,0},{1... | collective-permute-start | bytes 196616 | tf_op jit(solution)/shard_map/ppermute | solution.py:346
  10.4 7.1 %collective-permute-start.2 = (f32[2,16,128]{2,1,0:T(8,128)S(1)}, f32[2,16,128]{2,1,0:T(8,128)S(1)}, u32[]{:S(2)}, u32[]{:S(2)}) collective-permute-start(f32[2,16,128]{2,1,0:T(8,128)S(1)} %get-tuple-element.28), channel_id=1, source_target_pairs={{0,15},{1,0},{2,1},{3,2},{4,3},{5,4},{6,5},{7,6},{8,7},{9,8},{10,9... | collective-permute-start | bytes 49160 | tf_op jit(solution)/shard_map/ppermute | solution.py:346
  16.7 5.9 %collective-permute-start.1 = (f32[2,16,128]{2,1,0:T(8,128)S(1)}, f32[2,16,128]{2,1,0:T(8,128)S(1)}, u32[]{:S(2)}, u32[]{:S(2)}) collective-permute-start(f32[2,16,128]{2,1,0:T(8,128)S(1)} %get-tuple-element.29), channel_id=1, source_target_pairs={{0,1},{1,2},{2,3},{3,4},{4,5},{5,6},{6,7},{7,8},{8,9},{9,10},{10,1... | collective-permute-start | bytes 49160 | tf_op jit(solution)/shard_map/ppermute | solution.py:346
  23.5 11.4 %all-to-all-start = ((bf16[16,64,128]{2,1,0:T(8,128)(2,1)}), bf16[16,64,128]{2,1,0:T(8,128)(2,1)S(1)}, u32[]{:S(2)}, u32[]{:S(2)}) async-start(bf16[16,64,128]{2,1,0:T(8,128)(2,1)} %own_block.1), calls=%async_computation | async-start | bytes 524288 | tf_op jit(solution)/shard_map/all_to_all | solution.py:389
  27.0 7.9 %copy-start = (s32[128]{0:T(128)S(1)}, s32[128]{0:T(128)}, u32[]{:S(2)}) copy-start(s32[128]{0:T(128)} %packing.1) | copy-start | bytes 1540
  35.6 5.6 %collective-permute-start.3 = (bf16[4,64,128]{2,1,0:T(8,128)(2,1)S(1)}, bf16[4,64,128]{2,1,0:T(8,128)(2,1)S(1)}, u32[]{:S(2)}, u32[]{:S(2)}) collective-permute-start(bf16[4,64,128]{2,1,0:T(8,128)(2,1)S(1)} %get-tuple-element.19), channel_id=1, source_target_pairs={{0,16},{16,0},{32,48},{48,32},{64,80},{80,64},{96,112},{112,96},{1... | collective-permute-start | bytes 196616 | tf_op jit(solution)/shard_map/ppermute | solution.py:341
  41.2 7.2 %collective-permute-start.6 = (bf16[4,64,128]{2,1,0:T(8,128)(2,1)S(1)}, bf16[4,64,128]{2,1,0:T(8,128)(2,1)S(1)}, u32[]{:S(2)}, u32[]{:S(2)}) collective-permute-start(bf16[4,64,128]{2,1,0:T(8,128)(2,1)S(1)} %add.28), channel_id=1, source_target_pairs={{0,96},{16,112},{32,64},{48,80},{64,32},{80,48},{96,0},{112,16},{1... | collective-permute-start | bytes 196616 | tf_op jit(solution)/shard_map/ppermute | solution.py:341
  42.6 7.3 %collective-permute-start.5 = (bf16[4,64,128]{2,1,0:T(8,128)(2,1)S(1)}, bf16[4,64,128]{2,1,0:T(8,128)(2,1)S(1)}, u32[]{:S(2)}, u32[]{:S(2)}) collective-permute-start(bf16[4,64,128]{2,1,0:T(8,128)(2,1)S(1)} %add.28), channel_id=1, source_target_pairs={{0,64},{16,80},{32,96},{48,112},{64,0},{80,16},{96,32},{112,48},{1... | collective-permute-start | bytes 196616 | tf_op jit(solution)/shard_map/ppermute | solution.py:341
  43.1 6.8 %collective-permute-start.4 = (bf16[4,64,128]{2,1,0:T(8,128)(2,1)S(1)}, bf16[4,64,128]{2,1,0:T(8,128)(2,1)S(1)}, u32[]{:S(2)}, u32[]{:S(2)}) collective-permute-start(bf16[4,64,128]{2,1,0:T(8,128)(2,1)S(1)} %add.28), channel_id=1, source_target_pairs={{0,32},{16,48},{32,0},{48,16},{64,96},{80,112},{96,64},{112,80},{1... | collective-permute-start | bytes 196616 | tf_op jit(solution)/shard_map/ppermute | solution.py:341
  44.6 2.1 %collective-permute-start.8 = (f32[80,128]{1,0:T(8,128)S(1)}, f32[80,128]{1,0:T(8,128)S(1)}, u32[]{:S(2)}, u32[]{:S(2)}) collective-permute-start(f32[80,128]{1,0:T(8,128)S(1)} %get-tuple-element.21), channel_id=1, source_target_pairs={{0,16},{16,0},{32,48},{48,32},{64,80},{80,64},{96,112},{112,96},{1... | collective-permute-start | bytes 122888 | tf_op jit(solution)/shard_map/ppermute | solution.py:341
  46.6 4.6 %collective-permute-start.11 = (f32[80,128]{1,0:T(8,128)S(1)}, f32[80,128]{1,0:T(8,128)S(1)}, u32[]{:S(2)}, u32[]{:S(2)}) collective-permute-start(f32[80,128]{1,0:T(8,128)S(1)} %add.32), channel_id=1, source_target_pairs={{0,96},{16,112},{32,64},{48,80},{64,32},{80,48},{96,0},{112,16},{1... | collective-permute-start | bytes 122888 | tf_op jit(solution)/shard_map/ppermute | solution.py:341
  47.9 4.4 %collective-permute-start.10 = (f32[80,128]{1,0:T(8,128)S(1)}, f32[80,128]{1,0:T(8,128)S(1)}, u32[]{:S(2)}, u32[]{:S(2)}) collective-permute-start(f32[80,128]{1,0:T(8,128)S(1)} %add.32), channel_id=1, source_target_pairs={{0,64},{16,80},{32,96},{48,112},{64,0},{80,16},{96,32},{112,48},{1... | collective-permute-start | bytes 122888 | tf_op jit(solution)/shard_map/ppermute | solution.py:341
  48.4 3.8 %collective-permute-start.9 = (f32[80,128]{1,0:T(8,128)S(1)}, f32[80,128]{1,0:T(8,128)S(1)}, u32[]{:S(2)}, u32[]{:S(2)}) collective-permute-start(f32[80,128]{1,0:T(8,128)S(1)} %add.32), channel_id=1, source_target_pairs={{0,32},{16,48},{32,0},{48,16},{64,96},{80,112},{96,64},{112,80},{1... | collective-permute-start | bytes 122888 | tf_op jit(solution)/shard_map/ppermute | solution.py:341
  49.9 4.5 %collective-permute-start.7 = (bf16[4,64,128]{2,1,0:T(8,128)(2,1)S(1)}, bf16[4,64,128]{2,1,0:T(8,128)(2,1)S(1)}, u32[]{:S(2)}, u32[]{:S(2)}) collective-permute-start(bf16[4,64,128]{2,1,0:T(8,128)(2,1)S(1)} %add_add_fusion.x_ref), channel_id=1, source_target_pairs={{0,16},{16,0},{32,48},{48,32},{64,80},{80,64},{96,112},{112,96},{1... | collective-permute-start | bytes 196616 | tf_op jit(solution)/shard_map/ppermute | solution.py:341

commit v3 on v2

--- a/solution.py
+++ b/solution.py
@@ -48,12 +48,62 @@
     return jax.ShapeDtypeStruct(shape, kind)
 
 
-def partial_kernel(
-    feat_hbm, gain_hbm, bias_hbm, lwt_hbm, lb_hbm, cw_hbm, out,
-    feat, gain, bias, lwt_ref, lb, cw, wt, gt, sems,
+def folded(lwt, cw, wt, gt, act, copies, at, taps):
+    chunk = taps // len(copies)
+    for i, c in enumerate(copies):
+        c.wait()
+        for k in range(i * chunk, (i + 1) * chunk):
+            high, low = halves(mm(lwt, cw[at + k], 1, 1))
+            wt[pl.ds(k * 16, 16), :] = high
+            wt[pl.ds(144 + k * 16, 16), :] = low
+    gt[...] = mm(wt[...], act, 1, 1)
+
+
+def shifted_sum(by_e):
+    lane = iota((16, 128), 1)
+    left = jnp.where(lane == 0, 0.0, pltpu.roll(by_e[0], 1, 1))
+    right = jnp.where(lane == 127, 0.0, pltpu.roll(by_e[2], 127, 1))
+    return left + by_e[1] + right
+
+
+def contributions(gts, fo, ro):
+    by_e = []
+    for e in range(3):
+        total = None
+        for f in range(2):
+            for r in range(2):
+                a, b = f + 2 - fo, r + 2 - ro
+                if a not in gts or not 0 <= b < 3:
+                    continue
+                k, q = b * 3 + e, f * 2 + r
+                part = (
+                    gts[a][pl.ds(k * 16, 16), pl.ds(q * 128, 128)]
+                    + gts[a][pl.ds(144 + k * 16, 16), pl.ds(q * 128, 128)]
+                )
+                total = part if total is None else total + part
+        by_e.append(total)
+    return shifted_sum(by_e)
+
+
+def chunked(source, target, sems, start, count, size, first_sem):
+    found = []
+    for i in range(count):
+        c = pltpu.make_async_copy(
+            source.at[pl.ds(start + i * size, size)],
+            target.at[pl.ds(i * size, size)],
+            sems.at[first_sem + i],
+        )
+        c.start()
+        found.append(c)
+    return found
+
+
+def early_kernel(
+    feat_hbm, gain_hbm, bias_hbm, lwt_hbm, lb_hbm, cw_hbm, ahead, own, act_out,
+    feat, gain, bias, lwt_ref, lb, cw, wt, gt0, gt1, sems,
 ):
     small = [
-        pltpu.make_async_copy(a, b, sems.at[9 + i])
+        pltpu.make_async_copy(a, b, sems.at[6 + i])
         for i, (a, b) in enumerate(
             (
                 (feat_hbm, feat),
@@ -66,64 +116,36 @@
     ]
     for c in small:
         c.start()
-    chunk = 3
-    copies = [
-        pltpu.make_async_copy(
-            cw_hbm.at[pl.ds(i * chunk, chunk)], cw.at[pl.ds(i * chunk, chunk)], sems.at[i]
-        )
-        for i in range(27 // chunk)
-    ]
-    for c in copies:
-        c.start()
+    copies = chunked(cw_hbm, cw, sems, 0, 6, 3, 0)
     for c in small:
         c.wait()
     values = feat[...].astype(f32)
     mean = jnp.mean(values * values, axis=-1, keepdims=True)
     y = values * lax.rsqrt(mean + epsilon) * gain[...].reshape(1, -1)
     act = (y / (1.0 + jnp.exp(-y))).astype(bf16)
+    act_out[...] = act
     lwt = lwt_ref[...]
     direct = mm(lwt, feat[...], 1, 1)
     const = jnp.sum(lwt.astype(f32) * bias[...].reshape(1, -1), axis=1, keepdims=True)
     const = const + jnp.transpose(lb[...].reshape(1, -1))
-    for i, c in enumerate(copies):
-        c.wait()
-        for k in range(i * chunk, (i + 1) * chunk):
-            high, low = halves(mm(lwt, cw[k], 1, 1))
-            wt[pl.ds(k * 16, 16), :] = high
-            wt[pl.ds(432 + k * 16, 16), :] = low
-    gt[...] = mm(wt[...], act, 1, 1)
-    lane = iota((16, 128), 1)
-    for fo in range(4):
-        for ro in range(4):
-            by_e = []
-            for e in range(3):
-                total = None
-                for f in range(2):
-                    for r in range(2):
-                        a, b = f + 2 - fo, r + 2 - ro
-                        if not (0 <= a < 3 and 0 <= b < 3):
-                            continue
-                        k, q = (a * 3 + b) * 3 + e, f * 2 + r
-                        part = (
-                            gt[pl.ds(k * 16, 16), pl.ds(q * 128, 128)]
-                            + gt[pl.ds(432 + k * 16, 16), pl.ds(q * 128, 128)]
-                        )
-                        total = part if total is None else total + part
-                by_e.append(total)
-            left = jnp.where(lane == 0, 0.0, pltpu.roll(by_e[0], 1, 1))
-            right = jnp.where(lane == 127, 0.0, pltpu.roll(by_e[2], 127, 1))
-            value = left + by_e[1] + right
-            if fo < 2 and 1 <= ro < 3:
+    folded(lwt, cw, wt, gt0, act, copies[:3], 0, 9)
+    folded(lwt, cw, wt, gt1, act, copies[3:], 9, 9)
+    for ro in range(4):
+        for fo in (2, 3):
+            ahead[fo - 2, ro] = contributions({0: gt0, 1: gt1}, fo, ro)
+        own[0, ro] = jnp.zeros((16, 128), f32)
+        own[1, ro] = contributions({1: gt1}, 1, ro)
+        if 1 <= ro < 3:
+            for fo in range(2):
                 q = fo * 2 + ro - 1
-                value = value + direct[:, q * 128 : (q + 1) * 128] + const
-            out[fo, ro] = value
-
-
-def partial_latents(*args):
-    return call(
-        partial_kernel,
-        "partial_latents",
-        array((4, 4, 16, 128), f32),
+                own[fo, ro] += direct[:, q * 128 : (q + 1) * 128] + const
+
+
+def early_latents(*args):
+    return call(
+        early_kernel,
+        "early_latents",
+        [array((2, 4, 16, 128), f32), array((2, 4, 16, 128), f32), array((512, 384), bf16)],
         [HBM] * 6,
         20,
         scratch=[
@@ -132,11 +154,41 @@
             pltpu.VMEM((384,), f32),
             pltpu.VMEM((16, 384), bf16),
             pltpu.VMEM((16,), f32),
-            pltpu.VMEM((27, 384, 384), bf16),
-            pltpu.VMEM((864, 384), bf16),
-            pltpu.VMEM((864, 512), f32),
-            pltpu.SemaphoreType.DMA((14,)),
+            pltpu.VMEM((18, 384, 384), bf16),
+            pltpu.VMEM((288, 384), bf16),
+            pltpu.VMEM((288, 512), f32),
+            pltpu.VMEM((288, 512), f32),
+            pltpu.SemaphoreType.DMA((11,)),
         ],
+    )(*args)
+
+
+def late_kernel(own, act, lwt_hbm, cw_hbm, out, lwt, cw, wt, gt, sems):
+    small = pltpu.make_async_copy(lwt_hbm, lwt, sems.at[3])
+    small.start()
+    copies = chunked(cw_hbm, cw, sems, 18, 3, 3, 0)
+    small.wait()
+    folded(lwt[...], cw, wt, gt, act[...], copies, 0, 9)
+    for fo in range(2):
+        for ro in range(4):
+            out[fo, ro] = own[fo, ro] + contributions({2: gt}, fo, ro)
+
+
+def late_latents(*args):
+    return call(
+        late_kernel,
+        "late_latents",
+        array((2, 4, 16, 128), f32),
+        [VMEM] * 2 + [HBM] * 2,
+        10,
+        scratch=[
+            pltpu.VMEM((16, 384), bf16),
+            pltpu.VMEM((9, 384, 384), bf16),
+            pltpu.VMEM((288, 384), bf16),
+            pltpu.VMEM((288, 512), f32),
+            pltpu.SemaphoreType.DMA((4,)),
+        ],
+        cost=pl.CostEstimate(flops=3 * 10**9, bytes_accessed=5 * 10**6, transcendentals=0),
     )(*args)
 
 
@@ -219,38 +271,46 @@
     )(pw, pb, shift, scale, wq, wk, bq, bk, gq, gk)
 
 
-def block_kernel(own, above, below, out):
-    row = lax.axis_index("rows")
-    first = jnp.where(row == 0, 0.0, 1.0)
-    final = jnp.where(row == lax.axis_size("rows") - 1, 0.0, 1.0)
-    upper = [(own[f, 1] + above[f] * first).astype(bf16) for f in range(2)]
-    lower = [(own[f, 2] + below[f] * final).astype(bf16) for f in range(2)]
-    values = jnp.concatenate(
-        [jnp.concatenate(upper, axis=1), jnp.concatenate(lower, axis=1)], axis=0
-    )
+def block_kernel(own, before, out):
+    first = jnp.where(lax.axis_index("tm") == 0, 0.0, 1.0)
+    rows = []
+    for ro in (1, 2, 3, 0):
+        frames = [own[f, ro] + before[f, ro] * first for f in range(2)]
+        rows.append(jnp.concatenate(frames, axis=1).astype(bf16))
     source, target = iota((256, 256), 0), iota((256, 256), 1)
     wanted = ((target // 64) % 2) * 128 + 2 * (target % 64) + target // 128
     pick = jnp.where(source == wanted, 1.0, 0.0).astype(bf16)
-    spread = mm(values, pick, 1, 0).astype(bf16)
-    block = jnp.concatenate([spread[:, :128], spread[:, 128:]], axis=0)
+    spread = mm(jnp.concatenate(rows, axis=0), pick, 1, 0).astype(bf16)
+    block = jnp.concatenate(
+        [spread[:32, :128], spread[:32, 128:], spread[32:, :128], spread[32:, 128:]], axis=0
+    )
     for i in range(out.shape[0]):
         out[i] = block
 
 
-def own_block(own, above, below):
-    return call(
-        block_kernel, "own_block", array((lax.axis_size("rows"), 64, 128), bf16), [VMEM] * 3, 4
-    )(own, above, below)
+def own_block(own, before):
+    return call(
+        block_kernel, "own_block", array((lax.axis_size("rows"), 128, 128), bf16), [VMEM] * 2, 4
+    )(own, before)
 
 
 def select_kernel(packing, blocks, keep, send):
     t, r = lax.axis_index("tm"), lax.axis_index("rows")
+    last = blocks.shape[0] - 1
     core = t % 2
+    upper = (iota((64, 128), 0) // 16) % 2 == 0
     for out, half in ((keep, core), (send, 1 - core)):
         for i in range(4):
             ident = packing[r * 8 + half * 4 + i]
-            here = jnp.where(ident // 16 == t, 1.0, 0.0).astype(bf16)
-            out[i] = blocks[ident % 16] * here
+            place = ident % 16
+            here = jnp.where(ident // 16 == t, 1.0, 0.0)
+            first = jnp.where(place == 0, 0.0, here)
+            final = jnp.where(place == last, 0.0, here)
+            own = blocks[place, pl.ds(0, 64)].astype(f32)
+            above = blocks[jnp.maximum(place - 1, 0), pl.ds(64, 64)].astype(f32)
+            below = blocks[jnp.minimum(place + 1, last), pl.ds(64, 64)].astype(f32)
+            value = own * here + jnp.where(upper, above * first, below * final)
+            out[i] = value.astype(bf16)
 
 
 def selected(packing, blocks):
@@ -367,24 +427,23 @@
 ):
     channels = features.shape[-1]
     row = lambda v: v.reshape(1, -1)
-    partial = partial_latents(
-        *map(
-            in_hbm,
-            (
-                features.reshape(-1, channels),
-                block_gain,
-                conv_bias,
-                latent_weight.T,
-                latent_bias,
-                conv_weight.reshape(27, channels, channels),
-            ),
-        )
-    )
-    before = moved(partial[2:], "tm", 1)
-    own = partial[:2] + jnp.where(lax.axis_index("tm") == 0, 0.0, before)
-    above = moved(own[:, 3], "rows", 1)
-    below = moved(own[:, 0], "rows", -1)
-    copies = own_block(own, above, below)
+    features, block_gain, conv_bias, lwt, latent_bias, conv_weight = map(
+        in_hbm,
+        (
+            features.reshape(-1, channels),
+            block_gain,
+            conv_bias,
+            latent_weight.T,
+            latent_bias,
+            conv_weight.reshape(27, channels, channels),
+        ),
+    )
+    ahead, own, act = early_latents(
+        features, block_gain, conv_bias, lwt, latent_bias, conv_weight
+    )
+    before = moved(ahead, "tm", 1)
+    own = late_latents(own, act, lwt, conv_weight)
+    copies = own_block(own, before)
     copies, patch_weight = lax.optimization_barrier((copies, patch_weight))
     plane = lax.all_to_all(copies, "rows", 0, 0, tiled=True)
 
@@ -400,8 +459,8 @@
         row(query_gain),
         row(key_gain),
     )
+    grams = grams + swapped(grams, "tm", 1)
     plane, grams = lax.optimization_barrier((plane, grams))
-    grams = grams + swapped(grams, "tm", 1)
     grams = grams + swapped(grams, "tm", 2) + swapped(grams, "tm", 4) + swapped(grams, "tm", 6)
     left = quadratic_forms(patch_gram, grams)
 

time: 56.9 us -> 48.5 us (0.85)
  the two profiles are of different devices: /device:TPU:1 before, /device:TPU:0 now
where the time goes in v3:
time: 48.5 us; the launch traced here: 48.3 us
  Pallas kernels  20.7 us (43%)
  starting transfers between devices  16.7 us (34%)
  waiting for transfers between devices  9.92 us (20%)
  between operations  0.9 us (2%)
    ppermute x9, starting transfers between devices, swapped(): lax.ppermute(x, axis, [(i, i ^ bits) for i in range(lax.axis_size(axis))])  8.52 us
    all_to_all x1, starting transfers between devices, per_device(): plane = lax.all_to_all(copies, 'rows', 0, 0, tiled=True)  8.13 us
    pallas_call x1, Pallas kernels, weights_only(): call(weights_kernel, 'weights_only', [array((3 * EXT, part), bf16), array...  7.82 us
    ppermute x9, waiting for transfers between devices, swapped(): lax.ppermute(x, axis, [(i, i ^ bits) for i in range(lax.axis_size(axis))])  5.8 us
    pallas_call x1, Pallas kernels, early_latents(): call(early_kernel, 'early_latents', [array((2, 4, 16, 128), f32), array((...  4.4 us
    pallas_call x2, Pallas kernels, tokens(): call(functools.partial(token_kernel, before is not None), 'tokens_other'...  3.74 us
    pallas_call x1, Pallas kernels, late_latents(): call(late_kernel, 'late_latents', array((2, 4, 16, 128), f32), [VMEM] * 2...  2.74 us
    all_to_all x1, waiting for transfers between devices, per_device(): plane = lax.all_to_all(copies, 'rows', 0, 0, tiled=True)  2.16 us
  transfers between devices with their start and end apart: 11, of which 7 were waited for; matrix products, arithmetic and copies ran while one was open for 0% of the time, Pallas kernels for 26%

profile of v3, /device:TPU:0, one launch (start us, length us, event | category | flops | bytes accessed | tf_op | source)
XLA Modules:
  0.0 48.3 jit_solution(2777093302795922277)
XLA Ops:
  0.6 4.4 %early_latents.1 = (f32[2,4,16,128]{3,2,1,0:T(8,128)S(1)}, f32[2,4,16,128]{3,2,1,0:T(8,128)S(1)}, bf16[512,384]{1,0:T(8,128)(2,1)S(1)}) custom-call(bf16[512,384]{1,0:T(8,128)(2,1)} %bitcast.11, f32[384]{0:T(512)} %gain_hbm.1, f32[384]{0:T(512)} %bias_hbm.1, bf16[16,384]{1,0:T(8,128)(2,1)} %bitcast.12, f32[16]{0:T(128)} %lb_hbm.1, bf16[27,384,384]{2,1,0:T(8,128)(2,1)} %bitcast.9), custom_call_target="tpu_custom_call" | custom-call | tf_op jit(solution)/shard_map/early_latents/pallas_call | solution.py:145
  5.0 0.0 collective-permute-start
  5.1 0.0 copy-start.5
  5.1 0.0 copy-start.6
  5.1 0.0 copy-start.7
  5.1 2.7 %late_latents.1.own = f32[2,4,16,128]{3,2,1,0:T(8,128)S(1)} custom-call(f32[2,4,16,128]{3,2,1,0:T(8,128)S(1)} %get-tuple-element.17.own, bf16[512,384]{1,0:T(8,128)(2,1)S(1)} %get-tuple-element.18.act, bf16[16,384]{1,0:T(8,128)(2,1)} %bitcast.13, bf16[27,384,384]{2,1,0:T(8,128)(2,1)} %bitcast.10), custom_call_target="tpu_custom_call" | custom-call | flops 3000000000 | bytes 5000000 | tf_op jit(solution)/shard_map/late_latents/pallas_call | solution.py:178
  7.9 0.0 copy-start.3
  7.9 0.0 copy-start.4
  8.0 2.0 %collective-permute-done.before = f32[2,4,16,128]{3,2,1,0:T(8,128)S(1)} collective-permute-done((f32[2,4,16,128]{3,2,1,0:T(8,128)S(1)}, f32[2,4,16,128]{3,2,1,0:T(8,128)S(1)}, u32[]{:S(2)}, u32[]{:S(2)}) %collective-permute-start) | collective-permute-done | bytes 65568 | tf_op jit(solution)/shard_map/ppermute | solution.py:406
  10.0 1.0 %own_block.1 = bf16[16,128,128]{2,1,0:T(8,128)(2,1)} custom-call(f32[2,4,16,128]{3,2,1,0:T(8,128)S(1)} %late_latents.1.own, f32[2,4,16,128]{3,2,1,0:T(8,128)S(1)} %collective-permute-done.before), custom_call_target="tpu_custom_call" | custom-call | tf_op jit(solution)/shard_map/own_block/pallas_call | solution.py:292
  11.0 8.1 %all-to-all-start = ((bf16[16,128,128]{2,1,0:T(8,128)(2,1)}), bf16[16,128,128]{2,1,0:T(8,128)(2,1)S(1)}, u32[]{:S(2)}, u32[]{:S(2)}) async-start(bf16[16,128,128]{2,1,0:T(8,128)(2,1)} %own_block.1), calls=%async_computation | async-start | bytes 1048576 | tf_op jit(solution)/shard_map/all_to_all | solution.py:448
  19.1 0.0 copy-start
  19.2 7.8 %weights_only.1 = (bf16[240,640]{1,0:T(8,128)(2,1)S(1)}, bf16[240,640]{1,0:T(8,128)(2,1)S(1)}, f32[80,80]{1,0:T(8,128)S(1)}, f32[80,128]{1,0:T(8,128)S(1)}) custom-call(bf16[64,5120]{1,0:T(8,128)(2,1)S(1)} %copy-done.1, f32[1,5120]{1,0:T(1,128)S(1)} %bitcast.6, f32[1,5120]{1,0:T(1,128)S(1)} %bitcast.7, f32[1,5120]{1,0:T(1,128)S(1)} %bitcast.8, ...), custom_call_target="tpu_custom_call" | custom-call | flops 8388608000 | bytes 13107200 | tf_op jit(solution)/shard_map/weights_only/pallas_call | solution.py:251
  27.0 0.1 collective-permute-start.1
  27.1 1.2 %collective-permute-done.1 = f32[80,128]{1,0:T(8,128)S(1)} collective-permute-done((f32[80,128]{1,0:T(8,128)S(1)}, f32[80,128]{1,0:T(8,128)S(1)}, u32[]{:S(2)}, u32[]{:S(2)}) %collective-permute-start.1) | collective-permute-done | bytes 40992 | tf_op jit(solution)/shard_map/ppermute | solution.py:401
  28.3 2.2 %all-to-all-done.blocks = bf16[16,128,128]{2,1,0:T(8,128)(2,1)S(1)} async-done(((bf16[16,128,128]{2,1,0:T(8,128)(2,1)}), bf16[16,128,128]{2,1,0:T(8,128)(2,1)S(1)}, u32[]{:S(2)}, u32[]{:S(2)}) %all-to-all-start) | async-done | bytes 524320 | tf_op jit(solution)/shard_map/all_to_all | solution.py:448
  30.5 0.7 %select_blocks.1 = (bf16[4,64,128]{2,1,0:T(8,128)(2,1)S(1)}, bf16[4,64,128]{2,1,0:T(8,128)(2,1)S(1)}) custom-call(s32[128]{0:T(128)S(1)} %copy-done, bf16[16,128,128]{2,1,0:T(8,128)(2,1)S(1)} %all-to-all-done.blocks), custom_call_target="tpu_custom_call" | custom-call | tf_op jit(solution)/shard_map/select_blocks/pallas_call | solution.py:317
  31.1 0.1 collective-permute-start.2
  31.2 1.2 %collective-permute-done.2 = bf16[4,64,128]{2,1,0:T(8,128)(2,1)S(1)} collective-permute-done((bf16[4,64,128]{2,1,0:T(8,128)(2,1)S(1)}, bf16[4,64,128]{2,1,0:T(8,128)(2,1)S(1)}, u32[]{:S(2)}, u32[]{:S(2)}) %collective-permute-start.2) | collective-permute-done | bytes 65568 | tf_op jit(solution)/shard_map/ppermute | solution.py:401
  32.5 1.8 %collective-permute-start.5 = (bf16[4,64,128]{2,1,0:T(8,128)(2,1)S(1)}, bf16[4,64,128]{2,1,0:T(8,128)(2,1)S(1)}, u32[]{:S(2)}, u32[]{:S(2)}) collective-permute-start(bf16[4,64,128]{2,1,0:T(8,128)(2,1)S(1)} %add.25), channel_id=1, source_target_pairs={{0,96},{16,112},{32,64},{48,80},{64,32},{80,48},{96,0},{112,16},{1... | collective-permute-start | bytes 196616 | tf_op jit(solution)/shard_map/ppermute | solution.py:401
  34.3 1.8 %collective-permute-start.4 = (bf16[4,64,128]{2,1,0:T(8,128)(2,1)S(1)}, bf16[4,64,128]{2,1,0:T(8,128)(2,1)S(1)}, u32[]{:S(2)}, u32[]{:S(2)}) collective-permute-start(bf16[4,64,128]{2,1,0:T(8,128)(2,1)S(1)} %add.25), channel_id=1, source_target_pairs={{0,64},{16,80},{32,96},{48,112},{64,0},{80,16},{96,32},{112,48},{1... | collective-permute-start | bytes 196616 | tf_op jit(solution)/shard_map/ppermute | solution.py:401
  36.1 0.5 %collective-permute-start.3 = (bf16[4,64,128]{2,1,0:T(8,128)(2,1)S(1)}, bf16[4,64,128]{2,1,0:T(8,128)(2,1)S(1)}, u32[]{:S(2)}, u32[]{:S(2)}) collective-permute-start(bf16[4,64,128]{2,1,0:T(8,128)(2,1)S(1)} %add.25), channel_id=1, source_target_pairs={{0,32},{16,48},{32,0},{48,16},{64,96},{80,112},{96,64},{112,80},{1... | collective-permute-start | bytes 196616 | tf_op jit(solution)/shard_map/ppermute | solution.py:401
  36.6 1.7 %collective-permute-start.9 = (f32[80,128]{1,0:T(8,128)S(1)}, f32[80,128]{1,0:T(8,128)S(1)}, u32[]{:S(2)}, u32[]{:S(2)}) collective-permute-start(f32[80,128]{1,0:T(8,128)S(1)} %add.24), channel_id=1, source_target_pairs={{0,96},{16,112},{32,64},{48,80},{64,32},{80,48},{96,0},{112,16},{1... | collective-permute-start | bytes 122888 | tf_op jit(solution)/shard_map/ppermute | solution.py:401
  38.4 1.8 %collective-permute-start.8 = (f32[80,128]{1,0:T(8,128)S(1)}, f32[80,128]{1,0:T(8,128)S(1)}, u32[]{:S(2)}, u32[]{:S(2)}) collective-permute-start(f32[80,128]{1,0:T(8,128)S(1)} %add.24), channel_id=1, source_target_pairs={{0,64},{16,80},{32,96},{48,112},{64,0},{80,16},{96,32},{112,48},{1... | collective-permute-start | bytes 122888 | tf_op jit(solution)/shard_map/ppermute | solution.py:401
  40.2 0.5 %collective-permute-start.7 = (f32[80,128]{1,0:T(8,128)S(1)}, f32[80,128]{1,0:T(8,128)S(1)}, u32[]{:S(2)}, u32[]{:S(2)}) collective-permute-start(f32[80,128]{1,0:T(8,128)S(1)} %add.24), channel_id=1, source_target_pairs={{0,32},{16,48},{32,0},{48,16},{64,96},{80,112},{96,64},{112,80},{1... | collective-permute-start | bytes 122888 | tf_op jit(solution)/shard_map/ppermute | solution.py:401
  40.8 0.1 collective-permute-start.6
  40.9 1.4 %collective-permute-done.9 = f32[80,128]{1,0:T(8,128)S(1)} collective-permute-done((f32[80,128]{1,0:T(8,128)S(1)}, f32[80,128]{1,0:T(8,128)S(1)}, u32[]{:S(2)}, u32[]{:S(2)}) %collective-permute-start.9) | collective-permute-done | bytes 40992 | tf_op jit(solution)/shard_map/ppermute | solution.py:401
  42.3 1.6 %collective-permute-done.8 = f32[80,128]{1,0:T(8,128)S(1)} collective-permute-done((f32[80,128]{1,0:T(8,128)S(1)}, f32[80,128]{1,0:T(8,128)S(1)}, u32[]{:S(2)}, u32[]{:S(2)}) %collective-permute-start.8) | collective-permute-done | bytes 40992 | tf_op jit(solution)/shard_map/ppermute | solution.py:401
  43.9 0.3 collective-permute-done.7
  44.2 0.3 quadratic_forms.1.left
  44.5 1.9 %tokens_mine.1 = (bf16[1024,640]{1,0:T(8,128)(2,1)}, bf16[1024,640]{1,0:T(8,128)(2,1)}) custom-call(bf16[4,64,128]{2,1,0:T(8,128)(2,1)S(1)} %add_add_fusion.x_ref, bf16[240,160]{1,0:T(8,128)(2,1)S(1)} %quadratic_forms.1.left, bf16[240,640]{1,0:T(8,128)(2,1)S(1)} %get-tuple-element.28.rq, bf16[240,640]{1,0:T(8,128)(2,1)S(1)} %get-tuple-element.29.rk), custom_call_target="tpu_custom_call" | custom-call | tf_op jit(solution)/shard_map/tokens_mine/pallas_call | solution.py:380
  46.4 1.9 %tokens_other.1 = (bf16[1024,640]{1,0:T(8,128)(2,1)}, bf16[1024,640]{1,0:T(8,128)(2,1)}) custom-call(bf16[4,64,128]{2,1,0:T(8,128)(2,1)S(1)} %collective-permute-done.6.x_ref, bf16[240,160]{1,0:T(8,128)(2,1)S(1)} %quadratic_forms.1.left, bf16[240,640]{1,0:T(8,128)(2,1)S(1)} %get-tuple-element.28.rq, ...), custom_call_target="tpu_custom_call", output_to_operand_aliasing={{0}: (4, {}), {1}: (5, {})} | custom-call | tf_op jit(solution)/shard_map/tokens_other/pallas_call | solution.py:380
  (24 shorter events, 0.1 us)
Async XLA Ops:
  5.0 4.9 %collective-permute-start = (f32[2,4,16,128]{3,2,1,0:T(8,128)S(1)}, f32[2,4,16,128]{3,2,1,0:T(8,128)S(1)}, u32[]{:S(2)}, u32[]{:S(2)}) collective-permute-start(f32[2,4,16,128]{3,2,1,0:T(8,128)S(1)} %get-tuple-element.19), channel_id=1, source_target_pairs={{0,16},{16,32},{32,48},{48,64},{64,80},{80,96},{96,112},{112,0},{1... | collective-permute-start | bytes 196616 | tf_op jit(solution)/shard_map/ppermute | solution.py:406
  5.1 2.8 %copy-start.5 = (f32[640]{0:T(1024)S(1)}, f32[640]{0:T(1024)}, u32[]{:S(2)}) copy-start(f32[640]{0:T(1024)} %param.28) | copy-start | bytes 7684
  5.1 2.9 %copy-start.6 = (f32[640]{0:T(1024)S(1)}, f32[640]{0:T(1024)}, u32[]{:S(2)}) copy-start(f32[640]{0:T(1024)} %param.29) | copy-start | bytes 7684
  5.1 2.9 %copy-start.7 = (f32[640]{0:T(1024)S(1)}, f32[640]{0:T(1024)}, u32[]{:S(2)}) copy-start(f32[640]{0:T(1024)} %param.31) | copy-start | bytes 7684
  5.1 2.9 %copy-start.8 = (f32[640]{0:T(1024)S(1)}, f32[640]{0:T(1024)}, u32[]{:S(2)}) copy-start(f32[640]{0:T(1024)} %param.32) | copy-start | bytes 7684
  7.9 11.2 %copy-start.1 = (bf16[64,5120]{1,0:T(8,128)(2,1)S(1)}, bf16[64,5120]{1,0:T(8,128)(2,1)}, u32[]{:S(2)}) copy-start(bf16[64,5120]{1,0:T(8,128)(2,1)} %pw) | copy-start | bytes 1966084
  7.9 11.2 %copy-start.2 = (f32[5120]{0:T(1024)S(1)}, f32[5120]{0:T(1024)}, u32[]{:S(2)}) copy-start(f32[5120]{0:T(1024)} %param.24) | copy-start | bytes 61444
  7.9 11.2 %copy-start.3 = (f32[5120]{0:T(1024)S(1)}, f32[5120]{0:T(1024)}, u32[]{:S(2)}) copy-start(f32[5120]{0:T(1024)} %param.25) | copy-start | bytes 61444
  7.9 11.2 %copy-start.4 = (f32[5120]{0:T(1024)S(1)}, f32[5120]{0:T(1024)}, u32[]{:S(2)}) copy-start(f32[5120]{0:T(1024)} %param.26) | copy-start | bytes 61444
  11.0 19.5 %all-to-all-start = ((bf16[16,128,128]{2,1,0:T(8,128)(2,1)}), bf16[16,128,128]{2,1,0:T(8,128)(2,1)S(1)}, u32[]{:S(2)}, u32[]{:S(2)}) async-start(bf16[16,128,128]{2,1,0:T(8,128)(2,1)} %own_block.1), calls=%async_computation | async-start | bytes 1048576 | tf_op jit(solution)/shard_map/all_to_all | solution.py:448
  19.1 11.3 %copy-start = (s32[128]{0:T(128)S(1)}, s32[128]{0:T(128)}, u32[]{:S(2)}) copy-start(s32[128]{0:T(128)} %packing.1) | copy-start | bytes 1540
  27.0 1.3 %collective-permute-start.1 = (f32[80,128]{1,0:T(8,128)S(1)}, f32[80,128]{1,0:T(8,128)S(1)}, u32[]{:S(2)}, u32[]{:S(2)}) collective-permute-start(f32[80,128]{1,0:T(8,128)S(1)} %get-tuple-element.22), channel_id=1, source_target_pairs={{0,16},{16,0},{32,48},{48,32},{64,80},{80,64},{96,112},{112,96},{1... | collective-permute-start | bytes 122888 | tf_op jit(solution)/shard_map/ppermute | solution.py:401
  31.1 1.3 %collective-permute-start.2 = (bf16[4,64,128]{2,1,0:T(8,128)(2,1)S(1)}, bf16[4,64,128]{2,1,0:T(8,128)(2,1)S(1)}, u32[]{:S(2)}, u32[]{:S(2)}) collective-permute-start(bf16[4,64,128]{2,1,0:T(8,128)(2,1)S(1)} %get-tuple-element.25), channel_id=1, source_target_pairs={{0,16},{16,0},{32,48},{48,32},{64,80},{80,64},{96,112},{112,96},{1... | collective-permute-start | bytes 196616 | tf_op jit(solution)/shard_map/ppermute | solution.py:401
  32.5 7.7 %collective-permute-start.5 = (bf16[4,64,128]{2,1,0:T(8,128)(2,1)S(1)}, bf16[4,64,128]{2,1,0:T(8,128)(2,1)S(1)}, u32[]{:S(2)}, u32[]{:S(2)}) collective-permute-start(bf16[4,64,128]{2,1,0:T(8,128)(2,1)S(1)} %add.25), channel_id=1, source_target_pairs={{0,96},{16,112},{32,64},{48,80},{64,32},{80,48},{96,0},{112,16},{1... | collective-permute-start | bytes 196616 | tf_op jit(solution)/shard_map/ppermute | solution.py:401
  34.3 6.5 %collective-permute-start.4 = (bf16[4,64,128]{2,1,0:T(8,128)(2,1)S(1)}, bf16[4,64,128]{2,1,0:T(8,128)(2,1)S(1)}, u32[]{:S(2)}, u32[]{:S(2)}) collective-permute-start(bf16[4,64,128]{2,1,0:T(8,128)(2,1)S(1)} %add.25), channel_id=1, source_target_pairs={{0,64},{16,80},{32,96},{48,112},{64,0},{80,16},{96,32},{112,48},{1... | collective-permute-start | bytes 196616 | tf_op jit(solution)/shard_map/ppermute | solution.py:401
  36.1 4.6 %collective-permute-start.3 = (bf16[4,64,128]{2,1,0:T(8,128)(2,1)S(1)}, bf16[4,64,128]{2,1,0:T(8,128)(2,1)S(1)}, u32[]{:S(2)}, u32[]{:S(2)}) collective-permute-start(bf16[4,64,128]{2,1,0:T(8,128)(2,1)S(1)} %add.25), channel_id=1, source_target_pairs={{0,32},{16,48},{32,0},{48,16},{64,96},{80,112},{96,64},{112,80},{1... | collective-permute-start | bytes 196616 | tf_op jit(solution)/shard_map/ppermute | solution.py:401
  36.6 5.7 %collective-permute-start.9 = (f32[80,128]{1,0:T(8,128)S(1)}, f32[80,128]{1,0:T(8,128)S(1)}, u32[]{:S(2)}, u32[]{:S(2)}) collective-permute-start(f32[80,128]{1,0:T(8,128)S(1)} %add.24), channel_id=1, source_target_pairs={{0,96},{16,112},{32,64},{48,80},{64,32},{80,48},{96,0},{112,16},{1... | collective-permute-start | bytes 122888 | tf_op jit(solution)/shard_map/ppermute | solution.py:401
  38.4 5.5 %collective-permute-start.8 = (f32[80,128]{1,0:T(8,128)S(1)}, f32[80,128]{1,0:T(8,128)S(1)}, u32[]{:S(2)}, u32[]{:S(2)}) collective-permute-start(f32[80,128]{1,0:T(8,128)S(1)} %add.24), channel_id=1, source_target_pairs={{0,64},{16,80},{32,96},{48,112},{64,0},{80,16},{96,32},{112,48},{1... | collective-permute-start | bytes 122888 | tf_op jit(solution)/shard_map/ppermute | solution.py:401
  40.2 4.0 %collective-permute-start.7 = (f32[80,128]{1,0:T(8,128)S(1)}, f32[80,128]{1,0:T(8,128)S(1)}, u32[]{:S(2)}, u32[]{:S(2)}) collective-permute-start(f32[80,128]{1,0:T(8,128)S(1)} %add.24), channel_id=1, source_target_pairs={{0,32},{16,48},{32,0},{48,16},{64,96},{80,112},{96,64},{112,80},{1... | collective-permute-start | bytes 122888 | tf_op jit(solution)/shard_map/ppermute | solution.py:401
  40.8 5.6 %collective-permute-start.6 = (bf16[4,64,128]{2,1,0:T(8,128)(2,1)S(1)}, bf16[4,64,128]{2,1,0:T(8,128)(2,1)S(1)}, u32[]{:S(2)}, u32[]{:S(2)}) collective-permute-start(bf16[4,64,128]{2,1,0:T(8,128)(2,1)S(1)} %add_add_fusion.x_ref), channel_id=1, source_target_pairs={{0,16},{16,0},{32,48},{48,32},{64,80},{80,64},{96,112},{112,96},{1... | collective-permute-start | bytes 196616 | tf_op jit(solution)/shard_map/ppermute | solution.py:401

commit v4 on v3

--- a/solution.py
+++ b/solution.py
@@ -48,15 +48,12 @@
     return jax.ShapeDtypeStruct(shape, kind)
 
 
-def folded(lwt, cw, wt, gt, act, copies, at, taps):
-    chunk = taps // len(copies)
-    for i, c in enumerate(copies):
-        c.wait()
-        for k in range(i * chunk, (i + 1) * chunk):
-            high, low = halves(mm(lwt, cw[at + k], 1, 1))
-            wt[pl.ds(k * 16, 16), :] = high
-            wt[pl.ds(144 + k * 16, 16), :] = low
-    gt[...] = mm(wt[...], act, 1, 1)
+def folded(lwt, cw, wt, first, count, a):
+    for k in range(first, first + count):
+        high, low = halves(mm(lwt, cw[k], 1, 1))
+        at = a * 288 + (k % 9) * 16
+        wt[pl.ds(at, 16), :] = high
+        wt[pl.ds(at + 144, 16), :] = low
 
 
 def shifted_sum(by_e):
@@ -85,22 +82,26 @@
     return shifted_sum(by_e)
 
 
-def chunked(source, target, sems, start, count, size, first_sem):
-    found = []
-    for i in range(count):
-        c = pltpu.make_async_copy(
+def chunks_of(source, target, sems, start, count, size, first_sem):
+    return [
+        pltpu.make_async_copy(
             source.at[pl.ds(start + i * size, size)],
             target.at[pl.ds(i * size, size)],
             sems.at[first_sem + i],
         )
-        c.start()
-        found.append(c)
-    return found
+        for i in range(count)
+    ]
+
+
+def silu_normed(values, gain):
+    mean = jnp.mean(values * values, axis=-1, keepdims=True)
+    y = values * lax.rsqrt(mean + epsilon) * gain
+    return (y / (1.0 + jnp.exp(-y))).astype(bf16)
 
 
 def early_kernel(
     feat_hbm, gain_hbm, bias_hbm, lwt_hbm, lb_hbm, cw_hbm, ahead, own, act_out,
-    feat, gain, bias, lwt_ref, lb, cw, wt, gt0, gt1, sems,
+    feat, gain, bias, lwt_ref, lb, cw, wt, gt, sems,
 ):
     small = [
         pltpu.make_async_copy(a, b, sems.at[6 + i])
@@ -116,20 +117,27 @@
     ]
     for c in small:
         c.start()
-    copies = chunked(cw_hbm, cw, sems, 0, 6, 3, 0)
+    copies = chunks_of(cw_hbm, cw, sems, 0, 6, 3, 0)
+    for c in copies[:3]:
+        c.start()
     for c in small:
         c.wait()
-    values = feat[...].astype(f32)
-    mean = jnp.mean(values * values, axis=-1, keepdims=True)
-    y = values * lax.rsqrt(mean + epsilon) * gain[...].reshape(1, -1)
-    act = (y / (1.0 + jnp.exp(-y))).astype(bf16)
-    act_out[...] = act
     lwt = lwt_ref[...]
+    for i, c in enumerate(copies):
+        if i < 4:
+            at = pl.ds(i * 128, 128)
+            act_out[at, :] = silu_normed(feat[at, :].astype(f32), gain[...].reshape(1, -1))
+        c.wait()
+        if i + 3 < len(copies):
+            copies[i + 3].start()
+        folded(lwt, cw, wt, i * 3, 3, i // 3)
+        if i == 3:
+            gt[pl.ds(0, 288), :] = mm(wt[pl.ds(0, 288), :], act_out[...], 1, 1)
     direct = mm(lwt, feat[...], 1, 1)
     const = jnp.sum(lwt.astype(f32) * bias[...].reshape(1, -1), axis=1, keepdims=True)
     const = const + jnp.transpose(lb[...].reshape(1, -1))
-    folded(lwt, cw, wt, gt0, act, copies[:3], 0, 9)
-    folded(lwt, cw, wt, gt1, act, copies[3:], 9, 9)
+    gt[pl.ds(288, 288), :] = mm(wt[pl.ds(288, 288), :], act_out[...], 1, 1)
+    gt0, gt1 = gt.at[pl.ds(0, 288)], gt.at[pl.ds(288, 288)]
     for ro in range(4):
         for fo in (2, 3):
             ahead[fo - 2, ro] = contributions({0: gt0, 1: gt1}, fo, ro)
@@ -155,9 +163,8 @@
             pltpu.VMEM((16, 384), bf16),
             pltpu.VMEM((16,), f32),
             pltpu.VMEM((18, 384, 384), bf16),
-            pltpu.VMEM((288, 384), bf16),
-            pltpu.VMEM((288, 512), f32),
-            pltpu.VMEM((288, 512), f32),
+            pltpu.VMEM((576, 384), bf16),
+            pltpu.VMEM((576, 512), f32),
             pltpu.SemaphoreType.DMA((11,)),
         ],
     )(*args)
@@ -166,9 +173,14 @@
 def late_kernel(own, act, lwt_hbm, cw_hbm, out, lwt, cw, wt, gt, sems):
     small = pltpu.make_async_copy(lwt_hbm, lwt, sems.at[3])
     small.start()
-    copies = chunked(cw_hbm, cw, sems, 18, 3, 3, 0)
+    copies = chunks_of(cw_hbm, cw, sems, 18, 3, 3, 0)
+    for c in copies:
+        c.start()
     small.wait()
-    folded(lwt[...], cw, wt, gt, act[...], copies, 0, 9)
+    for i, c in enumerate(copies):
+        c.wait()
+        folded(lwt[...], cw, wt, i * 3, 3, 0)
+    gt[...] = mm(wt[...], act[...], 1, 1)
     for fo in range(2):
         for ro in range(4):
             out[fo, ro] = own[fo, ro] + contributions({2: gt}, fo, ro)
@@ -198,14 +210,10 @@
 ):
     width = pw.shape[1]
     chunk = width // 4
-    copies = []
-    for n, (a, b) in enumerate(((wq_hbm, wq), (wk_hbm, wk))):
-        copies.append([])
-        for i in range(4):
-            at = pl.ds(i * chunk, chunk)
-            c = pltpu.make_async_copy(a.at[at], b.at[at], sems.at[n * 4 + i])
-            c.start()
-            copies[n].append(c)
+    copies = chunks_of(wq_hbm, wq, sems, 0, 4, chunk, 0)
+    copies = copies + chunks_of(wk_hbm, wk, sems, 0, 4, chunk, 4)
+    for c in copies[:3]:
+        c.start()
     to, at = iota((64, 64), 0), iota((64, 64), 1)
     wanted = 4 * (to % 16) + 2 * ((to // 16) % 2) + to // 32
     order = jnp.where(at == wanted, 1.0, 0.0).astype(bf16)
@@ -225,8 +233,10 @@
     found = []
     for n, (w, bias, gain, right) in enumerate(((wq, bq, gq, rq), (wk, bk, gk, rk))):
         both = None
-        for i, c in enumerate(copies[n]):
-            c.wait()
+        for i in range(4):
+            copies[n * 4 + i].wait()
+            if n * 4 + i + 3 < 8:
+                copies[n * 4 + i + 3].start()
             at = pl.ds(i * chunk, chunk)
             part = mm(parts[:, at], w[at, :], 1, 0)
             both = part if both is None else both + part
@@ -294,7 +304,7 @@
     )(own, before)
 
 
-def select_kernel(packing, blocks, keep, send):
+def select_kernel(packing, blocks, grams, keep, send):
     t, r = lax.axis_index("tm"), lax.axis_index("rows")
     last = blocks.shape[0] - 1
     core = t % 2
@@ -310,18 +320,49 @@
             above = blocks[jnp.maximum(place - 1, 0), pl.ds(64, 64)].astype(f32)
             below = blocks[jnp.minimum(place + 1, last), pl.ds(64, 64)].astype(f32)
             value = own * here + jnp.where(upper, above * first, below * final)
-            out[i] = value.astype(bf16)
-
-
-def selected(packing, blocks):
-    return call(
-        select_kernel, "select_blocks", [array((4, 64, 128), bf16)] * 2, [SMEM, VMEM], 4
-    )(packing, blocks)
-
-
-def forms_kernel(patch_gram, grams, left):
+            out[pl.ds(i * 64, 64), :] = value.astype(bf16)
+    send[pl.ds(256, EXT), :], send[pl.ds(256 + EXT, EXT), :] = halves(grams[...])
+
+
+def selected(packing, blocks, grams):
+    return call(
+        select_kernel,
+        "select_blocks",
+        [array((256, 128), bf16), array((256 + 2 * EXT, 128), bf16)],
+        [SMEM, VMEM, VMEM],
+        4,
+    )(packing, blocks, grams)
+
+
+def sent_grams(sent):
+    return sent[pl.ds(256, EXT), :].astype(f32) + sent[pl.ds(256 + EXT, EXT), :].astype(f32)
+
+
+def pair_kernel(keep, grams, sent, pair, pair_grams):
+    pair[pl.ds(0, 256), :] = keep[...] + sent[pl.ds(0, 256), :]
+    total = grams[...] + sent_grams(sent)
+    pair_grams[...] = total
+    pair[pl.ds(256, EXT), :], pair[pl.ds(256 + EXT, EXT), :] = halves(total)
+
+
+def paired(keep, grams, sent):
+    return call(
+        pair_kernel,
+        "pair_sums",
+        [array(sent.shape, bf16), array(grams.shape, f32)],
+        [VMEM] * 3,
+        4,
+    )(keep, grams, sent)
+
+
+def forms_kernel(patch_gram, pair, pair_grams, s1, s2, s3, mine, left):
+    blocks, total = pair[pl.ds(0, 256), :], pair_grams[...]
+    for sent in (s1, s2, s3):
+        blocks = blocks + sent[pl.ds(0, 256), :]
+        total = total + sent_grams(sent)
+    mine[...] = blocks
     i, j = iota((EXT, EXT), 0), iota((EXT, EXT), 1)
-    total = grams[...] * (1.0 / 5120.0)
+    total = total * (1.0 / 5120.0)
     square = total[:, :EXT]
     gq = jnp.where(i > j, 2.0 * square, 0.0) + jnp.where(i == j, square, 0.0)
     gk = jnp.where(i > j, 2.0 * jnp.transpose(square), 0.0)
@@ -333,64 +374,89 @@
         left[pl.ds((n + 1) * EXT, EXT), :] = jnp.concatenate(halves(g), axis=1)
 
 
-def quadratic_forms(patch_gram, grams):
-    return call(
-        forms_kernel, "quadratic_forms", array((3 * EXT, 2 * EXT), bf16), [VMEM] * 2, 4
-    )(patch_gram, grams)
-
-
-def token_kernel(other_half, x_ref, left, rq, rk, *refs):
-    q_out, k_out, q_buf, k_buf, sems = refs[-5:]
+def quadratic_forms(*args):
+    return call(
+        forms_kernel,
+        "quadratic_forms",
+        [array((256, 128), bf16), array((3 * EXT, 2 * EXT), bf16)],
+        [VMEM] * 6,
+        4,
+    )(*args)
+
+
+def token_rows(x_ref, part, left, rights):
+    at = part * 128
+    x = jnp.concatenate([x_ref[pl.ds(at, 64), :], x_ref[pl.ds(at + 64, 64), :]], axis=1)
+    tail = iota((EXT - 64, 256), 0)
+    xf = jnp.concatenate([x.astype(f32), jnp.where(tail == 0, 1.0, 0.0)], axis=0)
+    xe = xf.astype(bf16)
+    t = mm(left[...], jnp.concatenate([xe, xe], axis=0), 1, 0)
+    spread = jnp.sum(t[:EXT] * xf, axis=0, keepdims=True)
+    scale = lax.rsqrt(spread + epsilon)
+    found = []
+    for n, right in enumerate(rights):
+        tn = t[(n + 1) * EXT : (n + 2) * EXT]
+        squares = (
+            scale * scale * jnp.sum(tn * xf, axis=0, keepdims=True)
+            + scale * tn[65:66]
+            + tn[66:67]
+        )
+        beta = lax.rsqrt(squares + epsilon)
+        alpha = scale * beta
+        y = xf * alpha + jnp.where(iota((EXT, 256), 0) == 65, beta, 0.0)
+        high, low = halves(y)
+        lhs = jnp.concatenate([high, low, high], axis=0)
+        found.append(mm(lhs, right[...], 0, 0).astype(bf16))
+    return found
+
+
+def first_kernel(x_ref, left, rq, rk, q_out, k_out):
+    for part in range(2):
+        at = pl.ds(part * 256, 256)
+        q_out[at, :], k_out[at, :] = token_rows(x_ref, part, left, (rq, rk))
+
+
+def first_tokens(x, left, rq, rk):
+    return call(
+        first_kernel, "first_tokens", [array((512, rq.shape[1]), bf16)] * 2, [VMEM] * 4, 6
+    )(x, left, rq, rk)
+
+
+def rest_kernel(x_ref, left, rq, rk, q_first, k_first, q_out, k_out, q_buf, k_buf, sems):
     core = lax.axis_index("tm") % 2
-    place = (1 - core if other_half else core) * 512
     copies = []
+
+    def send(source, target, at, size):
+        at = pl.ds(pl.multiple_of(at, 256), size)
+        c = pltpu.make_async_copy(source, target.at[at], sems.at[len(copies)])
+        c.start()
+        copies.append(c)
+
+    send(q_first, q_out, core * 512, 512)
+    send(k_first, k_out, core * 512, 512)
     for part in range(2):
-        x = jnp.concatenate([x_ref[2 * part], x_ref[2 * part + 1]], axis=1)
-        tail = iota((EXT - 64, 256), 0)
-        xf = jnp.concatenate([x.astype(f32), jnp.where(tail == 0, 1.0, 0.0)], axis=0)
-        xe = xf.astype(bf16)
-        t = mm(left[...], jnp.concatenate([xe, xe], axis=0), 1, 0)
-        spread = jnp.sum(t[:EXT] * xf, axis=0, keepdims=True)
-        scale = lax.rsqrt(spread + epsilon)
-        for n, (right, buf, out) in enumerate(((rq, q_buf, q_out), (rk, k_buf, k_out))):
-            tn = t[(n + 1) * EXT : (n + 2) * EXT]
-            squares = (
-                scale * scale * jnp.sum(tn * xf, axis=0, keepdims=True)
-                + scale * tn[65:66]
-                + tn[66:67]
-            )
-            beta = lax.rsqrt(squares + epsilon)
-            alpha = scale * beta
-            y = xf * alpha + jnp.where(iota((EXT, 256), 0) == 65, beta, 0.0)
-            high, low = halves(y)
-            lhs = jnp.concatenate([high, low, high], axis=0)
-            buf[part] = mm(lhs, right[...], 0, 0).astype(bf16)
-            c = pltpu.make_async_copy(
-                buf.at[part], out.at[pl.ds(pl.multiple_of(place + part * 256, 256), 256)], sems.at[part * 2 + n]
-            )
-            c.start()
-            copies.append(c)
+        q_buf[part], k_buf[part] = token_rows(x_ref, part, left, (rq, rk))
+        send(q_buf.at[part], q_out, (1 - core) * 512 + part * 256, 256)
+        send(k_buf.at[part], k_out, (1 - core) * 512 + part * 256, 256)
     for c in copies:
         c.wait()
 
 
-def tokens(x, left, rq, rk, before=None):
+def all_tokens(x, left, rq, rk, q_first, k_first):
     width = rq.shape[1]
-    given = () if before is None else tuple(before)
-    return call(
-        functools.partial(token_kernel, before is not None),
-        "tokens_other" if given else "tokens_mine",
+    return call(
+        rest_kernel,
+        "rest_tokens",
         [array((1024, width), bf16)] * 2,
-        [VMEM] * 4 + [HBM] * len(given),
-        12,
+        [VMEM] * 6,
+        8,
         scratch=[
             pltpu.VMEM((2, 256, width), bf16),
             pltpu.VMEM((2, 256, width), bf16),
-            pltpu.SemaphoreType.DMA((4,)),
+            pltpu.SemaphoreType.DMA((6,)),
         ],
         out_specs=[HBM, HBM],
-        input_output_aliases={4: 0, 5: 1} if given else {},
-    )(x, left, rq, rk, *given)
+    )(x, left, rq, rk, q_first, k_first)
 
 
 def in_hbm(x):
@@ -459,16 +525,13 @@
         row(query_gain),
         row(key_gain),
     )
-    grams = grams + swapped(grams, "tm", 1)
     plane, grams = lax.optimization_barrier((plane, grams))
-    grams = grams + swapped(grams, "tm", 2) + swapped(grams, "tm", 4) + swapped(grams, "tm", 6)
-    left = quadratic_forms(patch_gram, grams)
-
-    keep, send = selected(packing, plane)
-    mine = keep + swapped(send, "tm", 1)
-    mine = mine + swapped(mine, "tm", 2) + swapped(mine, "tm", 4) + swapped(mine, "tm", 6)
+    keep, send = selected(packing, plane, grams)
+    pair, pair_grams = paired(keep, grams, swapped(send, "tm", 1))
+    sent = [swapped(pair, "tm", bits) for bits in (2, 4, 6)]
+    mine, left = quadratic_forms(patch_gram, pair, pair_grams, *sent)
     other = swapped(mine, "tm", 1)
-    return tokens(other, left, rq, rk, tokens(mine, left, rq, rk))
+    return all_tokens(other, left, rq, rk, *first_tokens(mine, left, rq, rk))
 
 
 def solution(mesh):

time: 48.5 us -> 47.3 us (0.975)
  the two profiles are of different devices: /device:TPU:0 before, /device:TPU:1 now
where the time goes in v4:
time: 47.3 us; the launch traced here: 47 us
  Pallas kernels  20.6 us (44%)
  starting transfers between devices  17.5 us (37%)
  waiting for transfers between devices  8.07 us (17%)
  between operations  0.87 us (2%)
    pallas_call x1, Pallas kernels, weights_only(): call(weights_kernel, 'weights_only', [array((3 * EXT, part), bf16), array...  7.96 us
    all_to_all x1, starting transfers between devices, per_device(): plane = lax.all_to_all(copies, 'rows', 0, 0, tiled=True)  7.77 us
    ppermute x5, starting transfers between devices, swapped(): lax.ppermute(x, axis, [(i, i ^ bits) for i in range(lax.axis_size(axis))])  7.08 us
    ppermute x5, waiting for transfers between devices, swapped(): lax.ppermute(x, axis, [(i, i ^ bits) for i in range(lax.axis_size(axis))])  5.75 us
    pallas_call x1, Pallas kernels, early_latents(): call(early_kernel, 'early_latents', [array((2, 4, 16, 128), f32), array((...  4.53 us
    pallas_call x1, Pallas kernels, late_latents(): call(late_kernel, 'late_latents', array((2, 4, 16, 128), f32), [VMEM] * 2...  2.72 us
    ppermute x1, starting transfers between devices, moved(): return lax.ppermute(x, axis, [(i, (i + by) % size) for i in range(size)])  2.61 us
    all_to_all x1, waiting for transfers between devices, per_device(): plane = lax.all_to_all(copies, 'rows', 0, 0, tiled=True)  2.32 us
  transfers between devices with their start and end apart: 7, of which 5 were waited for; matrix products, arithmetic and copies ran while one was open for 0% of the time, Pallas kernels for 25%

profile of v4, /device:TPU:1, one launch (start us, length us, event | category | flops | bytes accessed | tf_op | source)
XLA Modules:
  0.0 47.0 jit_solution(1984007517143254814)
XLA Ops:
  0.6 4.5 %early_latents.1 = (f32[2,4,16,128]{3,2,1,0:T(8,128)S(1)}, f32[2,4,16,128]{3,2,1,0:T(8,128)S(1)}, bf16[512,384]{1,0:T(8,128)(2,1)S(1)}) custom-call(bf16[512,384]{1,0:T(8,128)(2,1)} %bitcast.11, f32[384]{0:T(512)} %gain_hbm.1, f32[384]{0:T(512)} %bias_hbm.1, bf16[16,384]{1,0:T(8,128)(2,1)} %bitcast.12, f32[16]{0:T(128)} %lb_hbm.1, bf16[27,384,384]{2,1,0:T(8,128)(2,1)} %bitcast.9), custom_call_target="tpu_custom_call" | custom-call | tf_op jit(solution)/shard_map/early_latents/pallas_call | solution.py:153
  5.2 0.0 copy-start.5
  5.2 0.0 copy-start.6
  5.2 0.0 copy-start.7
  5.2 0.0 copy-start.8
  5.2 0.0 copy-start.1
  5.2 0.0 copy-start.2
  5.2 0.0 copy-start.3
  5.2 0.0 copy-start.4
  5.3 2.6 %collective-permute-start = (f32[2,4,16,128]{3,2,1,0:T(8,128)S(1)}, f32[2,4,16,128]{3,2,1,0:T(8,128)S(1)}, u32[]{:S(2)}, u32[]{:S(2)}) collective-permute-start(f32[2,4,16,128]{3,2,1,0:T(8,128)S(1)} %get-tuple-element.23), channel_id=1, source_target_pairs={{0,16},{16,32},{32,48},{48,64},{64,80},{80,96},{96,112},{112,0},{1... | collective-permute-start | bytes 196616 | tf_op jit(solution)/shard_map/ppermute | solution.py:472
  7.9 2.7 %late_latents.1.own = f32[2,4,16,128]{3,2,1,0:T(8,128)S(1)} custom-call(f32[2,4,16,128]{3,2,1,0:T(8,128)S(1)} %get-tuple-element.21.own, bf16[512,384]{1,0:T(8,128)(2,1)S(1)} %get-tuple-element.22.act, bf16[16,384]{1,0:T(8,128)(2,1)} %bitcast.13, bf16[27,384,384]{2,1,0:T(8,128)(2,1)} %bitcast.10), custom_call_target="tpu_custom_call" | custom-call | flops 3000000000 | bytes 5000000 | tf_op jit(solution)/shard_map/late_latents/pallas_call | solution.py:190
  10.6 0.0 copy-done.5
  10.7 0.0 collective-permute-done.before
  10.7 1.0 %own_block.1 = bf16[16,128,128]{2,1,0:T(8,128)(2,1)} custom-call(f32[2,4,16,128]{3,2,1,0:T(8,128)S(1)} %late_latents.1.own, f32[2,4,16,128]{3,2,1,0:T(8,128)S(1)} %collective-permute-done.before), custom_call_target="tpu_custom_call" | custom-call | tf_op jit(solution)/shard_map/own_block/pallas_call | solution.py:302
  11.7 7.8 %all-to-all-start = ((bf16[16,128,128]{2,1,0:T(8,128)(2,1)}), bf16[16,128,128]{2,1,0:T(8,128)(2,1)S(1)}, u32[]{:S(2)}, u32[]{:S(2)}) async-start(bf16[16,128,128]{2,1,0:T(8,128)(2,1)} %own_block.1), calls=%async_computation | async-start | bytes 1048576 | tf_op jit(solution)/shard_map/all_to_all | solution.py:514
  19.5 0.0 copy-start
  19.5 8.0 %weights_only.1 = (bf16[240,640]{1,0:T(8,128)(2,1)S(1)}, bf16[240,640]{1,0:T(8,128)(2,1)S(1)}, f32[80,80]{1,0:T(8,128)S(1)}, f32[80,128]{1,0:T(8,128)S(1)}) custom-call(bf16[64,5120]{1,0:T(8,128)(2,1)S(1)} %copy-done.1, f32[1,5120]{1,0:T(1,128)S(1)} %bitcast.6, f32[1,5120]{1,0:T(1,128)S(1)} %bitcast.7, f32[1,5120]{1,0:T(1,128)S(1)} %bitcast.8, ...), custom_call_target="tpu_custom_call" | custom-call | flops 8388608000 | bytes 13107200 | tf_op jit(solution)/shard_map/weights_only/pallas_call | solution.py:261
  27.5 2.3 %all-to-all-done.blocks = bf16[16,128,128]{2,1,0:T(8,128)(2,1)S(1)} async-done(((bf16[16,128,128]{2,1,0:T(8,128)(2,1)}), bf16[16,128,128]{2,1,0:T(8,128)(2,1)S(1)}, u32[]{:S(2)}, u32[]{:S(2)}) %all-to-all-start) | async-done | bytes 524320 | tf_op jit(solution)/shard_map/all_to_all | solution.py:514
  29.8 0.7 %select_blocks.1 = (bf16[256,128]{1,0:T(8,128)(2,1)S(1)}, bf16[416,128]{1,0:T(8,128)(2,1)S(1)}) custom-call(s32[128]{0:T(128)S(1)} %copy-done, bf16[16,128,128]{2,1,0:T(8,128)(2,1)S(1)} %all-to-all-done.blocks, f32[80,128]{1,0:T(8,128)S(1)} %get-tuple-element.29.grams), custom_call_target="tpu_custom_call" | custom-call | tf_op jit(solution)/shard_map/select_blocks/pallas_call | solution.py:328
  30.5 2.2 %collective-permute-start.1 = (bf16[416,128]{1,0:T(8,128)(2,1)S(1)}, bf16[416,128]{1,0:T(8,128)(2,1)S(1)}, u32[]{:S(2)}, u32[]{:S(2)}) collective-permute-start(bf16[416,128]{1,0:T(8,128)(2,1)S(1)} %get-tuple-element.31), channel_id=1, source_target_pairs={{0,16},{16,0},{32,48},{48,32},{64,80},{80,64},{96,112},{112,96},{1... | collective-permute-start | bytes 319496 | tf_op jit(solution)/shard_map/ppermute | solution.py:467
  32.7 1.0 %collective-permute-done.1.sent = bf16[416,128]{1,0:T(8,128)(2,1)S(1)} collective-permute-done((bf16[416,128]{1,0:T(8,128)(2,1)S(1)}, bf16[416,128]{1,0:T(8,128)(2,1)S(1)}, u32[]{:S(2)}, u32[]{:S(2)}) %collective-permute-start.1) | collective-permute-done | bytes 106528 | tf_op jit(solution)/shard_map/ppermute | solution.py:467
  33.7 1.6 %collective-permute-start.4 = (bf16[416,128]{1,0:T(8,128)(2,1)S(1)}, bf16[416,128]{1,0:T(8,128)(2,1)S(1)}, u32[]{:S(2)}, u32[]{:S(2)}) collective-permute-start(bf16[416,128]{1,0:T(8,128)(2,1)S(1)} %get-tuple-element.32.pair), channel_id=1, source_target_pairs={{0,96},{16,112},{32,64},{48,80},{64,32},{80,48},{96,0},{112,16},{1... | collective-permute-start | bytes 319496 | tf_op jit(solution)/shard_map/ppermute | solution.py:467
  35.3 1.5 %collective-permute-start.3 = (bf16[416,128]{1,0:T(8,128)(2,1)S(1)}, bf16[416,128]{1,0:T(8,128)(2,1)S(1)}, u32[]{:S(2)}, u32[]{:S(2)}) collective-permute-start(bf16[416,128]{1,0:T(8,128)(2,1)S(1)} %get-tuple-element.32.pair), channel_id=1, source_target_pairs={{0,64},{16,80},{32,96},{48,112},{64,0},{80,16},{96,32},{112,48},{1... | collective-permute-start | bytes 319496 | tf_op jit(solution)/shard_map/ppermute | solution.py:467
  36.8 0.3 collective-permute-start.2
  37.0 2.2 %collective-permute-done.4.s3 = bf16[416,128]{1,0:T(8,128)(2,1)S(1)} collective-permute-done((bf16[416,128]{1,0:T(8,128)(2,1)S(1)}, bf16[416,128]{1,0:T(8,128)(2,1)S(1)}, u32[]{:S(2)}, u32[]{:S(2)}) %collective-permute-start.4) | collective-permute-done | bytes 106528 | tf_op jit(solution)/shard_map/ppermute | solution.py:467
  39.2 1.5 %collective-permute-done.3.s2 = bf16[416,128]{1,0:T(8,128)(2,1)S(1)} collective-permute-done((bf16[416,128]{1,0:T(8,128)(2,1)S(1)}, bf16[416,128]{1,0:T(8,128)(2,1)S(1)}, u32[]{:S(2)}, u32[]{:S(2)}) %collective-permute-start.3) | collective-permute-done | bytes 106528 | tf_op jit(solution)/shard_map/ppermute | solution.py:467
  40.7 1.1 %collective-permute-done.2.s1 = bf16[416,128]{1,0:T(8,128)(2,1)S(1)} collective-permute-done((bf16[416,128]{1,0:T(8,128)(2,1)S(1)}, bf16[416,128]{1,0:T(8,128)(2,1)S(1)}, u32[]{:S(2)}, u32[]{:S(2)}) %collective-permute-start.2) | collective-permute-done | bytes 106528 | tf_op jit(solution)/shard_map/ppermute | solution.py:467
  41.8 0.3 quadratic_forms.1
  42.2 1.5 %collective-permute-start.5 = (bf16[256,128]{1,0:T(8,128)(2,1)S(1)}, bf16[256,128]{1,0:T(8,128)(2,1)S(1)}, u32[]{:S(2)}, u32[]{:S(2)}) collective-permute-start(bf16[256,128]{1,0:T(8,128)(2,1)S(1)} %get-tuple-element.34.x_ref), channel_id=1, source_target_pairs={{0,16},{16,0},{32,48},{48,32},{64,80},{80,64},{96,112},{112,96},{1... | collective-permute-start | bytes 196616 | tf_op jit(solution)/shard_map/ppermute | solution.py:467
  43.7 1.1 %first_tokens.1 = (bf16[512,640]{1,0:T(8,128)(2,1)S(1)}, bf16[512,640]{1,0:T(8,128)(2,1)S(1)}) custom-call(bf16[256,128]{1,0:T(8,128)(2,1)S(1)} %get-tuple-element.34.x_ref, bf16[240,160]{1,0:T(8,128)(2,1)S(1)} %get-tuple-element.35.left, bf16[240,640]{1,0:T(8,128)(2,1)S(1)} %get-tuple-element.36.rq, bf16[240,640]{1,0:T(8,128)(2,1)S(1)} %get-tuple-element.37.rk), custom_call_target="tpu_custom_call" | custom-call | tf_op jit(solution)/shard_map/first_tokens/pallas_call | solution.py:420
  44.7 0.0 collective-permute-done.5.x_ref
  44.8 2.3 %rest_tokens.1 = (bf16[1024,640]{1,0:T(8,128)(2,1)}, bf16[1024,640]{1,0:T(8,128)(2,1)}) custom-call(bf16[256,128]{1,0:T(8,128)(2,1)S(1)} %collective-permute-done.5.x_ref, bf16[240,160]{1,0:T(8,128)(2,1)S(1)} %get-tuple-element.35.left, bf16[240,640]{1,0:T(8,128)(2,1)S(1)} %get-tuple-element.36.rq, bf16[240,640]{1,0:T(8,128)(2,1)S(1)} %get-tuple-element.37.rk, ...), custom_call_target="tpu_custom_call" | custom-call | tf_op jit(solution)/shard_map/rest_tokens/pallas_call | solution.py:447
  (13 shorter events, 0.1 us)
Async XLA Ops:
  5.2 5.4 %copy-start.5 = (f32[640]{0:T(1024)S(1)}, f32[640]{0:T(1024)}, u32[]{:S(2)}) copy-start(f32[640]{0:T(1024)} %param.28) | copy-start | bytes 7684
  5.2 5.5 %copy-start.6 = (f32[640]{0:T(1024)S(1)}, f32[640]{0:T(1024)}, u32[]{:S(2)}) copy-start(f32[640]{0:T(1024)} %param.29) | copy-start | bytes 7684
  5.2 5.5 %copy-start.7 = (f32[640]{0:T(1024)S(1)}, f32[640]{0:T(1024)}, u32[]{:S(2)}) copy-start(f32[640]{0:T(1024)} %param.31) | copy-start | bytes 7684
  5.2 5.5 %copy-start.8 = (f32[640]{0:T(1024)S(1)}, f32[640]{0:T(1024)}, u32[]{:S(2)}) copy-start(f32[640]{0:T(1024)} %param.32) | copy-start | bytes 7684
  5.2 14.3 %copy-start.1 = (bf16[64,5120]{1,0:T(8,128)(2,1)S(1)}, bf16[64,5120]{1,0:T(8,128)(2,1)}, u32[]{:S(2)}) copy-start(bf16[64,5120]{1,0:T(8,128)(2,1)} %pw) | copy-start | bytes 1966084
  5.2 14.3 %copy-start.2 = (f32[5120]{0:T(1024)S(1)}, f32[5120]{0:T(1024)}, u32[]{:S(2)}) copy-start(f32[5120]{0:T(1024)} %param.24) | copy-start | bytes 61444
  5.2 14.3 %copy-start.3 = (f32[5120]{0:T(1024)S(1)}, f32[5120]{0:T(1024)}, u32[]{:S(2)}) copy-start(f32[5120]{0:T(1024)} %param.25) | copy-start | bytes 61444
  5.2 14.3 %copy-start.4 = (f32[5120]{0:T(1024)S(1)}, f32[5120]{0:T(1024)}, u32[]{:S(2)}) copy-start(f32[5120]{0:T(1024)} %param.26) | copy-start | bytes 61444
  5.3 5.4 %collective-permute-start = (f32[2,4,16,128]{3,2,1,0:T(8,128)S(1)}, f32[2,4,16,128]{3,2,1,0:T(8,128)S(1)}, u32[]{:S(2)}, u32[]{:S(2)}) collective-permute-start(f32[2,4,16,128]{3,2,1,0:T(8,128)S(1)} %get-tuple-element.23), channel_id=1, source_target_pairs={{0,16},{16,32},{32,48},{48,64},{64,80},{80,96},{96,112},{112,0},{1... | collective-permute-start | bytes 196616 | tf_op jit(solution)/shard_map/ppermute | solution.py:472
  11.7 18.1 %all-to-all-start = ((bf16[16,128,128]{2,1,0:T(8,128)(2,1)}), bf16[16,128,128]{2,1,0:T(8,128)(2,1)S(1)}, u32[]{:S(2)}, u32[]{:S(2)}) async-start(bf16[16,128,128]{2,1,0:T(8,128)(2,1)} %own_block.1), calls=%async_computation | async-start | bytes 1048576 | tf_op jit(solution)/shard_map/all_to_all | solution.py:514
  19.5 10.3 %copy-start = (s32[128]{0:T(128)S(1)}, s32[128]{0:T(128)}, u32[]{:S(2)}) copy-start(s32[128]{0:T(128)} %packing.1) | copy-start | bytes 1540
  30.5 3.2 %collective-permute-start.1 = (bf16[416,128]{1,0:T(8,128)(2,1)S(1)}, bf16[416,128]{1,0:T(8,128)(2,1)S(1)}, u32[]{:S(2)}, u32[]{:S(2)}) collective-permute-start(bf16[416,128]{1,0:T(8,128)(2,1)S(1)} %get-tuple-element.31), channel_id=1, source_target_pairs={{0,16},{16,0},{32,48},{48,32},{64,80},{80,64},{96,112},{112,96},{1... | collective-permute-start | bytes 319496 | tf_op jit(solution)/shard_map/ppermute | solution.py:467
  33.7 5.5 %collective-permute-start.4 = (bf16[416,128]{1,0:T(8,128)(2,1)S(1)}, bf16[416,128]{1,0:T(8,128)(2,1)S(1)}, u32[]{:S(2)}, u32[]{:S(2)}) collective-permute-start(bf16[416,128]{1,0:T(8,128)(2,1)S(1)} %get-tuple-element.32.pair), channel_id=1, source_target_pairs={{0,96},{16,112},{32,64},{48,80},{64,32},{80,48},{96,0},{112,16},{1... | collective-permute-start | bytes 319496 | tf_op jit(solution)/shard_map/ppermute | solution.py:467
  35.3 5.5 %collective-permute-start.3 = (bf16[416,128]{1,0:T(8,128)(2,1)S(1)}, bf16[416,128]{1,0:T(8,128)(2,1)S(1)}, u32[]{:S(2)}, u32[]{:S(2)}) collective-permute-start(bf16[416,128]{1,0:T(8,128)(2,1)S(1)} %get-tuple-element.32.pair), channel_id=1, source_target_pairs={{0,64},{16,80},{32,96},{48,112},{64,0},{80,16},{96,32},{112,48},{1... | collective-permute-start | bytes 319496 | tf_op jit(solution)/shard_map/ppermute | solution.py:467
  36.8 5.0 %collective-permute-start.2 = (bf16[416,128]{1,0:T(8,128)(2,1)S(1)}, bf16[416,128]{1,0:T(8,128)(2,1)S(1)}, u32[]{:S(2)}, u32[]{:S(2)}) collective-permute-start(bf16[416,128]{1,0:T(8,128)(2,1)S(1)} %get-tuple-element.32.pair), channel_id=1, source_target_pairs={{0,32},{16,48},{32,0},{48,16},{64,96},{80,112},{96,64},{112,80},{1... | collective-permute-start | bytes 319496 | tf_op jit(solution)/shard_map/ppermute | solution.py:467
  42.2 2.6 %collective-permute-start.5 = (bf16[256,128]{1,0:T(8,128)(2,1)S(1)}, bf16[256,128]{1,0:T(8,128)(2,1)S(1)}, u32[]{:S(2)}, u32[]{:S(2)}) collective-permute-start(bf16[256,128]{1,0:T(8,128)(2,1)S(1)} %get-tuple-element.34.x_ref), channel_id=1, source_target_pairs={{0,16},{16,0},{32,48},{48,32},{64,80},{80,64},{96,112},{112,96},{1... | collective-permute-start | bytes 196616 | tf_op jit(solution)/shard_map/ppermute | solution.py:467

commit v5 on v4

--- a/solution.py
+++ b/solution.py
@@ -15,6 +15,7 @@
 HBM = pl.BlockSpec(memory_space=pltpu.HBM)
 MIB = 1 << 20
 EXT = 80
+GRAM = 48
 
 
 def mm(a, b, ca, cb):
@@ -48,10 +49,10 @@
     return jax.ShapeDtypeStruct(shape, kind)
 
 
-def folded(lwt, cw, wt, first, count, a):
+def folded(lwt, cw, wt, first, count):
     for k in range(first, first + count):
         high, low = halves(mm(lwt, cw[k], 1, 1))
-        at = a * 288 + (k % 9) * 16
+        at = (k // 9) * 288 + (k % 9) * 16
         wt[pl.ds(at, 16), :] = high
         wt[pl.ds(at + 144, 16), :] = low
 
@@ -117,22 +118,17 @@
     ]
     for c in small:
         c.start()
-    copies = chunks_of(cw_hbm, cw, sems, 0, 6, 3, 0)
-    for c in copies[:3]:
+    copies = chunks_of(cw_hbm, cw, sems, 0, 3, 6, 0)
+    for c in copies:
         c.start()
     for c in small:
         c.wait()
     lwt = lwt_ref[...]
+    act_out[...] = silu_normed(feat[...].astype(f32), gain[...].reshape(1, -1))
     for i, c in enumerate(copies):
-        if i < 4:
-            at = pl.ds(i * 128, 128)
-            act_out[at, :] = silu_normed(feat[at, :].astype(f32), gain[...].reshape(1, -1))
         c.wait()
-        if i + 3 < len(copies):
-            copies[i + 3].start()
-        folded(lwt, cw, wt, i * 3, 3, i // 3)
-        if i == 3:
-            gt[pl.ds(0, 288), :] = mm(wt[pl.ds(0, 288), :], act_out[...], 1, 1)
+        folded(lwt, cw, wt, i * 6, 6)
+    gt[pl.ds(0, 288), :] = mm(wt[pl.ds(0, 288), :], act_out[...], 1, 1)
     direct = mm(lwt, feat[...], 1, 1)
     const = jnp.sum(lwt.astype(f32) * bias[...].reshape(1, -1), axis=1, keepdims=True)
     const = const + jnp.transpose(lb[...].reshape(1, -1))
@@ -179,7 +175,7 @@
     small.wait()
     for i, c in enumerate(copies):
         c.wait()
-        folded(lwt[...], cw, wt, i * 3, 3, 0)
+        folded(lwt[...], cw, wt, i * 3, 3)
     gt[...] = mm(wt[...], act[...], 1, 1)
     for fo in range(2):
         for ro in range(4):
@@ -206,7 +202,7 @@
 
 def weights_kernel(
     pw, pb, shift, scale, wq_hbm, wk_hbm, bq, bk, gq, gk,
-    rq, rk, patch_gram, grams, wq, wk, parts, sems,
+    rq, rk, last, patch_gram, grams, wq, wk, parts, sems,
 ):
     width = pw.shape[1]
     chunk = width // 4
@@ -246,14 +242,20 @@
         pairs = mm(jnp.concatenate([high, low], axis=0), high, 1, 1)
         cross = pairs[EXT:, :]
         found.append(pairs[:EXT, :] + cross + jnp.transpose(cross))
-        high, low = halves(rows * gain[...])
+        rows = rows * gain[...]
+        shifted = iota(rows.shape, 0) == 65
+        high, low = halves(jnp.where(shifted, 0.0, rows))
         right[pl.ds(0, EXT), :] = high
-        right[pl.ds(EXT, EXT), :] = high
-        right[pl.ds(2 * EXT, EXT), :] = low
+        right[pl.ds(EXT, EXT), :] = low
+        last[n : n + 1, :] = jnp.sum(jnp.where(shifted, rows, 0.0), axis=0, keepdims=True)
     i, j = iota((EXT, EXT), 0), iota((EXT, EXT), 1)
-    diagonal = jnp.sum(jnp.where(i == j, found[1], 0.0), axis=1, keepdims=True)
-    grams[:, :EXT] = jnp.where(i >= j, found[0], found[1])
-    grams[:, EXT:] = jnp.broadcast_to(diagonal, (EXT, 128 - EXT))
+    square = jnp.where(i >= j, found[0], found[1])
+    grams[pl.ds(0, 32), :] = jnp.concatenate([square[:32, :64], square[32:64, :64]], axis=1)
+    grams[pl.ds(32, 16), :] = jnp.zeros((16, 128), f32)
+    grams[pl.ds(32, 2), pl.ds(0, EXT)] = found[0][64:66]
+    grams[pl.ds(34, 2), pl.ds(0, EXT)] = found[1][64:66]
+    diagonal = jnp.sum(jnp.where(i == j, found[1], 0.0), axis=0, keepdims=True)
+    grams[pl.ds(36, 1), pl.ds(0, EXT)] = diagonal
 
 
 def weights_only(pw, pb, shift, scale, wq, wk, bq, bk, gq, gk):
@@ -262,10 +264,11 @@
         weights_kernel,
         "weights_only",
         [
-            array((3 * EXT, part), bf16),
-            array((3 * EXT, part), bf16),
+            array((2 * EXT, part), bf16),
+            array((2 * EXT, part), bf16),
+            array((8, part), f32),
             array((EXT, EXT), f32),
-            array((EXT, 128), f32),
+            array((GRAM, 128), f32),
         ],
         [VMEM] * 4 + [HBM] * 2 + [VMEM] * 4,
         36,
@@ -302,6 +305,10 @@
     return call(
         block_kernel, "own_block", array((lax.axis_size("rows"), 128, 128), bf16), [VMEM] * 2, 4
     )(own, before)
+
+
+SLOTS = 256
+SENT = SLOTS + 2 * GRAM
 
 
 def select_kernel(packing, blocks, grams, keep, send):
@@ -321,80 +328,97 @@
             below = blocks[jnp.minimum(place + 1, last), pl.ds(64, 64)].astype(f32)
             value = own * here + jnp.where(upper, above * first, below * final)
             out[pl.ds(i * 64, 64), :] = value.astype(bf16)
-    send[pl.ds(256, EXT), :], send[pl.ds(256 + EXT, EXT), :] = halves(grams[...])
+    send[pl.ds(SLOTS, GRAM), :], send[pl.ds(SLOTS + GRAM, GRAM), :] = halves(grams[...])
 
 
 def selected(packing, blocks, grams):
     return call(
         select_kernel,
         "select_blocks",
-        [array((256, 128), bf16), array((256 + 2 * EXT, 128), bf16)],
+        [array((SLOTS, 128), bf16), array((SENT, 128), bf16)],
         [SMEM, VMEM, VMEM],
         4,
     )(packing, blocks, grams)
 
 
 def sent_grams(sent):
-    return sent[pl.ds(256, EXT), :].astype(f32) + sent[pl.ds(256 + EXT, EXT), :].astype(f32)
-
-
-def pair_kernel(keep, grams, sent, pair, pair_grams):
-    pair[pl.ds(0, 256), :] = keep[...] + sent[pl.ds(0, 256), :]
+    return sent[pl.ds(SLOTS, GRAM), :].astype(f32) + sent[pl.ds(SLOTS + GRAM, GRAM), :].astype(f32)
+
+
+def add_kernel(own, grams, sent, out, out_grams):
+    slots = pl.ds(0, SLOTS)
+    out[slots, :] = own[slots, :] + sent[slots, :]
     total = grams[...] + sent_grams(sent)
-    pair_grams[...] = total
-    pair[pl.ds(256, EXT), :], pair[pl.ds(256 + EXT, EXT), :] = halves(total)
-
-
-def paired(keep, grams, sent):
-    return call(
-        pair_kernel,
-        "pair_sums",
-        [array(sent.shape, bf16), array(grams.shape, f32)],
+    out_grams[...] = total
+    out[pl.ds(SLOTS, GRAM), :], out[pl.ds(SLOTS + GRAM, GRAM), :] = halves(total)
+
+
+def added(own, grams, sent):
+    return call(
+        add_kernel,
+        "add_sums",
+        [array((SENT, 128), bf16), array(grams.shape, f32)],
         [VMEM] * 3,
         4,
-    )(keep, grams, sent)
-
-
-def forms_kernel(patch_gram, pair, pair_grams, s1, s2, s3, mine, left):
-    blocks, total = pair[pl.ds(0, 256), :], pair_grams[...]
-    for sent in (s1, s2, s3):
-        blocks = blocks + sent[pl.ds(0, 256), :]
-        total = total + sent_grams(sent)
-    mine[...] = blocks
-    i, j = iota((EXT, EXT), 0), iota((EXT, EXT), 1)
+    )(own, grams, sent)
+
+
+def quadratic_forms(patch_gram, total):
     total = total * (1.0 / 5120.0)
-    square = total[:, :EXT]
-    gq = jnp.where(i > j, 2.0 * square, 0.0) + jnp.where(i == j, square, 0.0)
-    gk = jnp.where(i > j, 2.0 * jnp.transpose(square), 0.0)
-    gk = gk + jnp.where(i == j, total[:, EXT : EXT + 1], 0.0)
-    left[pl.ds(0, EXT), :] = jnp.concatenate(halves(patch_gram[...]), axis=1)
-    for n, g in enumerate((gq, gk)):
-        end = jnp.sum(jnp.where((i == 65) & (j == 65), g, 0.0), keepdims=True)
-        g = jnp.where((i == 66) & (j == 64), end, g)
-        left[pl.ds((n + 1) * EXT, EXT), :] = jnp.concatenate(halves(g), axis=1)
-
-
-def quadratic_forms(*args):
-    return call(
-        forms_kernel,
-        "quadratic_forms",
-        [array((256, 128), bf16), array((3 * EXT, 2 * EXT), bf16)],
+    i, j = iota((64, 64), 0), iota((64, 64), 1)
+    square = jnp.concatenate([total[:32, :64], total[:32, 64:]], axis=0)
+    turned = jnp.transpose(square)
+    squares = (
+        jnp.where(i > j, 2.0 * square, jnp.where(i == j, square, 0.0)),
+        jnp.where(i > j, 2.0 * turned, jnp.where(i == j, total[36:37, :64], 0.0)),
+    )
+    row, lane = iota((EXT - 64, EXT), 0), iota((EXT - 64, EXT), 1)
+    forms = [jnp.concatenate(halves(patch_gram), axis=1)]
+    for n, g in enumerate(squares):
+        const = total[32 + 2 * n : 33 + 2 * n, :EXT]
+        shift = total[33 + 2 * n : 34 + 2 * n, :EXT]
+        end = total[33 + 2 * n : 34 + 2 * n, 65:66]
+        below = jnp.where(lane < 64, 2.0 * const, jnp.where(lane == 64, const, 0.0))
+        linear = jnp.where(lane <= 64, 2.0 * shift, 0.0)
+        last = jnp.where(lane == 64, end, 0.0)
+        below = jnp.where(row == 0, below, jnp.where(row == 1, linear, 0.0))
+        below = jnp.where(row == 2, last, below)
+        g = jnp.concatenate([g, jnp.zeros((64, EXT - 64), f32)], axis=1)
+        g = jnp.concatenate([g, below], axis=0)
+        forms.append(jnp.concatenate(halves(g), axis=1))
+    return jnp.concatenate(forms, axis=0)
+
+
+def total_kernel(patch_gram, own, own_grams, s1, s2, s3, mine, forms):
+    slots = pl.ds(0, SLOTS)
+    mine[...] = own[slots, :] + s1[slots, :] + s2[slots, :] + s3[slots, :]
+    total = own_grams[...] + sent_grams(s1) + sent_grams(s2) + sent_grams(s3)
+    forms[...] = quadratic_forms(patch_gram[...], total)
+
+
+def totals(*args):
+    return call(
+        total_kernel,
+        "total_sums",
+        [array((SLOTS, 128), bf16), array((3 * EXT, 2 * EXT), bf16)],
         [VMEM] * 6,
         4,
     )(*args)
 
 
-def token_rows(x_ref, part, left, rights):
+def token_rows(x_ref, part, forms, rights, last):
     at = part * 128
     x = jnp.concatenate([x_ref[pl.ds(at, 64), :], x_ref[pl.ds(at + 64, 64), :]], axis=1)
-    tail = iota((EXT - 64, 256), 0)
-    xf = jnp.concatenate([x.astype(f32), jnp.where(tail == 0, 1.0, 0.0)], axis=0)
+    tail = jnp.where(iota((EXT - 64, 256), 0) == 0, 1.0, 0.0)
+    xf = jnp.concatenate([x.astype(f32), tail], axis=0)
     xe = xf.astype(bf16)
-    t = mm(left[...], jnp.concatenate([xe, xe], axis=0), 1, 0)
-    spread = jnp.sum(t[:EXT] * xf, axis=0, keepdims=True)
-    scale = lax.rsqrt(spread + epsilon)
-    found = []
-    for n, right in enumerate(rights):
+    lhs = jnp.transpose(xf).astype(bf16)
+    lhs = jnp.concatenate([lhs, lhs], axis=1)
+    t = mm(forms[...], jnp.concatenate([xe, xe], axis=0), 1, 0)
+    scale = lax.rsqrt(jnp.sum(t[:EXT] * xf, axis=0, keepdims=True) + epsilon)
+    row = iota((8, 256), 0)
+    stacked = jnp.zeros((8, 256), f32)
+    for n in range(2):
         tn = t[(n + 1) * EXT : (n + 2) * EXT]
         squares = (
             scale * scale * jnp.sum(tn * xf, axis=0, keepdims=True)
@@ -402,27 +426,32 @@
             + tn[66:67]
         )
         beta = lax.rsqrt(squares + epsilon)
-        alpha = scale * beta
-        y = xf * alpha + jnp.where(iota((EXT, 256), 0) == 65, beta, 0.0)
-        high, low = halves(y)
-        lhs = jnp.concatenate([high, low, high], axis=0)
-        found.append(mm(lhs, right[...], 0, 0).astype(bf16))
+        stacked = jnp.where(row == 2 * n, scale * beta, stacked)
+        stacked = jnp.where(row == 2 * n + 1, beta, stacked)
+    columns = jnp.transpose(stacked)
+    found = []
+    for n, right in enumerate(rights):
+        alpha, beta = columns[:, 2 * n : 2 * n + 1], columns[:, 2 * n + 1 : 2 * n + 2]
+        value = mm(lhs, right[...], 1, 0) * alpha + beta * last[n : n + 1, :]
+        found.append(value.astype(bf16))
     return found
 
 
-def first_kernel(x_ref, left, rq, rk, q_out, k_out):
+def first_kernel(x_ref, forms, rq, rk, last, q_out, k_out):
     for part in range(2):
         at = pl.ds(part * 256, 256)
-        q_out[at, :], k_out[at, :] = token_rows(x_ref, part, left, (rq, rk))
-
-
-def first_tokens(x, left, rq, rk):
-    return call(
-        first_kernel, "first_tokens", [array((512, rq.shape[1]), bf16)] * 2, [VMEM] * 4, 6
-    )(x, left, rq, rk)
-
-
-def rest_kernel(x_ref, left, rq, rk, q_first, k_first, q_out, k_out, q_buf, k_buf, sems):
+        q_out[at, :], k_out[at, :] = token_rows(x_ref, part, forms, (rq, rk), last)
+
+
+def first_tokens(x, forms, rq, rk, last):
+    return call(
+        first_kernel, "first_tokens", [array((512, rq.shape[1]), bf16)] * 2, [VMEM] * 5, 6
+    )(x, forms, rq, rk, last)
+
+
+def rest_kernel(
+    x_ref, forms, rq, rk, last, q_first, k_first, q_out, k_out, q_buf, k_buf, sems
+):
     core = lax.axis_index("tm") % 2
     copies = []
 
@@ -435,20 +464,20 @@
     send(q_first, q_out, core * 512, 512)
     send(k_first, k_out, core * 512, 512)
     for part in range(2):
-        q_buf[part], k_buf[part] = token_rows(x_ref, part, left, (rq, rk))
+        q_buf[part], k_buf[part] = token_rows(x_ref, part, forms, (rq, rk), last)
         send(q_buf.at[part], q_out, (1 - core) * 512 + part * 256, 256)
         send(k_buf.at[part], k_out, (1 - core) * 512 + part * 256, 256)
     for c in copies:
         c.wait()
 
 
-def all_tokens(x, left, rq, rk, q_first, k_first):
+def all_tokens(x, forms, rq, rk, last, q_first, k_first):
     width = rq.shape[1]
     return call(
         rest_kernel,
         "rest_tokens",
         [array((1024, width), bf16)] * 2,
-        [VMEM] * 6,
+        [VMEM] * 7,
         8,
         scratch=[
             pltpu.VMEM((2, 256, width), bf16),
@@ -456,7 +485,7 @@
             pltpu.SemaphoreType.DMA((6,)),
         ],
         out_specs=[HBM, HBM],
-    )(x, left, rq, rk, q_first, k_first)
+    )(x, forms, rq, rk, last, q_first, k_first)
 
 
 def in_hbm(x):
@@ -465,6 +494,11 @@
 
 def swapped(x, axis, bits):
     return lax.ppermute(x, axis, [(i, i ^ bits) for i in range(lax.axis_size(axis))])
+
+
+def by_core(x, axis, bits0, bits1):
+    route = [(i, i ^ (bits1 if i % 2 else bits0)) for i in range(lax.axis_size(axis))]
+    return lax.ppermute(x, axis, route)
 
 
 def moved(x, axis, by):
@@ -513,7 +547,7 @@
     copies, patch_weight = lax.optimization_barrier((copies, patch_weight))
     plane = lax.all_to_all(copies, "rows", 0, 0, tiled=True)
 
-    rq, rk, patch_gram, grams = weights_only(
+    rq, rk, last, patch_gram, grams = weights_only(
         patch_weight,
         row(patch_bias),
         row(shift_mod),
@@ -527,11 +561,11 @@
     )
     plane, grams = lax.optimization_barrier((plane, grams))
     keep, send = selected(packing, plane, grams)
-    pair, pair_grams = paired(keep, grams, swapped(send, "tm", 1))
-    sent = [swapped(pair, "tm", bits) for bits in (2, 4, 6)]
-    mine, left = quadratic_forms(patch_gram, pair, pair_grams, *sent)
-    other = swapped(mine, "tm", 1)
-    return all_tokens(other, left, rq, rk, *first_tokens(mine, left, rq, rk))
+    own, grams = added(keep, grams, swapped(send, "tm", 1))
+    sent = [swapped(own, "tm", bits) for bits in (2, 4, 6)]
+    mine, forms = totals(patch_gram, own, grams, *sent)
+    first = first_tokens(mine, forms, rq, rk, last)
+    return all_tokens(swapped(mine, "tm", 1), forms, rq, rk, last, *first)
 
 
 def solution(mesh):

time: 47.3 us -> 46.2 us (0.977)
  waiting for transfers between devices: 8.07 us -> 7.57 us
  transfers between devices with their start and end apart: 7 -> 7, of which waited for: 5 -> 5; matrix products, arithmetic and copies ran while one was open for 0% -> 0% of each run, Pallas kernels for 25% -> 26%
where the time goes in v5:
time: 46.2 us; the launch traced here: 46 us
  Pallas kernels  20.2 us (44%)
  starting transfers between devices  17.3 us (37%)
  waiting for transfers between devices  7.57 us (16%)
  between operations  0.87 us (2%)
    pallas_call x1, Pallas kernels, weights_only(): call(weights_kernel, 'weights_only', [array((2 * EXT, part), bf16), array...  8.04 us
    all_to_all x1, starting transfers between devices, per_device(): plane = lax.all_to_all(copies, 'rows', 0, 0, tiled=True)  7.77 us
    ppermute x5, starting transfers between devices, swapped(): lax.ppermute(x, axis, [(i, i ^ bits) for i in range(lax.axis_size(axis))])  6.92 us
    ppermute x5, waiting for transfers between devices, swapped(): lax.ppermute(x, axis, [(i, i ^ bits) for i in range(lax.axis_size(axis))])  5.31 us
    pallas_call x1, Pallas kernels, early_latents(): call(early_kernel, 'early_latents', [array((2, 4, 16, 128), f32), array((...  4.25 us
    pallas_call x1, Pallas kernels, late_latents(): call(late_kernel, 'late_latents', array((2, 4, 16, 128), f32), [VMEM] * 2...  2.72 us
    ppermute x1, starting transfers between devices, moved(): return lax.ppermute(x, axis, [(i, (i + by) % size) for i in range(size)])  2.61 us
    all_to_all x1, waiting for transfers between devices, per_device(): plane = lax.all_to_all(copies, 'rows', 0, 0, tiled=True)  2.25 us
  transfers between devices with their start and end apart: 7, of which 5 were waited for; matrix products, arithmetic and copies ran while one was open for 0% of the time, Pallas kernels for 26%

profile of v5, /device:TPU:1, one launch (start us, length us, event | category | flops | bytes accessed | tf_op | source)
XLA Modules:
  0.0 46.0 jit_solution(15378348036323233489)
XLA Ops:
  0.6 4.3 %early_latents.1 = (f32[2,4,16,128]{3,2,1,0:T(8,128)S(1)}, f32[2,4,16,128]{3,2,1,0:T(8,128)S(1)}, bf16[512,384]{1,0:T(8,128)(2,1)S(1)}) custom-call(bf16[512,384]{1,0:T(8,128)(2,1)} %bitcast.11, f32[384]{0:T(512)} %gain_hbm.1, f32[384]{0:T(512)} %bias_hbm.1, bf16[16,384]{1,0:T(8,128)(2,1)} %bitcast.12, f32[16]{0:T(128)} %lb_hbm.1, bf16[27,384,384]{2,1,0:T(8,128)(2,1)} %bitcast.9), custom_call_target="tpu_custom_call" | custom-call | tf_op jit(solution)/shard_map/early_latents/pallas_call | solution.py:149
  4.9 0.0 copy-start.5
  4.9 0.0 copy-start.6
  4.9 0.0 copy-start.7
  4.9 0.0 copy-start.8
  4.9 0.0 copy-start.1
  4.9 0.0 copy-start.2
  5.0 0.0 copy-start.3
  5.0 0.0 copy-start.4
  5.0 2.6 %collective-permute-start = (f32[2,4,16,128]{3,2,1,0:T(8,128)S(1)}, f32[2,4,16,128]{3,2,1,0:T(8,128)S(1)}, u32[]{:S(2)}, u32[]{:S(2)}) collective-permute-start(f32[2,4,16,128]{3,2,1,0:T(8,128)S(1)} %get-tuple-element.24), channel_id=1, source_target_pairs={{0,16},{16,32},{32,48},{48,64},{64,80},{80,96},{96,112},{112,0},{1... | collective-permute-start | bytes 196616 | tf_op jit(solution)/shard_map/ppermute | solution.py:506
  7.6 2.7 %late_latents.1.own = f32[2,4,16,128]{3,2,1,0:T(8,128)S(1)} custom-call(f32[2,4,16,128]{3,2,1,0:T(8,128)S(1)} %get-tuple-element.22.own, bf16[512,384]{1,0:T(8,128)(2,1)S(1)} %get-tuple-element.23.act, bf16[16,384]{1,0:T(8,128)(2,1)} %bitcast.13, bf16[27,384,384]{2,1,0:T(8,128)(2,1)} %bitcast.10), custom_call_target="tpu_custom_call" | custom-call | flops 3000000000 | bytes 5000000 | tf_op jit(solution)/shard_map/late_latents/pallas_call | solution.py:186
  10.3 0.0 copy-done.5
  10.4 0.0 collective-permute-done.before
  10.4 1.0 %own_block.1 = bf16[16,128,128]{2,1,0:T(8,128)(2,1)} custom-call(f32[2,4,16,128]{3,2,1,0:T(8,128)S(1)} %late_latents.1.own, f32[2,4,16,128]{3,2,1,0:T(8,128)S(1)} %collective-permute-done.before), custom_call_target="tpu_custom_call" | custom-call | tf_op jit(solution)/shard_map/own_block/pallas_call | solution.py:305
  11.4 7.8 %all-to-all-start = ((bf16[16,128,128]{2,1,0:T(8,128)(2,1)}), bf16[16,128,128]{2,1,0:T(8,128)(2,1)S(1)}, u32[]{:S(2)}, u32[]{:S(2)}) async-start(bf16[16,128,128]{2,1,0:T(8,128)(2,1)} %own_block.1), calls=%async_computation | async-start | bytes 1048576 | tf_op jit(solution)/shard_map/all_to_all | solution.py:548
  19.3 0.0 copy-start
  19.3 8.0 %weights_only.1 = (bf16[160,640]{1,0:T(8,128)(2,1)S(1)}, bf16[160,640]{1,0:T(8,128)(2,1)S(1)}, f32[8,640]{1,0:T(8,128)S(1)}, f32[80,80]{1,0:T(8,128)S(1)}, f32[48,128]{1,0:T(8,128)S(1)}) custom-call(bf16[64,5120]{1,0:T(8,128)(2,1)S(1)} %copy-done.1, f32[1,5120]{1,0:T(1,128)S(1)} %bitcast.6, f32[1,5120]{1,0:T(1,128)S(1)} %bitcast.7, f32[1,5120]{1,0:T(1,128)S(1)} %bitcast.8, ...), custom_call_target="tpu_custom_call" | custom-call | flops 8388608000 | bytes 13107200 | tf_op jit(solution)/shard_map/weights_only/pallas_call | solution.py:263
  27.3 2.2 %all-to-all-done.blocks = bf16[16,128,128]{2,1,0:T(8,128)(2,1)S(1)} async-done(((bf16[16,128,128]{2,1,0:T(8,128)(2,1)}), bf16[16,128,128]{2,1,0:T(8,128)(2,1)S(1)}, u32[]{:S(2)}, u32[]{:S(2)}) %all-to-all-start) | async-done | bytes 524320 | tf_op jit(solution)/shard_map/all_to_all | solution.py:548
  29.6 0.7 %select_blocks.1 = (bf16[256,128]{1,0:T(8,128)(2,1)S(1)}, bf16[352,128]{1,0:T(8,128)(2,1)S(1)}) custom-call(s32[128]{0:T(128)S(1)} %copy-done, bf16[16,128,128]{2,1,0:T(8,128)(2,1)S(1)} %all-to-all-done.blocks, f32[48,128]{1,0:T(8,128)S(1)} %get-tuple-element.30.grams), custom_call_target="tpu_custom_call" | custom-call | tf_op jit(solution)/shard_map/select_blocks/pallas_call | solution.py:335
  30.2 2.2 %collective-permute-start.1 = (bf16[352,128]{1,0:T(8,128)(2,1)S(1)}, bf16[352,128]{1,0:T(8,128)(2,1)S(1)}, u32[]{:S(2)}, u32[]{:S(2)}) collective-permute-start(bf16[352,128]{1,0:T(8,128)(2,1)S(1)} %get-tuple-element.32), channel_id=1, source_target_pairs={{0,16},{16,0},{32,48},{48,32},{64,80},{80,64},{96,112},{112,96},{1... | collective-permute-start | bytes 270344 | tf_op jit(solution)/shard_map/ppermute | solution.py:496
  32.4 0.9 %collective-permute-done.1.sent = bf16[352,128]{1,0:T(8,128)(2,1)S(1)} collective-permute-done((bf16[352,128]{1,0:T(8,128)(2,1)S(1)}, bf16[352,128]{1,0:T(8,128)(2,1)S(1)}, u32[]{:S(2)}, u32[]{:S(2)}) %collective-permute-start.1) | collective-permute-done | bytes 90144 | tf_op jit(solution)/shard_map/ppermute | solution.py:496
  33.4 1.5 %collective-permute-start.4 = (bf16[352,128]{1,0:T(8,128)(2,1)S(1)}, bf16[352,128]{1,0:T(8,128)(2,1)S(1)}, u32[]{:S(2)}, u32[]{:S(2)}) collective-permute-start(bf16[352,128]{1,0:T(8,128)(2,1)S(1)} %get-tuple-element.33.own), channel_id=1, source_target_pairs={{0,96},{16,112},{32,64},{48,80},{64,32},{80,48},{96,0},{112,16},{1... | collective-permute-start | bytes 270344 | tf_op jit(solution)/shard_map/ppermute | solution.py:496
  35.0 1.5 %collective-permute-start.3 = (bf16[352,128]{1,0:T(8,128)(2,1)S(1)}, bf16[352,128]{1,0:T(8,128)(2,1)S(1)}, u32[]{:S(2)}, u32[]{:S(2)}) collective-permute-start(bf16[352,128]{1,0:T(8,128)(2,1)S(1)} %get-tuple-element.33.own), channel_id=1, source_target_pairs={{0,64},{16,80},{32,96},{48,112},{64,0},{80,16},{96,32},{112,48},{1... | collective-permute-start | bytes 270344 | tf_op jit(solution)/shard_map/ppermute | solution.py:496
  36.5 0.3 collective-permute-start.2
  36.7 1.8 %collective-permute-done.4.s3 = bf16[352,128]{1,0:T(8,128)(2,1)S(1)} collective-permute-done((bf16[352,128]{1,0:T(8,128)(2,1)S(1)}, bf16[352,128]{1,0:T(8,128)(2,1)S(1)}, u32[]{:S(2)}, u32[]{:S(2)}) %collective-permute-start.4) | collective-permute-done | bytes 90144 | tf_op jit(solution)/shard_map/ppermute | solution.py:496
  38.5 1.4 %collective-permute-done.3.s2 = bf16[352,128]{1,0:T(8,128)(2,1)S(1)} collective-permute-done((bf16[352,128]{1,0:T(8,128)(2,1)S(1)}, bf16[352,128]{1,0:T(8,128)(2,1)S(1)}, u32[]{:S(2)}, u32[]{:S(2)}) %collective-permute-start.3) | collective-permute-done | bytes 90144 | tf_op jit(solution)/shard_map/ppermute | solution.py:496
  39.9 1.2 %collective-permute-done.2.s1 = bf16[352,128]{1,0:T(8,128)(2,1)S(1)} collective-permute-done((bf16[352,128]{1,0:T(8,128)(2,1)S(1)}, bf16[352,128]{1,0:T(8,128)(2,1)S(1)}, u32[]{:S(2)}, u32[]{:S(2)}) %collective-permute-start.2) | collective-permute-done | bytes 90144 | tf_op jit(solution)/shard_map/ppermute | solution.py:496
  41.1 0.3 total_sums.1
  41.4 1.4 %collective-permute-start.5 = (bf16[256,128]{1,0:T(8,128)(2,1)S(1)}, bf16[256,128]{1,0:T(8,128)(2,1)S(1)}, u32[]{:S(2)}, u32[]{:S(2)}) collective-permute-start(bf16[256,128]{1,0:T(8,128)(2,1)S(1)} %get-tuple-element.35.x_ref), channel_id=1, source_target_pairs={{0,16},{16,0},{32,48},{48,32},{64,80},{80,64},{96,112},{112,96},{1... | collective-permute-start | bytes 196616 | tf_op jit(solution)/shard_map/ppermute | solution.py:496
  42.8 1.0 %first_tokens.1 = (bf16[512,640]{1,0:T(8,128)(2,1)S(1)}, bf16[512,640]{1,0:T(8,128)(2,1)S(1)}) custom-call(bf16[256,128]{1,0:T(8,128)(2,1)S(1)} %get-tuple-element.35.x_ref, bf16[240,160]{1,0:T(8,128)(2,1)S(1)} %get-tuple-element.36.forms, bf16[160,640]{1,0:T(8,128)(2,1)S(1)} %get-tuple-element.37.rq, bf16[160,640]{1,0:T(8,128)(2,1)S(1)} %get-tuple-element.38.rk, ...), custom_call_target="tpu_custom_call" | custom-call | tf_op jit(solution)/shard_map/first_tokens/pallas_call | solution.py:447
  43.8 0.0 collective-permute-done.5.x_ref
  43.8 2.2 %rest_tokens.1 = (bf16[1024,640]{1,0:T(8,128)(2,1)}, bf16[1024,640]{1,0:T(8,128)(2,1)}) custom-call(bf16[256,128]{1,0:T(8,128)(2,1)S(1)} %collective-permute-done.5.x_ref, bf16[240,160]{1,0:T(8,128)(2,1)S(1)} %get-tuple-element.36.forms, bf16[160,640]{1,0:T(8,128)(2,1)S(1)} %get-tuple-element.37.rq, bf16[160,640]{1,0:T(8,128)(2,1)S(1)} %get-tuple-element.38.rk, ...), custom_call_target="tpu_custom_call" | custom-call | tf_op jit(solution)/shard_map/rest_tokens/pallas_call | solution.py:476
  (13 shorter events, 0.1 us)
Async XLA Ops:
  4.9 5.4 %copy-start.5 = (f32[640]{0:T(1024)S(1)}, f32[640]{0:T(1024)}, u32[]{:S(2)}) copy-start(f32[640]{0:T(1024)} %param.28) | copy-start | bytes 7684
  4.9 5.5 %copy-start.6 = (f32[640]{0:T(1024)S(1)}, f32[640]{0:T(1024)}, u32[]{:S(2)}) copy-start(f32[640]{0:T(1024)} %param.29) | copy-start | bytes 7684
  4.9 5.5 %copy-start.7 = (f32[640]{0:T(1024)S(1)}, f32[640]{0:T(1024)}, u32[]{:S(2)}) copy-start(f32[640]{0:T(1024)} %param.31) | copy-start | bytes 7684
  4.9 5.5 %copy-start.8 = (f32[640]{0:T(1024)S(1)}, f32[640]{0:T(1024)}, u32[]{:S(2)}) copy-start(f32[640]{0:T(1024)} %param.32) | copy-start | bytes 7684
  4.9 14.3 %copy-start.1 = (bf16[64,5120]{1,0:T(8,128)(2,1)S(1)}, bf16[64,5120]{1,0:T(8,128)(2,1)}, u32[]{:S(2)}) copy-start(bf16[64,5120]{1,0:T(8,128)(2,1)} %pw) | copy-start | bytes 1966084
  4.9 14.3 %copy-start.2 = (f32[5120]{0:T(1024)S(1)}, f32[5120]{0:T(1024)}, u32[]{:S(2)}) copy-start(f32[5120]{0:T(1024)} %param.24) | copy-start | bytes 61444
  5.0 14.3 %copy-start.3 = (f32[5120]{0:T(1024)S(1)}, f32[5120]{0:T(1024)}, u32[]{:S(2)}) copy-start(f32[5120]{0:T(1024)} %param.25) | copy-start | bytes 61444
  5.0 14.3 %copy-start.4 = (f32[5120]{0:T(1024)S(1)}, f32[5120]{0:T(1024)}, u32[]{:S(2)}) copy-start(f32[5120]{0:T(1024)} %param.26) | copy-start | bytes 61444
  5.0 5.4 %collective-permute-start = (f32[2,4,16,128]{3,2,1,0:T(8,128)S(1)}, f32[2,4,16,128]{3,2,1,0:T(8,128)S(1)}, u32[]{:S(2)}, u32[]{:S(2)}) collective-permute-start(f32[2,4,16,128]{3,2,1,0:T(8,128)S(1)} %get-tuple-element.24), channel_id=1, source_target_pairs={{0,16},{16,32},{32,48},{48,64},{64,80},{80,96},{96,112},{112,0},{1... | collective-permute-start | bytes 196616 | tf_op jit(solution)/shard_map/ppermute | solution.py:506
  11.4 18.1 %all-to-all-start = ((bf16[16,128,128]{2,1,0:T(8,128)(2,1)}), bf16[16,128,128]{2,1,0:T(8,128)(2,1)S(1)}, u32[]{:S(2)}, u32[]{:S(2)}) async-start(bf16[16,128,128]{2,1,0:T(8,128)(2,1)} %own_block.1), calls=%async_computation | async-start | bytes 1048576 | tf_op jit(solution)/shard_map/all_to_all | solution.py:548
  19.3 10.3 %copy-start = (s32[128]{0:T(128)S(1)}, s32[128]{0:T(128)}, u32[]{:S(2)}) copy-start(s32[128]{0:T(128)} %packing.1) | copy-start | bytes 1540
  30.2 3.2 %collective-permute-start.1 = (bf16[352,128]{1,0:T(8,128)(2,1)S(1)}, bf16[352,128]{1,0:T(8,128)(2,1)S(1)}, u32[]{:S(2)}, u32[]{:S(2)}) collective-permute-start(bf16[352,128]{1,0:T(8,128)(2,1)S(1)} %get-tuple-element.32), channel_id=1, source_target_pairs={{0,16},{16,0},{32,48},{48,32},{64,80},{80,64},{96,112},{112,96},{1... | collective-permute-start | bytes 270344 | tf_op jit(solution)/shard_map/ppermute | solution.py:496
  33.4 5.1 %collective-permute-start.4 = (bf16[352,128]{1,0:T(8,128)(2,1)S(1)}, bf16[352,128]{1,0:T(8,128)(2,1)S(1)}, u32[]{:S(2)}, u32[]{:S(2)}) collective-permute-start(bf16[352,128]{1,0:T(8,128)(2,1)S(1)} %get-tuple-element.33.own), channel_id=1, source_target_pairs={{0,96},{16,112},{32,64},{48,80},{64,32},{80,48},{96,0},{112,16},{1... | collective-permute-start | bytes 270344 | tf_op jit(solution)/shard_map/ppermute | solution.py:496
  35.0 5.0 %collective-permute-start.3 = (bf16[352,128]{1,0:T(8,128)(2,1)S(1)}, bf16[352,128]{1,0:T(8,128)(2,1)S(1)}, u32[]{:S(2)}, u32[]{:S(2)}) collective-permute-start(bf16[352,128]{1,0:T(8,128)(2,1)S(1)} %get-tuple-element.33.own), channel_id=1, source_target_pairs={{0,64},{16,80},{32,96},{48,112},{64,0},{80,16},{96,32},{112,48},{1... | collective-permute-start | bytes 270344 | tf_op jit(solution)/shard_map/ppermute | solution.py:496
  36.5 4.6 %collective-permute-start.2 = (bf16[352,128]{1,0:T(8,128)(2,1)S(1)}, bf16[352,128]{1,0:T(8,128)(2,1)S(1)}, u32[]{:S(2)}, u32[]{:S(2)}) collective-permute-start(bf16[352,128]{1,0:T(8,128)(2,1)S(1)} %get-tuple-element.33.own), channel_id=1, source_target_pairs={{0,32},{16,48},{32,0},{48,16},{64,96},{80,112},{96,64},{112,80},{1... | collective-permute-start | bytes 270344 | tf_op jit(solution)/shard_map/ppermute | solution.py:496
  41.4 2.4 %collective-permute-start.5 = (bf16[256,128]{1,0:T(8,128)(2,1)S(1)}, bf16[256,128]{1,0:T(8,128)(2,1)S(1)}, u32[]{:S(2)}, u32[]{:S(2)}) collective-permute-start(bf16[256,128]{1,0:T(8,128)(2,1)S(1)} %get-tuple-element.35.x_ref), channel_id=1, source_target_pairs={{0,16},{16,0},{32,48},{48,32},{64,80},{80,64},{96,112},{112,96},{1... | collective-permute-start | bytes 196616 | tf_op jit(solution)/shard_map/ppermute | solution.py:496

commit v6 on v5

--- a/solution.py
+++ b/solution.py
@@ -323,9 +323,9 @@
             here = jnp.where(ident // 16 == t, 1.0, 0.0)
             first = jnp.where(place == 0, 0.0, here)
             final = jnp.where(place == last, 0.0, here)
-            own = blocks[place, pl.ds(0, 64)].astype(f32)
-            above = blocks[jnp.maximum(place - 1, 0), pl.ds(64, 64)].astype(f32)
-            below = blocks[jnp.minimum(place + 1, last), pl.ds(64, 64)].astype(f32)
+            own = blocks[last - place, pl.ds(0, 64)].astype(f32)
+            above = blocks[last - jnp.maximum(place - 1, 0), pl.ds(64, 64)].astype(f32)
+            below = blocks[last - jnp.minimum(place + 1, last), pl.ds(64, 64)].astype(f32)
             value = own * here + jnp.where(upper, above * first, below * final)
             out[pl.ds(i * 64, 64), :] = value.astype(bf16)
     send[pl.ds(SLOTS, GRAM), :], send[pl.ds(SLOTS + GRAM, GRAM), :] = halves(grams[...])
@@ -545,7 +545,8 @@
     own = late_latents(own, act, lwt, conv_weight)
     copies = own_block(own, before)
     copies, patch_weight = lax.optimization_barrier((copies, patch_weight))
-    plane = lax.all_to_all(copies, "rows", 0, 0, tiled=True)
+    backwards = [list(range(lax.axis_size("rows")))[::-1]]
+    plane = lax.all_to_all(copies, "rows", 0, 0, tiled=True, axis_index_groups=backwards)
 
     rq, rk, last, patch_gram, grams = weights_only(
         patch_weight,

time: 46.2 us -> 44.9 us (0.972)
  waiting for transfers between devices: 7.57 us -> 4.94 us
  starting transfers between devices: 17.3 us -> 18.5 us
    all_to_all x1, waiting for transfers between devices: 2.25 us -> 0.01 us  [per_device(): lax.all_to_all(copies, 'rows', 0, 0, tiled=True, axis_index_groups=backwa...]
    all_to_all x1, starting transfers between devices: 7.77 us -> 9.67 us  [per_device(): lax.all_to_all(copies, 'rows', 0, 0, tiled=True, axis_index_groups=backwa...]
    ppermute x5, starting transfers between devices: 6.92 us -> 6.27 us  [swapped(): lax.ppermute(x, axis, [(i, i ^ bits) for i in range(lax.axis_size(axis))])]
  transfers between devices with their start and end apart: 7 -> 7, of which waited for: 5 -> 4; matrix products, arithmetic and copies ran while one was open for 0% -> 0% of each run, Pallas kernels for 26% -> 26%
where the time goes in v6:
time: 44.9 us; the launch traced here: 44.6 us
  Pallas kernels  20.2 us (45%)
  starting transfers between devices  18.5 us (41%)
  waiting for transfers between devices  4.94 us (11%)
  between operations  0.87 us (2%)
    all_to_all x1, starting transfers between devices, per_device(): lax.all_to_all(copies, 'rows', 0, 0, tiled=True, axis_index_groups=backwa...  9.67 us
    pallas_call x1, Pallas kernels, weights_only(): call(weights_kernel, 'weights_only', [array((2 * EXT, part), bf16), array...  8.05 us
    ppermute x5, starting transfers between devices, swapped(): lax.ppermute(x, axis, [(i, i ^ bits) for i in range(lax.axis_size(axis))])  6.27 us
    ppermute x5, waiting for transfers between devices, swapped(): lax.ppermute(x, axis, [(i, i ^ bits) for i in range(lax.axis_size(axis))])  4.93 us
    pallas_call x1, Pallas kernels, early_latents(): call(early_kernel, 'early_latents', [array((2, 4, 16, 128), f32), array((...  4.25 us
    pallas_call x1, Pallas kernels, late_latents(): call(late_kernel, 'late_latents', array((2, 4, 16, 128), f32), [VMEM] * 2...  2.72 us
    ppermute x1, starting transfers between devices, moved(): return lax.ppermute(x, axis, [(i, (i + by) % size) for i in range(size)])  2.61 us
    pallas_call x1, Pallas kernels, all_tokens(): call(rest_kernel, 'rest_tokens', [array((1024, width), bf16)] * 2, [VMEM]...  2.2 us
  transfers between devices with their start and end apart: 7, of which 4 were waited for; matrix products, arithmetic and copies ran while one was open for 0% of the time, Pallas kernels for 26%

profile of v6, /device:TPU:1, one launch (start us, length us, event | category | flops | bytes accessed | tf_op | source)
XLA Modules:
  0.0 44.6 jit_solution(9566141097755012035)
XLA Ops:
  0.6 4.3 %early_latents.1 = (f32[2,4,16,128]{3,2,1,0:T(8,128)S(1)}, f32[2,4,16,128]{3,2,1,0:T(8,128)S(1)}, bf16[512,384]{1,0:T(8,128)(2,1)S(1)}) custom-call(bf16[512,384]{1,0:T(8,128)(2,1)} %bitcast.11, f32[384]{0:T(512)} %gain_hbm.1, f32[384]{0:T(512)} %bias_hbm.1, bf16[16,384]{1,0:T(8,128)(2,1)} %bitcast.12, f32[16]{0:T(128)} %lb_hbm.1, bf16[27,384,384]{2,1,0:T(8,128)(2,1)} %bitcast.9), custom_call_target="tpu_custom_call" | custom-call | tf_op jit(solution)/shard_map/early_latents/pallas_call | solution.py:149
  4.9 0.0 copy-start.5
  4.9 0.0 copy-start.6
  4.9 0.0 copy-start.7
  4.9 0.0 copy-start.8
  4.9 0.0 copy-start.1
  4.9 0.0 copy-start.2
  5.0 0.0 copy-start.3
  5.0 0.0 copy-start.4
  5.0 2.6 %collective-permute-start = (f32[2,4,16,128]{3,2,1,0:T(8,128)S(1)}, f32[2,4,16,128]{3,2,1,0:T(8,128)S(1)}, u32[]{:S(2)}, u32[]{:S(2)}) collective-permute-start(f32[2,4,16,128]{3,2,1,0:T(8,128)S(1)} %get-tuple-element.24), channel_id=1, source_target_pairs={{0,16},{16,32},{32,48},{48,64},{64,80},{80,96},{96,112},{112,0},{1... | collective-permute-start | bytes 196616 | tf_op jit(solution)/shard_map/ppermute | solution.py:506
  7.6 2.7 %late_latents.1.own = f32[2,4,16,128]{3,2,1,0:T(8,128)S(1)} custom-call(f32[2,4,16,128]{3,2,1,0:T(8,128)S(1)} %get-tuple-element.22.own, bf16[512,384]{1,0:T(8,128)(2,1)S(1)} %get-tuple-element.23.act, bf16[16,384]{1,0:T(8,128)(2,1)} %bitcast.13, bf16[27,384,384]{2,1,0:T(8,128)(2,1)} %bitcast.10), custom_call_target="tpu_custom_call" | custom-call | flops 3000000000 | bytes 5000000 | tf_op jit(solution)/shard_map/late_latents/pallas_call | solution.py:186
  10.4 0.0 collective-permute-done.before
  10.4 1.0 %own_block.1 = bf16[16,128,128]{2,1,0:T(8,128)(2,1)} custom-call(f32[2,4,16,128]{3,2,1,0:T(8,128)S(1)} %late_latents.1.own, f32[2,4,16,128]{3,2,1,0:T(8,128)S(1)} %collective-permute-done.before), custom_call_target="tpu_custom_call" | custom-call | tf_op jit(solution)/shard_map/own_block/pallas_call | solution.py:305
  11.4 9.7 %all-to-all-start = ((bf16[16,128,128]{2,1,0:T(8,128)(2,1)}), bf16[16,128,128]{2,1,0:T(8,128)(2,1)S(1)}, u32[]{:S(2)}, u32[]{:S(2)}) async-start(bf16[16,128,128]{2,1,0:T(8,128)(2,1)} %own_block.1), calls=%async_computation | async-start | bytes 1048576 | tf_op jit(solution)/shard_map/all_to_all | solution.py:549
  21.1 0.0 copy-done.2
  21.1 0.0 copy-start
  21.2 8.0 %weights_only.1 = (bf16[160,640]{1,0:T(8,128)(2,1)S(1)}, bf16[160,640]{1,0:T(8,128)(2,1)S(1)}, f32[8,640]{1,0:T(8,128)S(1)}, f32[80,80]{1,0:T(8,128)S(1)}, f32[48,128]{1,0:T(8,128)S(1)}) custom-call(bf16[64,5120]{1,0:T(8,128)(2,1)S(1)} %copy-done.1, f32[1,5120]{1,0:T(1,128)S(1)} %bitcast.6, f32[1,5120]{1,0:T(1,128)S(1)} %bitcast.7, f32[1,5120]{1,0:T(1,128)S(1)} %bitcast.8, ...), custom_call_target="tpu_custom_call" | custom-call | flops 8388608000 | bytes 13107200 | tf_op jit(solution)/shard_map/weights_only/pallas_call | solution.py:263
  29.2 0.0 all-to-all-done.blocks
  29.2 0.7 %select_blocks.1 = (bf16[256,128]{1,0:T(8,128)(2,1)S(1)}, bf16[352,128]{1,0:T(8,128)(2,1)S(1)}) custom-call(s32[128]{0:T(128)S(1)} %copy-done, bf16[16,128,128]{2,1,0:T(8,128)(2,1)S(1)} %all-to-all-done.blocks, f32[48,128]{1,0:T(8,128)S(1)} %get-tuple-element.30.grams), custom_call_target="tpu_custom_call" | custom-call | tf_op jit(solution)/shard_map/select_blocks/pallas_call | solution.py:335
  29.9 1.3 %collective-permute-start.1 = (bf16[352,128]{1,0:T(8,128)(2,1)S(1)}, bf16[352,128]{1,0:T(8,128)(2,1)S(1)}, u32[]{:S(2)}, u32[]{:S(2)}) collective-permute-start(bf16[352,128]{1,0:T(8,128)(2,1)S(1)} %get-tuple-element.32), channel_id=1, source_target_pairs={{0,16},{16,0},{32,48},{48,32},{64,80},{80,64},{96,112},{112,96},{1... | collective-permute-start | bytes 270344 | tf_op jit(solution)/shard_map/ppermute | solution.py:496
  31.2 0.9 %collective-permute-done.1.sent = bf16[352,128]{1,0:T(8,128)(2,1)S(1)} collective-permute-done((bf16[352,128]{1,0:T(8,128)(2,1)S(1)}, bf16[352,128]{1,0:T(8,128)(2,1)S(1)}, u32[]{:S(2)}, u32[]{:S(2)}) %collective-permute-start.1) | collective-permute-done | bytes 90144 | tf_op jit(solution)/shard_map/ppermute | solution.py:496
  32.2 1.3 %collective-permute-start.4 = (bf16[352,128]{1,0:T(8,128)(2,1)S(1)}, bf16[352,128]{1,0:T(8,128)(2,1)S(1)}, u32[]{:S(2)}, u32[]{:S(2)}) collective-permute-start(bf16[352,128]{1,0:T(8,128)(2,1)S(1)} %get-tuple-element.33.own), channel_id=1, source_target_pairs={{0,96},{16,112},{32,64},{48,80},{64,32},{80,48},{96,0},{112,16},{1... | collective-permute-start | bytes 270344 | tf_op jit(solution)/shard_map/ppermute | solution.py:496
  33.5 1.2 %collective-permute-start.3 = (bf16[352,128]{1,0:T(8,128)(2,1)S(1)}, bf16[352,128]{1,0:T(8,128)(2,1)S(1)}, u32[]{:S(2)}, u32[]{:S(2)}) collective-permute-start(bf16[352,128]{1,0:T(8,128)(2,1)S(1)} %get-tuple-element.33.own), channel_id=1, source_target_pairs={{0,64},{16,80},{32,96},{48,112},{64,0},{80,16},{96,32},{112,48},{1... | collective-permute-start | bytes 270344 | tf_op jit(solution)/shard_map/ppermute | solution.py:496
  34.8 0.8 %collective-permute-start.2 = (bf16[352,128]{1,0:T(8,128)(2,1)S(1)}, bf16[352,128]{1,0:T(8,128)(2,1)S(1)}, u32[]{:S(2)}, u32[]{:S(2)}) collective-permute-start(bf16[352,128]{1,0:T(8,128)(2,1)S(1)} %get-tuple-element.33.own), channel_id=1, source_target_pairs={{0,32},{16,48},{32,0},{48,16},{64,96},{80,112},{96,64},{112,80},{1... | collective-permute-start | bytes 270344 | tf_op jit(solution)/shard_map/ppermute | solution.py:496
  35.5 1.8 %collective-permute-done.4.s3 = bf16[352,128]{1,0:T(8,128)(2,1)S(1)} collective-permute-done((bf16[352,128]{1,0:T(8,128)(2,1)S(1)}, bf16[352,128]{1,0:T(8,128)(2,1)S(1)}, u32[]{:S(2)}, u32[]{:S(2)}) %collective-permute-start.4) | collective-permute-done | bytes 90144 | tf_op jit(solution)/shard_map/ppermute | solution.py:496
  37.3 1.2 %collective-permute-done.3.s2 = bf16[352,128]{1,0:T(8,128)(2,1)S(1)} collective-permute-done((bf16[352,128]{1,0:T(8,128)(2,1)S(1)}, bf16[352,128]{1,0:T(8,128)(2,1)S(1)}, u32[]{:S(2)}, u32[]{:S(2)}) %collective-permute-start.3) | collective-permute-done | bytes 90144 | tf_op jit(solution)/shard_map/ppermute | solution.py:496
  38.5 1.0 %collective-permute-done.2.s1 = bf16[352,128]{1,0:T(8,128)(2,1)S(1)} collective-permute-done((bf16[352,128]{1,0:T(8,128)(2,1)S(1)}, bf16[352,128]{1,0:T(8,128)(2,1)S(1)}, u32[]{:S(2)}, u32[]{:S(2)}) %collective-permute-start.2) | collective-permute-done | bytes 90144 | tf_op jit(solution)/shard_map/ppermute | solution.py:496
  39.5 0.3 total_sums.1
  39.8 1.6 %collective-permute-start.5 = (bf16[256,128]{1,0:T(8,128)(2,1)S(1)}, bf16[256,128]{1,0:T(8,128)(2,1)S(1)}, u32[]{:S(2)}, u32[]{:S(2)}) collective-permute-start(bf16[256,128]{1,0:T(8,128)(2,1)S(1)} %get-tuple-element.35.x_ref), channel_id=1, source_target_pairs={{0,16},{16,0},{32,48},{48,32},{64,80},{80,64},{96,112},{112,96},{1... | collective-permute-start | bytes 196616 | tf_op jit(solution)/shard_map/ppermute | solution.py:496
  41.4 1.0 %first_tokens.1 = (bf16[512,640]{1,0:T(8,128)(2,1)S(1)}, bf16[512,640]{1,0:T(8,128)(2,1)S(1)}) custom-call(bf16[256,128]{1,0:T(8,128)(2,1)S(1)} %get-tuple-element.35.x_ref, bf16[240,160]{1,0:T(8,128)(2,1)S(1)} %get-tuple-element.36.forms, bf16[160,640]{1,0:T(8,128)(2,1)S(1)} %get-tuple-element.37.rq, bf16[160,640]{1,0:T(8,128)(2,1)S(1)} %get-tuple-element.38.rk, ...), custom_call_target="tpu_custom_call" | custom-call | tf_op jit(solution)/shard_map/first_tokens/pallas_call | solution.py:447
  42.4 0.0 collective-permute-done.5.x_ref
  42.4 2.2 %rest_tokens.1 = (bf16[1024,640]{1,0:T(8,128)(2,1)}, bf16[1024,640]{1,0:T(8,128)(2,1)}) custom-call(bf16[256,128]{1,0:T(8,128)(2,1)S(1)} %collective-permute-done.5.x_ref, bf16[240,160]{1,0:T(8,128)(2,1)S(1)} %get-tuple-element.36.forms, bf16[160,640]{1,0:T(8,128)(2,1)S(1)} %get-tuple-element.37.rq, bf16[160,640]{1,0:T(8,128)(2,1)S(1)} %get-tuple-element.38.rk, ...), custom_call_target="tpu_custom_call" | custom-call | tf_op jit(solution)/shard_map/rest_tokens/pallas_call | solution.py:476
  (13 shorter events, 0.1 us)
Async XLA Ops:
  4.9 5.4 %copy-start.5 = (f32[640]{0:T(1024)S(1)}, f32[640]{0:T(1024)}, u32[]{:S(2)}) copy-start(f32[640]{0:T(1024)} %param.28) | copy-start | bytes 7684
  4.9 5.5 %copy-start.6 = (f32[640]{0:T(1024)S(1)}, f32[640]{0:T(1024)}, u32[]{:S(2)}) copy-start(f32[640]{0:T(1024)} %param.29) | copy-start | bytes 7684
  4.9 5.5 %copy-start.7 = (f32[640]{0:T(1024)S(1)}, f32[640]{0:T(1024)}, u32[]{:S(2)}) copy-start(f32[640]{0:T(1024)} %param.31) | copy-start | bytes 7684
  4.9 5.5 %copy-start.8 = (f32[640]{0:T(1024)S(1)}, f32[640]{0:T(1024)}, u32[]{:S(2)}) copy-start(f32[640]{0:T(1024)} %param.32) | copy-start | bytes 7684
  4.9 16.2 %copy-start.1 = (bf16[64,5120]{1,0:T(8,128)(2,1)S(1)}, bf16[64,5120]{1,0:T(8,128)(2,1)}, u32[]{:S(2)}) copy-start(bf16[64,5120]{1,0:T(8,128)(2,1)} %pw) | copy-start | bytes 1966084
  4.9 16.2 %copy-start.2 = (f32[5120]{0:T(1024)S(1)}, f32[5120]{0:T(1024)}, u32[]{:S(2)}) copy-start(f32[5120]{0:T(1024)} %param.24) | copy-start | bytes 61444
  5.0 16.2 %copy-start.3 = (f32[5120]{0:T(1024)S(1)}, f32[5120]{0:T(1024)}, u32[]{:S(2)}) copy-start(f32[5120]{0:T(1024)} %param.25) | copy-start | bytes 61444
  5.0 16.2 %copy-start.4 = (f32[5120]{0:T(1024)S(1)}, f32[5120]{0:T(1024)}, u32[]{:S(2)}) copy-start(f32[5120]{0:T(1024)} %param.26) | copy-start | bytes 61444
  5.0 5.4 %collective-permute-start = (f32[2,4,16,128]{3,2,1,0:T(8,128)S(1)}, f32[2,4,16,128]{3,2,1,0:T(8,128)S(1)}, u32[]{:S(2)}, u32[]{:S(2)}) collective-permute-start(f32[2,4,16,128]{3,2,1,0:T(8,128)S(1)} %get-tuple-element.24), channel_id=1, source_target_pairs={{0,16},{16,32},{32,48},{48,64},{64,80},{80,96},{96,112},{112,0},{1... | collective-permute-start | bytes 196616 | tf_op jit(solution)/shard_map/ppermute | solution.py:506
  11.4 17.8 %all-to-all-start = ((bf16[16,128,128]{2,1,0:T(8,128)(2,1)}), bf16[16,128,128]{2,1,0:T(8,128)(2,1)S(1)}, u32[]{:S(2)}, u32[]{:S(2)}) async-start(bf16[16,128,128]{2,1,0:T(8,128)(2,1)} %own_block.1), calls=%async_computation | async-start | bytes 1048576 | tf_op jit(solution)/shard_map/all_to_all | solution.py:549
  21.1 8.1 %copy-start = (s32[128]{0:T(128)S(1)}, s32[128]{0:T(128)}, u32[]{:S(2)}) copy-start(s32[128]{0:T(128)} %packing.1) | copy-start | bytes 1540
  29.9 2.3 %collective-permute-start.1 = (bf16[352,128]{1,0:T(8,128)(2,1)S(1)}, bf16[352,128]{1,0:T(8,128)(2,1)S(1)}, u32[]{:S(2)}, u32[]{:S(2)}) collective-permute-start(bf16[352,128]{1,0:T(8,128)(2,1)S(1)} %get-tuple-element.32), channel_id=1, source_target_pairs={{0,16},{16,0},{32,48},{48,32},{64,80},{80,64},{96,112},{112,96},{1... | collective-permute-start | bytes 270344 | tf_op jit(solution)/shard_map/ppermute | solution.py:496
  32.2 5.1 %collective-permute-start.4 = (bf16[352,128]{1,0:T(8,128)(2,1)S(1)}, bf16[352,128]{1,0:T(8,128)(2,1)S(1)}, u32[]{:S(2)}, u32[]{:S(2)}) collective-permute-start(bf16[352,128]{1,0:T(8,128)(2,1)S(1)} %get-tuple-element.33.own), channel_id=1, source_target_pairs={{0,96},{16,112},{32,64},{48,80},{64,32},{80,48},{96,0},{112,16},{1... | collective-permute-start | bytes 270344 | tf_op jit(solution)/shard_map/ppermute | solution.py:496
  33.5 5.0 %collective-permute-start.3 = (bf16[352,128]{1,0:T(8,128)(2,1)S(1)}, bf16[352,128]{1,0:T(8,128)(2,1)S(1)}, u32[]{:S(2)}, u32[]{:S(2)}) collective-permute-start(bf16[352,128]{1,0:T(8,128)(2,1)S(1)} %get-tuple-element.33.own), channel_id=1, source_target_pairs={{0,64},{16,80},{32,96},{48,112},{64,0},{80,16},{96,32},{112,48},{1... | collective-permute-start | bytes 270344 | tf_op jit(solution)/shard_map/ppermute | solution.py:496
  34.8 4.8 %collective-permute-start.2 = (bf16[352,128]{1,0:T(8,128)(2,1)S(1)}, bf16[352,128]{1,0:T(8,128)(2,1)S(1)}, u32[]{:S(2)}, u32[]{:S(2)}) collective-permute-start(bf16[352,128]{1,0:T(8,128)(2,1)S(1)} %get-tuple-element.33.own), channel_id=1, source_target_pairs={{0,32},{16,48},{32,0},{48,16},{64,96},{80,112},{96,64},{112,80},{1... | collective-permute-start | bytes 270344 | tf_op jit(solution)/shard_map/ppermute | solution.py:496
  39.8 2.6 %collective-permute-start.5 = (bf16[256,128]{1,0:T(8,128)(2,1)S(1)}, bf16[256,128]{1,0:T(8,128)(2,1)S(1)}, u32[]{:S(2)}, u32[]{:S(2)}) collective-permute-start(bf16[256,128]{1,0:T(8,128)(2,1)S(1)} %get-tuple-element.35.x_ref), channel_id=1, source_target_pairs={{0,16},{16,0},{32,48},{48,32},{64,80},{80,64},{96,112},{112,96},{1... | collective-permute-start | bytes 196616 | tf_op jit(solution)/shard_map/ppermute | solution.py:496

commit v7 on v6

--- a/solution.py
+++ b/solution.py
@@ -136,7 +136,7 @@
     gt0, gt1 = gt.at[pl.ds(0, 288)], gt.at[pl.ds(288, 288)]
     for ro in range(4):
         for fo in (2, 3):
-            ahead[fo - 2, ro] = contributions({0: gt0, 1: gt1}, fo, ro)
+            ahead[fo - 2, ro] = contributions({0: gt0, 1: gt1}, fo, ro).astype(bf16)
         own[0, ro] = jnp.zeros((16, 128), f32)
         own[1, ro] = contributions({1: gt1}, 1, ro)
         if 1 <= ro < 3:
@@ -149,7 +149,7 @@
     return call(
         early_kernel,
         "early_latents",
-        [array((2, 4, 16, 128), f32), array((2, 4, 16, 128), f32), array((512, 384), bf16)],
+        [array((2, 4, 16, 128), bf16), array((2, 4, 16, 128), f32), array((512, 384), bf16)],
         [HBM] * 6,
         20,
         scratch=[
@@ -288,7 +288,7 @@
     first = jnp.where(lax.axis_index("tm") == 0, 0.0, 1.0)
     rows = []
     for ro in (1, 2, 3, 0):
-        frames = [own[f, ro] + before[f, ro] * first for f in range(2)]
+        frames = [own[f, ro] + before[f, ro].astype(f32) * first for f in range(2)]
         rows.append(jnp.concatenate(frames, axis=1).astype(bf16))
     source, target = iota((256, 256), 0), iota((256, 256), 1)
     wanted = ((target // 64) % 2) * 128 + 2 * (target % 64) + target // 128
@@ -406,18 +406,18 @@
     )(*args)
 
 
-def token_rows(x_ref, part, forms, rights, last):
-    at = part * 128
-    x = jnp.concatenate([x_ref[pl.ds(at, 64), :], x_ref[pl.ds(at + 64, 64), :]], axis=1)
-    tail = jnp.where(iota((EXT - 64, 256), 0) == 0, 1.0, 0.0)
+def token_rows(x_ref, slots, forms, rights, last):
+    x = jnp.concatenate([x_ref[pl.ds(i * 64, 64), :] for i in slots], axis=1)
+    count = x.shape[1]
+    tail = jnp.where(iota((EXT - 64, count), 0) == 0, 1.0, 0.0)
     xf = jnp.concatenate([x.astype(f32), tail], axis=0)
     xe = xf.astype(bf16)
     lhs = jnp.transpose(xf).astype(bf16)
     lhs = jnp.concatenate([lhs, lhs], axis=1)
     t = mm(forms[...], jnp.concatenate([xe, xe], axis=0), 1, 0)
     scale = lax.rsqrt(jnp.sum(t[:EXT] * xf, axis=0, keepdims=True) + epsilon)
-    row = iota((8, 256), 0)
-    stacked = jnp.zeros((8, 256), f32)
+    row = iota((8, count), 0)
+    stacked = jnp.zeros((8, count), f32)
     for n in range(2):
         tn = t[(n + 1) * EXT : (n + 2) * EXT]
         squares = (
@@ -438,9 +438,7 @@
 
 
 def first_kernel(x_ref, forms, rq, rk, last, q_out, k_out):
-    for part in range(2):
-        at = pl.ds(part * 256, 256)
-        q_out[at, :], k_out[at, :] = token_rows(x_ref, part, forms, (rq, rk), last)
+    q_out[...], k_out[...] = token_rows(x_ref, range(4), forms, (rq, rk), last)
 
 
 def first_tokens(x, forms, rq, rk, last):
@@ -464,7 +462,7 @@
     send(q_first, q_out, core * 512, 512)
     send(k_first, k_out, core * 512, 512)
     for part in range(2):
-        q_buf[part], k_buf[part] = token_rows(x_ref, part, forms, (rq, rk), last)
+        q_buf[part], k_buf[part] = token_rows(x_ref, (2 * part, 2 * part + 1), forms, (rq, rk), last)
         send(q_buf.at[part], q_out, (1 - core) * 512 + part * 256, 256)
         send(k_buf.at[part], k_out, (1 - core) * 512 + part * 256, 256)
     for c in copies:
@@ -563,7 +561,7 @@
     plane, grams = lax.optimization_barrier((plane, grams))
     keep, send = selected(packing, plane, grams)
     own, grams = added(keep, grams, swapped(send, "tm", 1))
-    sent = [swapped(own, "tm", bits) for bits in (2, 4, 6)]
+    sent = [by_core(own, "tm", 2, 6), swapped(own, "tm", 4), by_core(own, "tm", 6, 2)]
     mine, forms = totals(patch_gram, own, grams, *sent)
     first = first_tokens(mine, forms, rq, rk, last)
     return all_tokens(swapped(mine, "tm", 1), forms, rq, rk, last, *first)

time: 44.9 us -> 44.3 us (0.987)
  starting transfers between devices: 18.5 us -> 17.3 us
  waiting for transfers between devices: 4.94 us -> 5.72 us
    ppermute x5 -> x3, starting transfers between devices: 6.27 us -> 2.81 us  [swapped(): lax.ppermute(x, axis, [(i, i ^ bits) for i in range(lax.axis_size(axis))])]
    ppermute x0 -> x2, waiting for transfers between devices: none -> 2.6 us  [by_core(): return lax.ppermute(x, axis, route)]
    ppermute x0 -> x2, starting transfers between devices: none -> 2.2 us  [by_core(): return lax.ppermute(x, axis, route)]
    ppermute x5 -> x3, waiting for transfers between devices: 4.93 us -> 3.11 us  [swapped(): lax.ppermute(x, axis, [(i, i ^ bits) for i in range(lax.axis_size(axis))])]
  transfers between devices with their start and end apart: 7 -> 7, of which waited for: 4 -> 4; matrix products, arithmetic and copies ran while one was open for 0% -> 0% of each run, Pallas kernels for 26% -> 27%
where the time goes in v7:
time: 44.3 us; the launch traced here: 44 us
  Pallas kernels  20.1 us (45%)
  starting transfers between devices  17.3 us (39%)
  waiting for transfers between devices  5.72 us (13%)
  between operations  0.87 us (2%)
    all_to_all x1, starting transfers between devices, per_device(): lax.all_to_all(copies, 'rows', 0, 0, tiled=True, axis_index_groups=backwa...  9.67 us
    pallas_call x1, Pallas kernels, weights_only(): call(weights_kernel, 'weights_only', [array((2 * EXT, part), bf16), array...  8.04 us
    pallas_call x1, Pallas kernels, early_latents(): call(early_kernel, 'early_latents', [array((2, 4, 16, 128), bf16), array(...  4.26 us
    ppermute x3, waiting for transfers between devices, swapped(): lax.ppermute(x, axis, [(i, i ^ bits) for i in range(lax.axis_size(axis))])  3.11 us
    ppermute x3, starting transfers between devices, swapped(): lax.ppermute(x, axis, [(i, i ^ bits) for i in range(lax.axis_size(axis))])  2.81 us
    pallas_call x1, Pallas kernels, late_latents(): call(late_kernel, 'late_latents', array((2, 4, 16, 128), f32), [VMEM] * 2...  2.72 us
    ppermute x1, starting transfers between devices, moved(): return lax.ppermute(x, axis, [(i, (i + by) % size) for i in range(size)])  2.61 us
    ppermute x2, waiting for transfers between devices, by_core(): return lax.ppermute(x, axis, route)  2.6 us
  transfers between devices with their start and end apart: 7, of which 4 were waited for; matrix products, arithmetic and copies ran while one was open for 0% of the time, Pallas kernels for 27%

profile of v7, /device:TPU:1, one launch (start us, length us, event | category | flops | bytes accessed | tf_op | source)
XLA Modules:
  0.0 44.0 jit_solution(464942994506000034)
XLA Ops:
  0.6 4.3 %early_latents.1 = (bf16[2,4,16,128]{3,2,1,0:T(8,128)(2,1)S(1)}, f32[2,4,16,128]{3,2,1,0:T(8,128)S(1)}, bf16[512,384]{1,0:T(8,128)(2,1)S(1)}) custom-call(bf16[512,384]{1,0:T(8,128)(2,1)} %bitcast.11, f32[384]{0:T(512)} %gain_hbm.1, f32[384]{0:T(512)} %bias_hbm.1, bf16[16,384]{1,0:T(8,128)(2,1)} %bitcast.12, f32[16]{0:T(128)} %lb_hbm.1, ...), custom_call_target="tpu_custom_call" | custom-call | tf_op jit(solution)/shard_map/early_latents/pallas_call | solution.py:149
  4.9 0.0 copy-start.5
  4.9 0.0 copy-start.6
  4.9 0.0 copy-start.7
  4.9 0.0 copy-start.8
  4.9 0.0 copy-start.1
  5.0 0.0 copy-start.2
  5.0 0.0 copy-start.3
  5.0 0.0 copy-start.4
  5.0 2.6 %collective-permute-start = (bf16[2,4,16,128]{3,2,1,0:T(8,128)(2,1)S(1)}, bf16[2,4,16,128]{3,2,1,0:T(8,128)(2,1)S(1)}, u32[]{:S(2)}, u32[]{:S(2)}) collective-permute-start(bf16[2,4,16,128]{3,2,1,0:T(8,128)(2,1)S(1)} %get-tuple-element.24), channel_id=1, source_target_pairs={{0,16},{16,32},{32,48},{48,64},{64,80},{80,96},{96,112},{112,0},{1... | collective-permute-start | bytes 98312 | tf_op jit(solution)/shard_map/ppermute | solution.py:504
  7.6 2.7 %late_latents.1.own = f32[2,4,16,128]{3,2,1,0:T(8,128)S(1)} custom-call(f32[2,4,16,128]{3,2,1,0:T(8,128)S(1)} %get-tuple-element.22.own, bf16[512,384]{1,0:T(8,128)(2,1)S(1)} %get-tuple-element.23.act, bf16[16,384]{1,0:T(8,128)(2,1)} %bitcast.13, bf16[27,384,384]{2,1,0:T(8,128)(2,1)} %bitcast.10), custom_call_target="tpu_custom_call" | custom-call | flops 3000000000 | bytes 5000000 | tf_op jit(solution)/shard_map/late_latents/pallas_call | solution.py:186
  10.3 0.0 copy-done.5
  10.4 0.0 collective-permute-done.before
  10.4 1.0 %own_block.1 = bf16[16,128,128]{2,1,0:T(8,128)(2,1)} custom-call(f32[2,4,16,128]{3,2,1,0:T(8,128)S(1)} %late_latents.1.own, bf16[2,4,16,128]{3,2,1,0:T(8,128)(2,1)S(1)} %collective-permute-done.before), custom_call_target="tpu_custom_call" | custom-call | tf_op jit(solution)/shard_map/own_block/pallas_call | solution.py:305
  11.4 9.7 %all-to-all-start = ((bf16[16,128,128]{2,1,0:T(8,128)(2,1)}), bf16[16,128,128]{2,1,0:T(8,128)(2,1)S(1)}, u32[]{:S(2)}, u32[]{:S(2)}) async-start(bf16[16,128,128]{2,1,0:T(8,128)(2,1)} %own_block.1), calls=%async_computation | async-start | bytes 1048576 | tf_op jit(solution)/shard_map/all_to_all | solution.py:547
  21.1 0.0 copy-start
  21.2 8.0 %weights_only.1 = (bf16[160,640]{1,0:T(8,128)(2,1)S(1)}, bf16[160,640]{1,0:T(8,128)(2,1)S(1)}, f32[8,640]{1,0:T(8,128)S(1)}, f32[80,80]{1,0:T(8,128)S(1)}, f32[48,128]{1,0:T(8,128)S(1)}) custom-call(bf16[64,5120]{1,0:T(8,128)(2,1)S(1)} %copy-done.1, f32[1,5120]{1,0:T(1,128)S(1)} %bitcast.6, f32[1,5120]{1,0:T(1,128)S(1)} %bitcast.7, f32[1,5120]{1,0:T(1,128)S(1)} %bitcast.8, ...), custom_call_target="tpu_custom_call" | custom-call | flops 8388608000 | bytes 13107200 | tf_op jit(solution)/shard_map/weights_only/pallas_call | solution.py:263
  29.2 0.0 all-to-all-done.blocks
  29.2 0.7 %select_blocks.1 = (bf16[256,128]{1,0:T(8,128)(2,1)S(1)}, bf16[352,128]{1,0:T(8,128)(2,1)S(1)}) custom-call(s32[128]{0:T(128)S(1)} %copy-done, bf16[16,128,128]{2,1,0:T(8,128)(2,1)S(1)} %all-to-all-done.blocks, f32[48,128]{1,0:T(8,128)S(1)} %get-tuple-element.30.grams), custom_call_target="tpu_custom_call" | custom-call | tf_op jit(solution)/shard_map/select_blocks/pallas_call | solution.py:335
  29.9 1.0 %collective-permute-start.1 = (bf16[352,128]{1,0:T(8,128)(2,1)S(1)}, bf16[352,128]{1,0:T(8,128)(2,1)S(1)}, u32[]{:S(2)}, u32[]{:S(2)}) collective-permute-start(bf16[352,128]{1,0:T(8,128)(2,1)S(1)} %get-tuple-element.32), channel_id=1, source_target_pairs={{0,16},{16,0},{32,48},{48,32},{64,80},{80,64},{96,112},{112,96},{1... | collective-permute-start | bytes 270344 | tf_op jit(solution)/shard_map/ppermute | solution.py:494
  30.9 0.9 %collective-permute-done.1.sent = bf16[352,128]{1,0:T(8,128)(2,1)S(1)} collective-permute-done((bf16[352,128]{1,0:T(8,128)(2,1)S(1)}, bf16[352,128]{1,0:T(8,128)(2,1)S(1)}, u32[]{:S(2)}, u32[]{:S(2)}) %collective-permute-start.1) | collective-permute-done | bytes 90144 | tf_op jit(solution)/shard_map/ppermute | solution.py:494
  31.8 0.8 %collective-permute-start.4 = (bf16[352,128]{1,0:T(8,128)(2,1)S(1)}, bf16[352,128]{1,0:T(8,128)(2,1)S(1)}, u32[]{:S(2)}, u32[]{:S(2)}) collective-permute-start(bf16[352,128]{1,0:T(8,128)(2,1)S(1)} %get-tuple-element.33.own), channel_id=1, source_target_pairs={{0,96},{16,48},{32,64},{48,16},{64,32},{80,112},{96,0},{112,80},{1... | collective-permute-start | bytes 270344 | tf_op jit(solution)/shard_map/ppermute | solution.py:499
  32.6 1.7 %collective-permute-start.3 = (bf16[352,128]{1,0:T(8,128)(2,1)S(1)}, bf16[352,128]{1,0:T(8,128)(2,1)S(1)}, u32[]{:S(2)}, u32[]{:S(2)}) collective-permute-start(bf16[352,128]{1,0:T(8,128)(2,1)S(1)} %get-tuple-element.33.own), channel_id=1, source_target_pairs={{0,64},{16,80},{32,96},{48,112},{64,0},{80,16},{96,32},{112,48},{1... | collective-permute-start | bytes 270344 | tf_op jit(solution)/shard_map/ppermute | solution.py:494
  34.4 1.4 %collective-permute-start.2 = (bf16[352,128]{1,0:T(8,128)(2,1)S(1)}, bf16[352,128]{1,0:T(8,128)(2,1)S(1)}, u32[]{:S(2)}, u32[]{:S(2)}) collective-permute-start(bf16[352,128]{1,0:T(8,128)(2,1)S(1)} %get-tuple-element.33.own), channel_id=1, source_target_pairs={{0,32},{16,112},{32,0},{48,80},{64,96},{80,48},{96,64},{112,16},{1... | collective-permute-start | bytes 270344 | tf_op jit(solution)/shard_map/ppermute | solution.py:499
  35.8 0.0 collective-permute-done.4.s3
  35.8 1.8 %collective-permute-done.3.s2 = bf16[352,128]{1,0:T(8,128)(2,1)S(1)} collective-permute-done((bf16[352,128]{1,0:T(8,128)(2,1)S(1)}, bf16[352,128]{1,0:T(8,128)(2,1)S(1)}, u32[]{:S(2)}, u32[]{:S(2)}) %collective-permute-start.3) | collective-permute-done | bytes 90144 | tf_op jit(solution)/shard_map/ppermute | solution.py:494
  37.6 2.6 %collective-permute-done.2.s1 = bf16[352,128]{1,0:T(8,128)(2,1)S(1)} collective-permute-done((bf16[352,128]{1,0:T(8,128)(2,1)S(1)}, bf16[352,128]{1,0:T(8,128)(2,1)S(1)}, u32[]{:S(2)}, u32[]{:S(2)}) %collective-permute-start.2) | collective-permute-done | bytes 90144 | tf_op jit(solution)/shard_map/ppermute | solution.py:499
  40.2 0.3 total_sums.1
  40.5 0.1 collective-permute-start.5
  40.6 0.9 %first_tokens.1 = (bf16[512,640]{1,0:T(8,128)(2,1)S(1)}, bf16[512,640]{1,0:T(8,128)(2,1)S(1)}) custom-call(bf16[256,128]{1,0:T(8,128)(2,1)S(1)} %get-tuple-element.35.x_ref, bf16[240,160]{1,0:T(8,128)(2,1)S(1)} %get-tuple-element.36.forms, bf16[160,640]{1,0:T(8,128)(2,1)S(1)} %get-tuple-element.37.rq, bf16[160,640]{1,0:T(8,128)(2,1)S(1)} %get-tuple-element.38.rk, ...), custom_call_target="tpu_custom_call" | custom-call | tf_op jit(solution)/shard_map/first_tokens/pallas_call | solution.py:445
  41.5 0.3 collective-permute-done.5.x_ref
  41.8 2.2 %rest_tokens.1 = (bf16[1024,640]{1,0:T(8,128)(2,1)}, bf16[1024,640]{1,0:T(8,128)(2,1)}) custom-call(bf16[256,128]{1,0:T(8,128)(2,1)S(1)} %collective-permute-done.5.x_ref, bf16[240,160]{1,0:T(8,128)(2,1)S(1)} %get-tuple-element.36.forms, bf16[160,640]{1,0:T(8,128)(2,1)S(1)} %get-tuple-element.37.rq, bf16[160,640]{1,0:T(8,128)(2,1)S(1)} %get-tuple-element.38.rk, ...), custom_call_target="tpu_custom_call" | custom-call | tf_op jit(solution)/shard_map/rest_tokens/pallas_call | solution.py:474
  (13 shorter events, 0.1 us)
Async XLA Ops:
  4.9 5.4 %copy-start.5 = (f32[640]{0:T(1024)S(1)}, f32[640]{0:T(1024)}, u32[]{:S(2)}) copy-start(f32[640]{0:T(1024)} %param.28) | copy-start | bytes 7684
  4.9 5.4 %copy-start.6 = (f32[640]{0:T(1024)S(1)}, f32[640]{0:T(1024)}, u32[]{:S(2)}) copy-start(f32[640]{0:T(1024)} %param.29) | copy-start | bytes 7684
  4.9 5.5 %copy-start.7 = (f32[640]{0:T(1024)S(1)}, f32[640]{0:T(1024)}, u32[]{:S(2)}) copy-start(f32[640]{0:T(1024)} %param.31) | copy-start | bytes 7684
  4.9 5.5 %copy-start.8 = (f32[640]{0:T(1024)S(1)}, f32[640]{0:T(1024)}, u32[]{:S(2)}) copy-start(f32[640]{0:T(1024)} %param.32) | copy-start | bytes 7684
  4.9 16.2 %copy-start.1 = (bf16[64,5120]{1,0:T(8,128)(2,1)S(1)}, bf16[64,5120]{1,0:T(8,128)(2,1)}, u32[]{:S(2)}) copy-start(bf16[64,5120]{1,0:T(8,128)(2,1)} %pw) | copy-start | bytes 1966084
  5.0 16.2 %copy-start.2 = (f32[5120]{0:T(1024)S(1)}, f32[5120]{0:T(1024)}, u32[]{:S(2)}) copy-start(f32[5120]{0:T(1024)} %param.24) | copy-start | bytes 61444
  5.0 16.2 %copy-start.3 = (f32[5120]{0:T(1024)S(1)}, f32[5120]{0:T(1024)}, u32[]{:S(2)}) copy-start(f32[5120]{0:T(1024)} %param.25) | copy-start | bytes 61444
  5.0 16.2 %copy-start.4 = (f32[5120]{0:T(1024)S(1)}, f32[5120]{0:T(1024)}, u32[]{:S(2)}) copy-start(f32[5120]{0:T(1024)} %param.26) | copy-start | bytes 61444
  5.0 5.4 %collective-permute-start = (bf16[2,4,16,128]{3,2,1,0:T(8,128)(2,1)S(1)}, bf16[2,4,16,128]{3,2,1,0:T(8,128)(2,1)S(1)}, u32[]{:S(2)}, u32[]{:S(2)}) collective-permute-start(bf16[2,4,16,128]{3,2,1,0:T(8,128)(2,1)S(1)} %get-tuple-element.24), channel_id=1, source_target_pairs={{0,16},{16,32},{32,48},{48,64},{64,80},{80,96},{96,112},{112,0},{1... | collective-permute-start | bytes 98312 | tf_op jit(solution)/shard_map/ppermute | solution.py:504
  11.4 17.8 %all-to-all-start = ((bf16[16,128,128]{2,1,0:T(8,128)(2,1)}), bf16[16,128,128]{2,1,0:T(8,128)(2,1)S(1)}, u32[]{:S(2)}, u32[]{:S(2)}) async-start(bf16[16,128,128]{2,1,0:T(8,128)(2,1)} %own_block.1), calls=%async_computation | async-start | bytes 1048576 | tf_op jit(solution)/shard_map/all_to_all | solution.py:547
  21.1 8.1 %copy-start = (s32[128]{0:T(128)S(1)}, s32[128]{0:T(128)}, u32[]{:S(2)}) copy-start(s32[128]{0:T(128)} %packing.1) | copy-start | bytes 1540
  29.9 1.9 %collective-permute-start.1 = (bf16[352,128]{1,0:T(8,128)(2,1)S(1)}, bf16[352,128]{1,0:T(8,128)(2,1)S(1)}, u32[]{:S(2)}, u32[]{:S(2)}) collective-permute-start(bf16[352,128]{1,0:T(8,128)(2,1)S(1)} %get-tuple-element.32), channel_id=1, source_target_pairs={{0,16},{16,0},{32,48},{48,32},{64,80},{80,64},{96,112},{112,96},{1... | collective-permute-start | bytes 270344 | tf_op jit(solution)/shard_map/ppermute | solution.py:494
  31.8 3.9 %collective-permute-start.4 = (bf16[352,128]{1,0:T(8,128)(2,1)S(1)}, bf16[352,128]{1,0:T(8,128)(2,1)S(1)}, u32[]{:S(2)}, u32[]{:S(2)}) collective-permute-start(bf16[352,128]{1,0:T(8,128)(2,1)S(1)} %get-tuple-element.33.own), channel_id=1, source_target_pairs={{0,96},{16,48},{32,64},{48,16},{64,32},{80,112},{96,0},{112,80},{1... | collective-permute-start | bytes 270344 | tf_op jit(solution)/shard_map/ppermute | solution.py:499
  32.6 5.0 %collective-permute-start.3 = (bf16[352,128]{1,0:T(8,128)(2,1)S(1)}, bf16[352,128]{1,0:T(8,128)(2,1)S(1)}, u32[]{:S(2)}, u32[]{:S(2)}) collective-permute-start(bf16[352,128]{1,0:T(8,128)(2,1)S(1)} %get-tuple-element.33.own), channel_id=1, source_target_pairs={{0,64},{16,80},{32,96},{48,112},{64,0},{80,16},{96,32},{112,48},{1... | collective-permute-start | bytes 270344 | tf_op jit(solution)/shard_map/ppermute | solution.py:494
  34.4 5.9 %collective-permute-start.2 = (bf16[352,128]{1,0:T(8,128)(2,1)S(1)}, bf16[352,128]{1,0:T(8,128)(2,1)S(1)}, u32[]{:S(2)}, u32[]{:S(2)}) collective-permute-start(bf16[352,128]{1,0:T(8,128)(2,1)S(1)} %get-tuple-element.33.own), channel_id=1, source_target_pairs={{0,32},{16,112},{32,0},{48,80},{64,96},{80,48},{96,64},{112,16},{1... | collective-permute-start | bytes 270344 | tf_op jit(solution)/shard_map/ppermute | solution.py:499
  40.5 1.3 %collective-permute-start.5 = (bf16[256,128]{1,0:T(8,128)(2,1)S(1)}, bf16[256,128]{1,0:T(8,128)(2,1)S(1)}, u32[]{:S(2)}, u32[]{:S(2)}) collective-permute-start(bf16[256,128]{1,0:T(8,128)(2,1)S(1)} %get-tuple-element.35.x_ref), channel_id=1, source_target_pairs={{0,16},{16,0},{32,48},{48,32},{64,80},{80,64},{96,112},{112,96},{1... | collective-permute-start | bytes 196616 | tf_op jit(solution)/shard_map/ppermute | solution.py:494
